TPU v7x, 32 devices: a whole 2x2x4 slice. The times are simulated.
32 devices in a mesh: seq: 8 (over z, y), batch: 4 (over x, core).
Axes of the slice: x: 2, y: 2, z: 4, core: 2. Of those that a mesh axis runs over, the one named last changes fastest.
Arguments:
- queries: bfloat16 [16384, 384], P(('batch', 'seq')), parts along dimension 0, may hold values from -400 to 400
- key_states: bfloat16 [16384, 384], P(('batch', 'seq')), parts along dimension 0, may hold values from -6 to 6
- value_states: bfloat16 [16384, 384], P(('batch', 'seq')), parts along dimension 0, may hold values from -6 to 6
- grad_output: bfloat16 [16384, 384], P(('batch', 'seq')), parts along dimension 0, may hold values from -6 to 6
- partners: int32 [12, 8], P('batch'), parts along dimension 0, may hold values from 0 to 7, each once within a row
- global_blocks: int32 [8], P('batch'), parts along dimension 0, may hold values from 0 to 7
Outputs:
- attended: bfloat16 [16384, 384], P(('batch', 'seq')), parts along dimension 0
- grad_queries: bfloat16 [16384, 384], P(('batch', 'seq')), parts along dimension 0
- grad_keys: bfloat16 [16384, 384], P(('batch', 'seq')), parts along dimension 0
- grad_values: bfloat16 [16384, 384], P(('batch', 'seq')), parts along dimension 0
There are 4 independent parts, one for each index of `batch`. A program takes and returns all parts, laid end to end along the dimension named above; each array names one. Nothing has to cross between parts.
Inputs may be any that keep to these rules, and one draw needn't show every extreme that they name: `partners`: each row names every sequence block once.
All inputs are finite; a program needn't handle non-finite values.
Results may differ from a plain program's by a relative error of at most 0.0065.
Values may be sent and summed in bfloat16 or wider, within the bound.
No kernel may reach another device: no remote copies, remote signals or barrier semaphores. Data moves between devices by JAX's collectives and lax.ppermute only.
A program may use at most 128 MiB of HBM per device.

v0:
```python
import math

import jax
import jax.numpy as jnp
from jax import lax
from jax.sharding import PartitionSpec as P

HEADS = 6
HD = 64


def extended(x, sides, width):
    for axis, dim in sides:
        devices, length = (lax.axis_size(axis), x.shape[dim])
        up = [(i, (i + 1) % devices) for i in range(devices)]
        down = [(j, i) for i, j in up]
        last = lax.slice_in_dim(x, length - width, length, axis=dim)
        first = lax.slice_in_dim(x, 0, width, axis=dim)
        before = lax.ppermute(last, axis, up)
        after = lax.ppermute(first, axis, down)
        x = jnp.concatenate([before, x, after], axis=dim)
    return x


def from_behind(x, axis, by):
    devices = lax.axis_size(axis)
    return lax.ppermute(x, axis, [(i, (i + by) % devices) for i in range(devices)])


def head_split(matrix):
    return matrix.reshape(matrix.shape[0], HEADS, HD).transpose(1, 0, 2)


def head_join(stacked):
    return stacked.transpose(1, 0, 2).reshape(stacked.shape[1], HEADS * HD)


def attend(queries, key_rows, grad_output):
    features = queries.shape[1]
    scale = 1.0 / math.sqrt(HD)
    contract_last = (((1,), (1,)), ((), ()))
    contract_first = (((0,), (0,)), ((), ()))

    def per_head(head_items):
        query_head, key_head, value_head, grad_head = head_items
        scores = (
            lax.dot_general(query_head, key_head, contract_last, preferred_element_type=jnp.float32)
            * scale
        )
        row_peak = jnp.max(scores, axis=-1, keepdims=True)
        exponent = jnp.exp(scores - row_peak)
        weights = exponent / jnp.sum(exponent, axis=-1, keepdims=True)
        weights_low = weights.astype(jnp.bfloat16)
        output_head = jnp.dot(weights_low, value_head, preferred_element_type=jnp.float32).astype(
            jnp.bfloat16
        )
        grad_weights = lax.dot_general(
            grad_head, value_head, contract_last, preferred_element_type=jnp.float32
        )
        row_dots = jnp.sum(weights * grad_weights, axis=-1, keepdims=True)
        grad_scores = (weights * (grad_weights - row_dots) * scale).astype(jnp.bfloat16)
        grad_query = jnp.dot(grad_scores, key_head, preferred_element_type=jnp.float32).astype(
            jnp.bfloat16
        )
        grad_key = lax.dot_general(
            grad_scores, query_head, contract_first, preferred_element_type=jnp.float32
        )
        grad_value = lax.dot_general(
            weights_low, grad_head, contract_first, preferred_element_type=jnp.float32
        )
        return (output_head, grad_query, grad_key, grad_value)

    outputs, grad_query, grad_key, grad_value = lax.map(
        per_head,
        (
            head_split(queries),
            head_split(key_rows[:, :features]),
            head_split(key_rows[:, features:]),
            head_split(grad_output),
        ),
    )
    grad_pair = jnp.concatenate([head_join(grad_key), head_join(grad_value)], axis=1)
    return (head_join(outputs), head_join(grad_query), grad_pair)


def route_forward(key_value, route_table, devices):
    block_rows, columns = key_value.shape
    pieces = key_value.reshape(devices, block_rows // devices, columns)
    spread = lax.all_to_all(pieces, "seq", split_axis=0, concat_axis=0, tiled=True)
    picked = jnp.take(spread, route_table, axis=0)
    arrived = lax.all_to_all(picked, "seq", split_axis=1, concat_axis=1, tiled=True)
    return arrived.reshape(route_table.shape[0], block_rows, columns)


def route_back(grad_terms, route_table, devices):
    routes, block_rows, columns = grad_terms.shape
    piece_rows = block_rows // devices
    pieces = grad_terms.reshape(routes, devices, piece_rows, columns)
    coming = lax.all_to_all(pieces, "seq", split_axis=1, concat_axis=1, tiled=True)
    block_ids = jnp.arange(devices, dtype=jnp.int32)
    one_hot = (route_table[:, :, None] == block_ids[None, None, :]).astype(jnp.float32)
    summed = jnp.einsum(
        "rds,rdx->sx",
        one_hot,
        coming.reshape(routes, devices, piece_rows * columns),
        precision=lax.Precision.HIGHEST,
    )
    returned = lax.all_to_all(
        summed.reshape(devices, piece_rows, columns), "seq", split_axis=0, concat_axis=0, tiled=True
    )
    return returned.reshape(block_rows, columns)


def local(queries, key_states, value_states, grad_output, partners, global_blocks):
    devices = lax.axis_size("seq")
    block_rows = queries.shape[0]
    features = queries.shape[1]
    key_value = jnp.concatenate([key_states, value_states], axis=1)
    table_rows = []
    table_rows = table_rows + [partners[0], partners[1], partners[2]]
    table_rows = table_rows + [
        jnp.full((devices,), global_blocks[0], jnp.int32),
        jnp.full((devices,), global_blocks[1], jnp.int32),
    ]
    route_table = jnp.stack(table_rows)
    fetched = route_forward(key_value, route_table, devices)
    padded = extended(key_value, (("seq", 0),), block_rows)
    left_block = padded[:block_rows]
    right_block = padded[2 * block_rows :]
    offset = 0
    random_blocks = [fetched[offset], fetched[offset + 1], fetched[offset + 2]]
    global_rows = [fetched[offset + 3], fetched[offset + 4]]
    key_rows = jnp.concatenate(
        [key_value, left_block, right_block] + random_blocks + global_rows, axis=0
    )
    attended, grad_queries, grad_pair = attend(queries, key_rows, grad_output)
    grad_parts = grad_pair.reshape(8, block_rows, 2 * features)
    grad_total = grad_parts[0]
    returning = []
    grad_total = grad_total + from_behind(grad_parts[1], "seq", -1)
    grad_total = grad_total + from_behind(grad_parts[2], "seq", 1)
    returning = returning + [grad_parts[3], grad_parts[4], grad_parts[5]]
    returning = returning + [grad_parts[6], grad_parts[7]]
    grad_total = grad_total + route_back(jnp.stack(returning), route_table, devices)
    return (
        attended,
        grad_queries,
        grad_total[:, :features].astype(jnp.bfloat16),
        grad_total[:, features:].astype(jnp.bfloat16),
    )


def solution(mesh):
    in_specs = (
        P(("batch", "seq"), None),
        P(("batch", "seq"), None),
        P(("batch", "seq"), None),
        P(("batch", "seq"), None),
        P("batch", None),
        P("batch"),
    )
    out_specs = (
        P(("batch", "seq"), None),
        P(("batch", "seq"), None),
        P(("batch", "seq"), None),
        P(("batch", "seq"), None),
    )
    return jax.shard_map(local, mesh=mesh, in_specs=in_specs, out_specs=out_specs, check_vma=False)
```

profile of v0, /device:TPU:0, one launch (start us, length us, event | category | flops | bytes accessed | tf_op | source)
XLA Modules:
  0.0 710.5 jit_solution(13146894143253555484)
XLA Ops:
  4.6 7.3 %all-to-all-start = ((bf16[8,64,768]{2,1,0:T(8,128)(2,1)}), bf16[8,64,768]{2,1,0:T(8,128)(2,1)S(1)}, u32[]{:S(2)}, u32[]{:S(2)}) async-start(bf16[8,64,768]{2,1,0:T(8,128)(2,1)} %bitcast.12), calls=%async_computation | async-start | bytes 1572864 | tf_op jit(solution)/shard_map/all_to_all | solution.py:89
  16.3 15.8 %all-to-all-done = bf16[8,64,768]{2,1,0:T(8,128)(2,1)S(1)} async-done(((bf16[8,64,768]{2,1,0:T(8,128)(2,1)}), bf16[8,64,768]{2,1,0:T(8,128)(2,1)S(1)}, u32[]{:S(2)}, u32[]{:S(2)}) %all-to-all-start) | async-done | bytes 786464 | tf_op jit(solution)/shard_map/all_to_all | solution.py:89
  50.5 78.6 %collective-permute-done = bf16[512,768]{1,0:T(8,128)(2,1)S(1)} collective-permute-done((bf16[512,768]{1,0:T(8,128)(2,1)}, bf16[512,768]{1,0:T(8,128)(2,1)S(1)}, u32[]{:S(2)}, u32[]{:S(2)}) %collective-permute-start) | collective-permute-done | bytes 786464 | tf_op jit(solution)/shard_map/ppermute | solution.py:19
  140.6 6.1 fusion.63
  154.7 204.2 %while.16 = (s32[]{:T(128)}, bf16[6,512,64]{1,2,0:T(8,128)(2,1)}, bf16[6,512,64]{1,2,0:T(8,128)(2,1)}, f32[6,4096,64]{1,2,0:T(8,128)}, f32[6,4096,64]{1,2,0:T(8,...) while((s32[]{:T(128)}, bf16[6,512,64]{1,2,0:T(8,128)(2,1)}, ...), condition=%wide.region_4.5_spmd, body=%wide.region_0.4_spmd.sunk | while | flops 1644231168 | bytes 143020256 | solution.py:73
  157.8 9.3 %multiply_reduce_fusion.5 = (f32[512]{0:T(512)S(1)}, f32[512,4096]{1,0:T(8,128)}, f32[512,4096]{1,0:T(8,128)}) fusion(f32[512]{0:T(512)S(1)} %fusion.90, f32[512]{0:T(512)S(1)} %get-tuple-element.216, f32[512,4096]{1,0:T(8,128)S(1)} %get-tuple-element.215, bf16[6,4096,64]{1,2,0:T(8,128)(2,1)} %get-tuple-element.247, s32[]{:T(128)} %get-tuple-element.230, ...), kind=kOutput, calls=%fused_computation.2.clone.1 | convolution fusion | flops 278920704 | bytes 25762816 | tf_op jit(solution)/shard_map/while/body/eval_jaxpr/dot_general | solution.py:57
  167.1 8.0 %multiply_convert_fusion.2 = bf16[512,4096]{1,0:T(8,128)(2,1)S(1)} fusion(f32[512,4096]{1,0:T(8,128)} %get-tuple-element.217, f32[512,4096]{1,0:T(8,128)} %get-tuple-element.218, f32[512]{0:T(512)S(1)} %get-tuple-element.219), kind=kLoop, calls=%fused_computation.1.clone.1 | loop fusion | flops 8388608 | bytes 20973568 | tf_op jit(solution)/shard_map/while/body/eval_jaxpr/convert_element_type | solution.py:61
  177.0 5.4 fusion.94
  191.8 9.3 %multiply_reduce_fusion.5 = (f32[512]{0:T(512)S(1)}, f32[512,4096]{1,0:T(8,128)}, f32[512,4096]{1,0:T(8,128)}) fusion(f32[512]{0:T(512)S(1)} %fusion.90, f32[512]{0:T(512)S(1)} %get-tuple-element.216, f32[512,4096]{1,0:T(8,128)S(1)} %get-tuple-element.215, bf16[6,4096,64]{1,2,0:T(8,128)(2,1)} %get-tuple-element.247, s32[]{:T(128)} %get-tuple-element.230, ...), kind=kOutput, calls=%fused_computation.2.clone.1 | convolution fusion | flops 278920704 | bytes 25762816 | tf_op jit(solution)/shard_map/while/body/eval_jaxpr/dot_general | solution.py:57
  201.0 8.0 %multiply_convert_fusion.2 = bf16[512,4096]{1,0:T(8,128)(2,1)S(1)} fusion(f32[512,4096]{1,0:T(8,128)} %get-tuple-element.217, f32[512,4096]{1,0:T(8,128)} %get-tuple-element.218, f32[512]{0:T(512)S(1)} %get-tuple-element.219), kind=kLoop, calls=%fused_computation.1.clone.1 | loop fusion | flops 8388608 | bytes 20973568 | tf_op jit(solution)/shard_map/while/body/eval_jaxpr/convert_element_type | solution.py:61
  210.9 5.5 fusion.94
  225.9 9.3 %multiply_reduce_fusion.5 = (f32[512]{0:T(512)S(1)}, f32[512,4096]{1,0:T(8,128)}, f32[512,4096]{1,0:T(8,128)}) fusion(f32[512]{0:T(512)S(1)} %fusion.90, f32[512]{0:T(512)S(1)} %get-tuple-element.216, f32[512,4096]{1,0:T(8,128)S(1)} %get-tuple-element.215, bf16[6,4096,64]{1,2,0:T(8,128)(2,1)} %get-tuple-element.247, s32[]{:T(128)} %get-tuple-element.230, ...), kind=kOutput, calls=%fused_computation.2.clone.1 | convolution fusion | flops 278920704 | bytes 25762816 | tf_op jit(solution)/shard_map/while/body/eval_jaxpr/dot_general | solution.py:57
  235.1 8.0 %multiply_convert_fusion.2 = bf16[512,4096]{1,0:T(8,128)(2,1)S(1)} fusion(f32[512,4096]{1,0:T(8,128)} %get-tuple-element.217, f32[512,4096]{1,0:T(8,128)} %get-tuple-element.218, f32[512]{0:T(512)S(1)} %get-tuple-element.219), kind=kLoop, calls=%fused_computation.1.clone.1 | loop fusion | flops 8388608 | bytes 20973568 | tf_op jit(solution)/shard_map/while/body/eval_jaxpr/convert_element_type | solution.py:61
  245.0 5.5 fusion.94
  260.0 9.3 %multiply_reduce_fusion.5 = (f32[512]{0:T(512)S(1)}, f32[512,4096]{1,0:T(8,128)}, f32[512,4096]{1,0:T(8,128)}) fusion(f32[512]{0:T(512)S(1)} %fusion.90, f32[512]{0:T(512)S(1)} %get-tuple-element.216, f32[512,4096]{1,0:T(8,128)S(1)} %get-tuple-element.215, bf16[6,4096,64]{1,2,0:T(8,128)(2,1)} %get-tuple-element.247, s32[]{:T(128)} %get-tuple-element.230, ...), kind=kOutput, calls=%fused_computation.2.clone.1 | convolution fusion | flops 278920704 | bytes 25762816 | tf_op jit(solution)/shard_map/while/body/eval_jaxpr/dot_general | solution.py:57
  269.2 8.0 %multiply_convert_fusion.2 = bf16[512,4096]{1,0:T(8,128)(2,1)S(1)} fusion(f32[512,4096]{1,0:T(8,128)} %get-tuple-element.217, f32[512,4096]{1,0:T(8,128)} %get-tuple-element.218, f32[512]{0:T(512)S(1)} %get-tuple-element.219), kind=kLoop, calls=%fused_computation.1.clone.1 | loop fusion | flops 8388608 | bytes 20973568 | tf_op jit(solution)/shard_map/while/body/eval_jaxpr/convert_element_type | solution.py:61
  279.1 5.4 fusion.94
  294.0 9.3 %multiply_reduce_fusion.5 = (f32[512]{0:T(512)S(1)}, f32[512,4096]{1,0:T(8,128)}, f32[512,4096]{1,0:T(8,128)}) fusion(f32[512]{0:T(512)S(1)} %fusion.90, f32[512]{0:T(512)S(1)} %get-tuple-element.216, f32[512,4096]{1,0:T(8,128)S(1)} %get-tuple-element.215, bf16[6,4096,64]{1,2,0:T(8,128)(2,1)} %get-tuple-element.247, s32[]{:T(128)} %get-tuple-element.230, ...), kind=kOutput, calls=%fused_computation.2.clone.1 | convolution fusion | flops 278920704 | bytes 25762816 | tf_op jit(solution)/shard_map/while/body/eval_jaxpr/dot_general | solution.py:57
  303.2 8.0 %multiply_convert_fusion.2 = bf16[512,4096]{1,0:T(8,128)(2,1)S(1)} fusion(f32[512,4096]{1,0:T(8,128)} %get-tuple-element.217, f32[512,4096]{1,0:T(8,128)} %get-tuple-element.218, f32[512]{0:T(512)S(1)} %get-tuple-element.219), kind=kLoop, calls=%fused_computation.1.clone.1 | loop fusion | flops 8388608 | bytes 20973568 | tf_op jit(solution)/shard_map/while/body/eval_jaxpr/convert_element_type | solution.py:61
  313.2 5.4 fusion.94
  328.0 9.3 %multiply_reduce_fusion.5 = (f32[512]{0:T(512)S(1)}, f32[512,4096]{1,0:T(8,128)}, f32[512,4096]{1,0:T(8,128)}) fusion(f32[512]{0:T(512)S(1)} %fusion.90, f32[512]{0:T(512)S(1)} %get-tuple-element.216, f32[512,4096]{1,0:T(8,128)S(1)} %get-tuple-element.215, bf16[6,4096,64]{1,2,0:T(8,128)(2,1)} %get-tuple-element.247, s32[]{:T(128)} %get-tuple-element.230, ...), kind=kOutput, calls=%fused_computation.2.clone.1 | convolution fusion | flops 278920704 | bytes 25762816 | tf_op jit(solution)/shard_map/while/body/eval_jaxpr/dot_general | solution.py:57
  337.2 8.0 %multiply_convert_fusion.2 = bf16[512,4096]{1,0:T(8,128)(2,1)S(1)} fusion(f32[512,4096]{1,0:T(8,128)} %get-tuple-element.217, f32[512,4096]{1,0:T(8,128)} %get-tuple-element.218, f32[512]{0:T(512)S(1)} %get-tuple-element.219), kind=kLoop, calls=%fused_computation.1.clone.1 | loop fusion | flops 8388608 | bytes 20973568 | tf_op jit(solution)/shard_map/while/body/eval_jaxpr/convert_element_type | solution.py:61
  347.1 5.4 fusion.94
  358.9 7.7 %fusion.50 = (f32[512,768]{0,1:T(8,128)}, f32[512,768]{0,1:T(8,128)}, f32[512,768]{0,1:T(8,128)}, f32[512,768]{0,1:T(8,128)}, f32[512,768]{0,1:T(8,128)}, /*index=5*/f32[512,768]{0,1:T(8,128)S(1)}, f32[512,768]{0,1:T(8,128)S(1)}) fusion(f32[4096,384]{0,1:T(8,128)} %bitcast.152, f32[4096,384]{0,1:T(8,128)} %bitcast.154), kind=kLoop, calls=%fused_computation.67 | loop fusion | flops 2752512 | bytes 23592960 | tf_op jit(solution)/shard_map/concatenate | solution.py:82
  388.8 7.3 %copy.97 = f32[5,8,64,768]{3,2,0,1:T(8,128)} copy(f32[5,8,64,768]{3,2,1,0:T(8,128)} %constant_dynamic-update-slice_fusion.11) | data formatting | bytes 15728640 | tf_op jit(solution)/shard_map/stack | solution.py:144
  396.0 19.6 %all-to-all-start.2 = ((f32[5,8,64,768]{3,2,0,1:T(8,128)}), f32[5,8,64,768]{3,2,0,1:T(8,128)}, u32[]{:S(2)}, u32[]{:S(2)}) async-start(f32[5,8,64,768]{3,2,0,1:T(8,128)} %copy.97), calls=%async_computation.2 | async-start | bytes 15728640 | tf_op jit(solution)/shard_map/all_to_all | solution.py:99
  415.7 173.4 %all-to-all-done.2 = f32[5,8,64,768]{3,2,0,1:T(8,128)} async-done(((f32[5,8,64,768]{3,2,0,1:T(8,128)}), f32[5,8,64,768]{3,2,0,1:T(8,128)}, u32[]{:S(2)}, u32[]{:S(2)}) %all-to-all-start.2) | async-done | bytes 7864352 | tf_op jit(solution)/shard_map/all_to_all | solution.py:99
  589.1 7.3 %copy.98 = f32[5,8,64,768]{3,2,1,0:T(8,128)} copy(f32[5,8,64,768]{3,2,0,1:T(8,128)} %all-to-all-done.2) | data formatting | bytes 15728640 | tf_op jit(solution)/shard_map/all_to_all | solution.py:99
  596.4 8.6 %reshape.185 = f32[5,8,49152]{2,1,0:T(8,128)} reshape(f32[5,8,64,768]{3,2,1,0:T(8,128)} %copy.98) | data formatting | bytes 15728640 | tf_op jit(solution)/shard_map/reshape | solution.py:105
  605.0 8.9 %fusion.56 = f32[8,64,768]{2,0,1:T(8,128)S(1)} fusion(f32[5,1,64,8,768]{4,3,2,1,0:T(8,128)} %bitcast.151, s32[5,8]{1,0:T(8,128)S(1)} %add_add_fusion), kind=kOutput, calls=%fused_computation.74 | convolution fusion | flops 188744000 | bytes 9437344 | tf_op jit(solution)/shard_map/rds,rdx->sx/dot_general | solution.py:102
  626.7 30.8 %all-to-all-done.3 = f32[8,64,768]{2,1,0:T(8,128)S(1)} async-done(((f32[8,64,768]{2,1,0:T(8,128)}), f32[8,64,768]{2,1,0:T(8,128)S(1)}, u32[]{:S(2)}, u32[]{:S(2)}) %all-to-all-start.3) | async-done | bytes 1572896 | tf_op jit(solution)/shard_map/all_to_all | solution.py:108
  658.0 47.7 %collective-permute-done.2 = f32[512,768]{0,1:T(8,128)} collective-permute-done((f32[512,768]{0,1:T(8,128)}, f32[512,768]{0,1:T(8,128)}, u32[]{:S(2)}, u32[]{:S(2)}) %collective-permute-start.2) | collective-permute-done | bytes 1572896 | tf_op jit(solution)/shard_map/ppermute | solution.py:27
  (158 shorter events, 154.0 us)
Async XLA Ops:
  4.6 27.5 %all-to-all-start = ((bf16[8,64,768]{2,1,0:T(8,128)(2,1)}), bf16[8,64,768]{2,1,0:T(8,128)(2,1)S(1)}, u32[]{:S(2)}, u32[]{:S(2)}) async-start(bf16[8,64,768]{2,1,0:T(8,128)(2,1)} %bitcast.12), calls=%async_computation | async-start | bytes 1572864 | tf_op jit(solution)/shard_map/all_to_all | solution.py:89
  14.0 23.7 %copy-start.7 = (s32[5]{0:T(128)}, s32[5]{0:T(128)S(1)}, u32[]{:S(2)}) copy-start(s32[5]{0:T(128)S(1)} %pad.6.clone) | copy-start | bytes 64
  14.7 23.0 %copy-start.9 = (s32[5]{0:T(128)}, s32[5]{0:T(128)S(1)}, u32[]{:S(2)}) copy-start(s32[5]{0:T(128)S(1)} %pad.7.clone) | copy-start | bytes 64
  37.7 11.7 %copy-start.3 = (bf16[512,384]{1,0:T(8,128)(2,1)S(1)}, bf16[512,384]{1,0:T(8,128)(2,1)}, u32[]{:S(2)}) copy-start(bf16[512,384]{1,0:T(8,128)(2,1)} %param.11) | copy-start | bytes 1179652
  39.9 10.4 %copy-start.4 = (bf16[512,384]{1,0:T(8,128)(2,1)S(1)}, bf16[512,384]{1,0:T(8,128)(2,1)}, u32[]{:S(2)}) copy-start(bf16[512,384]{1,0:T(8,128)(2,1)} %param.8) | copy-start | bytes 1179652
  39.9 93.6 %all-to-all-start.1 = ((bf16[5,8,64,768]{3,2,0,1:T(8,128)(2,1)}), bf16[5,8,64,768]{3,2,0,1:T(8,128)(2,1)}, u32[]{:S(2)}, u32[]{:S(2)}) async-start(bf16[5,8,64,768]{3,2,0,1:T(8,128)(2,1)} %copy.79), calls=%async_computation.1 | async-start | bytes 7864320 | tf_op jit(solution)/shard_map/all_to_all | solution.py:91
  44.6 84.6 %collective-permute-start = (bf16[512,768]{1,0:T(8,128)(2,1)}, bf16[512,768]{1,0:T(8,128)(2,1)S(1)}, u32[]{:S(2)}, u32[]{:S(2)}) collective-permute-start(bf16[512,768]{1,0:T(8,128)(2,1)} %get-tuple-element.149), channel_id=1, source_target_pairs={{0,4},{4,8},{8,12},{12,16},{16,20},{20,24},{24,28},{28,0},{1,5},{5... | collective-permute-start | bytes 2359304 | tf_op jit(solution)/shard_map/ppermute | solution.py:19
  46.5 83.6 %collective-permute-start.1 = (bf16[512,768]{1,0:T(8,128)(2,1)}, bf16[512,768]{1,0:T(8,128)(2,1)S(1)}, u32[]{:S(2)}, u32[]{:S(2)}) collective-permute-start(bf16[512,768]{1,0:T(8,128)(2,1)} %get-tuple-element.149), channel_id=1, source_target_pairs={{4,0},{8,4},{12,8},{16,12},{20,16},{24,20},{28,24},{0,28},{5,1},{9... | collective-permute-start | bytes 2359304 | tf_op jit(solution)/shard_map/ppermute | solution.py:20
  175.1 10.3 %slice-start = ((s8[8388608]{0:T(1024)(128)(4,1)}), s8[4194304]{0:T(1024)(128)(4,1)S(1)}, s32[]{:S(2)}) async-start(s8[8388608]{0:T(1024)(128)(4,1)} %bitcast.149), calls=%async_computation.4 | async-start | bytes 8388608 | tf_op jit(solution)/shard_map/while
  177.0 8.5 %slice-start.1 = ((s8[8388608]{0:T(1024)(128)(4,1)}), s8[4194304]{0:T(1024)(128)(4,1)S(1)}, s32[]{:S(2)}) async-start(s8[8388608]{0:T(1024)(128)(4,1)} %bitcast.149), calls=%async_computation.5 | async-start | bytes 8388608 | tf_op jit(solution)/shard_map/while
  209.1 10.4 %slice-start = ((s8[8388608]{0:T(1024)(128)(4,1)}), s8[4194304]{0:T(1024)(128)(4,1)S(1)}, s32[]{:S(2)}) async-start(s8[8388608]{0:T(1024)(128)(4,1)} %bitcast.149), calls=%async_computation.4 | async-start | bytes 8388608 | tf_op jit(solution)/shard_map/while
  210.9 8.6 %slice-start.1 = ((s8[8388608]{0:T(1024)(128)(4,1)}), s8[4194304]{0:T(1024)(128)(4,1)S(1)}, s32[]{:S(2)}) async-start(s8[8388608]{0:T(1024)(128)(4,1)} %bitcast.149), calls=%async_computation.5 | async-start | bytes 8388608 | tf_op jit(solution)/shard_map/while
  219.5 3.2 copy-start.1
  243.2 10.4 %slice-start = ((s8[8388608]{0:T(1024)(128)(4,1)}), s8[4194304]{0:T(1024)(128)(4,1)S(1)}, s32[]{:S(2)}) async-start(s8[8388608]{0:T(1024)(128)(4,1)} %bitcast.149), calls=%async_computation.4 | async-start | bytes 8388608 | tf_op jit(solution)/shard_map/while
  245.0 8.6 %slice-start.1 = ((s8[8388608]{0:T(1024)(128)(4,1)}), s8[4194304]{0:T(1024)(128)(4,1)S(1)}, s32[]{:S(2)}) async-start(s8[8388608]{0:T(1024)(128)(4,1)} %bitcast.149), calls=%async_computation.5 | async-start | bytes 8388608 | tf_op jit(solution)/shard_map/while
  253.6 3.2 copy-start.1
  277.3 10.3 %slice-start = ((s8[8388608]{0:T(1024)(128)(4,1)}), s8[4194304]{0:T(1024)(128)(4,1)S(1)}, s32[]{:S(2)}) async-start(s8[8388608]{0:T(1024)(128)(4,1)} %bitcast.149), calls=%async_computation.4 | async-start | bytes 8388608 | tf_op jit(solution)/shard_map/while
  279.1 8.5 %slice-start.1 = ((s8[8388608]{0:T(1024)(128)(4,1)}), s8[4194304]{0:T(1024)(128)(4,1)S(1)}, s32[]{:S(2)}) async-start(s8[8388608]{0:T(1024)(128)(4,1)} %bitcast.149), calls=%async_computation.5 | async-start | bytes 8388608 | tf_op jit(solution)/shard_map/while
  311.3 10.3 %slice-start = ((s8[8388608]{0:T(1024)(128)(4,1)}), s8[4194304]{0:T(1024)(128)(4,1)S(1)}, s32[]{:S(2)}) async-start(s8[8388608]{0:T(1024)(128)(4,1)} %bitcast.149), calls=%async_computation.4 | async-start | bytes 8388608 | tf_op jit(solution)/shard_map/while
  313.2 8.5 %slice-start.1 = ((s8[8388608]{0:T(1024)(128)(4,1)}), s8[4194304]{0:T(1024)(128)(4,1)S(1)}, s32[]{:S(2)}) async-start(s8[8388608]{0:T(1024)(128)(4,1)} %bitcast.149), calls=%async_computation.5 | async-start | bytes 8388608 | tf_op jit(solution)/shard_map/while
  345.3 10.3 %slice-start = ((s8[8388608]{0:T(1024)(128)(4,1)}), s8[4194304]{0:T(1024)(128)(4,1)S(1)}, s32[]{:S(2)}) async-start(s8[8388608]{0:T(1024)(128)(4,1)} %bitcast.149), calls=%async_computation.4 | async-start | bytes 8388608 | tf_op jit(solution)/shard_map/while
  347.1 8.5 %slice-start.1 = ((s8[8388608]{0:T(1024)(128)(4,1)}), s8[4194304]{0:T(1024)(128)(4,1)S(1)}, s32[]{:S(2)}) async-start(s8[8388608]{0:T(1024)(128)(4,1)} %bitcast.149), calls=%async_computation.5 | async-start | bytes 8388608 | tf_op jit(solution)/shard_map/while
  355.6 3.2 copy-start.1
  380.6 5.5 copy-start.2
  396.0 19.6 %copy-start.6 = (s32[3,8]{1,0:T(4,128)S(1)}, s32[3,8]{1,0:T(4,128)}, u32[]{:S(2)}) copy-start(s32[3,8]{1,0:T(4,128)} %param.12) | copy-start | bytes 292
  396.0 19.6 %copy-start.8 = (s32[5]{0:T(128)S(1)}, s32[5]{0:T(128)}, u32[]{:S(2)}) copy-start(s32[5]{0:T(128)} %copy-done.7) | copy-start | bytes 64
  396.0 19.6 %copy-start.10 = (s32[5]{0:T(128)S(1)}, s32[5]{0:T(128)}, u32[]{:S(2)}) copy-start(s32[5]{0:T(128)} %copy-done.9) | copy-start | bytes 64
  396.0 193.1 %all-to-all-start.2 = ((f32[5,8,64,768]{3,2,0,1:T(8,128)}), f32[5,8,64,768]{3,2,0,1:T(8,128)}, u32[]{:S(2)}, u32[]{:S(2)}) async-start(f32[5,8,64,768]{3,2,0,1:T(8,128)} %copy.97), calls=%async_computation.2 | async-start | bytes 15728640 | tf_op jit(solution)/shard_map/all_to_all | solution.py:99
  605.0 20.8 %copy-start.5 = (bf16[6,512,64]{1,2,0:T(8,128)(2,1)S(1)}, bf16[6,512,64]{1,2,0:T(8,128)(2,1)}, u32[]{:S(2)}) copy-start(bf16[6,512,64]{1,2,0:T(8,128)(2,1)} %get-tuple-element.55) | copy-start | bytes 1179652
  615.6 41.9 %all-to-all-start.3 = ((f32[8,64,768]{2,1,0:T(8,128)}), f32[8,64,768]{2,1,0:T(8,128)S(1)}, u32[]{:S(2)}, u32[]{:S(2)}) async-start(f32[8,64,768]{2,1,0:T(8,128)} %copy.100), calls=%async_computation.3 | async-start | bytes 3145728 | tf_op jit(solution)/shard_map/all_to_all | solution.py:108
  619.2 86.5 %collective-permute-start.2 = (f32[512,768]{0,1:T(8,128)}, f32[512,768]{0,1:T(8,128)}, u32[]{:S(2)}, u32[]{:S(2)}) collective-permute-start(f32[512,768]{0,1:T(8,128)} %get-tuple-element.133), channel_id=1, source_target_pairs={{0,28},{4,0},{8,4},{12,8},{16,12},{20,16},{24,20},{28,24},{1,29},{... | collective-permute-start | bytes 4718600 | tf_op jit(solution)/shard_map/ppermute | solution.py:27
  623.8 81.8 %collective-permute-start.3 = (f32[512,768]{0,1:T(8,128)}, f32[512,768]{0,1:T(8,128)}, u32[]{:S(2)}, u32[]{:S(2)}) collective-permute-start(f32[512,768]{0,1:T(8,128)} %get-tuple-element.134), channel_id=1, source_target_pairs={{0,4},{4,8},{8,12},{12,16},{16,20},{20,24},{24,28},{28,0},{1,5},{5... | collective-permute-start | bytes 4718600 | tf_op jit(solution)/shard_map/ppermute | solution.py:27
  (9 other events, 19.4 us)
where the time goes:
time: 712 us; the launch traced here: 711 us
  waiting for transfers between devices  349 us (49%)
  matrix products  154 us (22%)
  local copies, waits for them, and re-layouts  90.1 us (13%)
  other arithmetic  72.1 us (10%)
  starting transfers between devices  44.5 us (6%)
    all_to_all x1, waiting for transfers between devices, route_back(): lax.all_to_all(pieces, 'seq', split_axis=1, concat_axis=1, tiled=True)  173 us
    ppermute x1, waiting for transfers between devices, extended(): before = lax.ppermute(last, axis, up)  78.6 us
    dot_general x6, matrix products, per_head(): lax.dot_general(grad_head, value_head, contract_last, preferred_element_t...  55.6 us
    convert_element_type x6, other arithmetic, per_head(): (weights * (grad_weights - row_dots) * scale).astype(jnp.bfloat16)  48.3 us
    ppermute x2, waiting for transfers between devices, from_behind(): lax.ppermute(x, axis, [(i, (i + by) % devices) for i in range(devices)])  47.7 us
    dot_general x6, matrix products, per_head(): lax.dot_general(weights_low, grad_head, contract_first, preferred_element...  32.6 us
    all_to_all x1, waiting for transfers between devices, route_back(): lax.all_to_all(summed.reshape(devices, piece_rows, columns), 'seq', split...  30.8 us
    unnamed x35, local copies, waits for them, and re-layouts  23.1 us
  transfers between devices with their start and end apart: 8, of which 6 were waited for; matrix products, arithmetic and copies ran while one was open for 2% of the time, Pallas kernels for 0%

commit v1 on v0

--- a/solution.py
+++ b/solution.py
@@ -3,6 +3,8 @@
 import jax
 import jax.numpy as jnp
 from jax import lax
+from jax.experimental import pallas as pl
+from jax.experimental.pallas import tpu as pltpu
 from jax.sharding import PartitionSpec as P
 
 HEADS = 6
@@ -111,7 +113,7 @@
     return returned.reshape(block_rows, columns)
 
 
-def local(queries, key_states, value_states, grad_output, partners, global_blocks):
+def routed_local(queries, key_states, value_states, grad_output, partners, global_blocks):
     devices = lax.axis_size("seq")
     block_rows = queries.shape[0]
     features = queries.shape[1]
@@ -150,6 +152,287 @@
     )
 
 
+LISTED = 8
+TO_LOG2 = 1.0 / (math.log(2.0) * math.sqrt(HD))
+VMEM_LIMIT = 56 * 1024 * 1024
+
+
+def matmul(a, b, contract_a, contract_b):
+    return lax.dot_general(
+        a, b, (((contract_a,), (contract_b,)), ((), ())), preferred_element_type=jnp.float32
+    )
+
+
+def placed(rows, side):
+    blank = jnp.zeros_like(rows)
+    return jnp.concatenate([rows, blank] if side == 0 else [blank, rows], axis=0)
+
+
+def pair_kernel(first, bias_ref, q_ref, do_ref, k_ref, v_ref, *refs):
+    if first:
+        e_ref, u_ref, acc_out, run_out, pair_out = refs
+    else:
+        acc_in, run_in, e_ref, u_ref, acc_out, run_out, pair_out = refs
+    keys = k_ref[...]
+    values = v_ref[...]
+    q_t = q_ref[...].T
+    do_t = do_ref[...].T
+    k_t = keys.T
+    v_t = values.T
+    bias = bias_ref[0]
+    for side in range(2):
+        rows = slice(side * HD, (side + 1) * HD)
+        scores = matmul(keys, placed(q_t[rows], side), 1, 0) * TO_LOG2
+        peak = jnp.max(scores, axis=0, keepdims=True)
+        exponent = jnp.exp2(scores - peak)
+        total = jnp.sum(exponent, axis=0, keepdims=True)
+        low = exponent.astype(jnp.bfloat16)
+        e_ref[side] = low
+        both = matmul(jnp.concatenate([v_t[rows], k_t[rows]], axis=0), low, 1, 0)
+        grad_weights = matmul(values, placed(do_t[rows], side), 1, 0)
+        dots = jnp.sum(both[:HD] * do_t[rows].astype(jnp.float32), axis=0, keepdims=True)
+        mean = dots / total
+        centred = (exponent * (grad_weights - mean)).astype(jnp.bfloat16)
+        u_ref[side] = centred
+        moved = matmul(k_t[rows], centred, 1, 0) + mean * both[HD:]
+        peak = peak + bias
+        if first:
+            acc_out[side, : 2 * HD] = both
+            acc_out[side, 2 * HD :] = moved
+            top, run_total, run_dots = peak, total, dots
+        else:
+            old = run_in[side, 0:1]
+            top = jnp.maximum(old, peak)
+            keep = jnp.exp2(old - top)
+            take = jnp.exp2(peak - top)
+            acc_out[side, : 2 * HD] = acc_in[side, : 2 * HD] * keep + both * take
+            acc_out[side, 2 * HD :] = acc_in[side, 2 * HD :] * keep + moved * take
+            run_total = run_in[side, 1:2] * keep + total * take
+            run_dots = run_in[side, 2:3] * keep + dots * take
+        run_out[side, 0:1] = top
+        run_out[side, 1:2] = run_total
+        run_out[side, 2:3] = run_dots
+        pair_out[side, 0:1] = peak
+        pair_out[side, 1:2] = mean
+
+
+def head_pairs(features):
+    return features // (2 * HD)
+
+
+def column_spec(rows, offset):
+    return pl.BlockSpec((rows, 2 * HD), lambda p: (0, p + offset))
+
+
+def per_head_spec(*tail):
+    return pl.BlockSpec((2,) + tail, lambda p: (p,) + (0,) * len(tail))
+
+
+def pair_terms(bias, query_grad, key_value, running):
+    rows, columns = query_grad.shape
+    keys = key_value.shape[0]
+    features = columns // 2
+    steps = head_pairs(features)
+    heads = 2 * steps
+    first = running is None
+    state = [] if first else list(running)
+    acc = jax.ShapeDtypeStruct((heads, 3 * HD, rows), jnp.float32)
+    stat = jax.ShapeDtypeStruct((heads, 8, rows), jnp.float32)
+    big = jax.ShapeDtypeStruct((heads, keys, rows), jnp.bfloat16)
+    acc_spec = per_head_spec(3 * HD, rows)
+    stat_spec = per_head_spec(8, rows)
+    big_spec = per_head_spec(keys, rows)
+    return pl.pallas_call(
+        lambda *refs: pair_kernel(first, *refs),
+        grid=(steps,),
+        in_specs=[
+            pl.BlockSpec(memory_space=pltpu.SMEM),
+            column_spec(rows, 0),
+            column_spec(rows, steps),
+            column_spec(keys, 0),
+            column_spec(keys, steps),
+        ]
+        + ([] if first else [acc_spec, stat_spec]),
+        out_specs=[big_spec, big_spec, acc_spec, stat_spec, stat_spec],
+        out_shape=[big, big, acc, stat, stat],
+        name="pair_first" if first else "pair_next",
+        compiler_params=pltpu.CompilerParams(vmem_limit_bytes=VMEM_LIMIT),
+        cost_estimate=pl.CostEstimate(
+            flops=8 * heads * HD * rows * keys,
+            transcendentals=heads * rows * keys,
+            bytes_accessed=4 * heads * rows * keys,
+        ),
+    )(bias, query_grad, query_grad, key_value, key_value, *state)
+
+
+def joined(mine, other, side):
+    top = jnp.maximum(mine[side, 0:1], other[side, 0:1])
+    here = jnp.exp2(mine[side, 0:1] - top)
+    there = jnp.exp2(other[side, 0:1] - top)
+    inverse = 1.0 / (mine[side, 1:2] * here + other[side, 1:2] * there)
+    mean = (mine[side, 2:3] * here + other[side, 2:3] * there) * inverse
+    return top, inverse, mean
+
+
+def key_kernel(*refs):
+    out_k, out_v = refs[-2:]
+    scale = 1.0 / math.sqrt(HD)
+    k_total = None
+    v_total = None
+    for at in range(0, len(refs) - 2, 7):
+        e_ref, u_ref, q_ref, do_ref, pair_ref, mine, other = refs[at : at + 7]
+        q_t = q_ref[...].T.astype(jnp.float32)
+        do_t = do_ref[...].T.astype(jnp.float32)
+        for side in range(2):
+            rows = slice(side * HD, (side + 1) * HD)
+            top, inverse, mean = joined(mine, other, side)
+            factor = jnp.exp2(pair_ref[side, 0:1] - top) * inverse
+            shift = pair_ref[side, 1:2] - mean
+            scaled_q = q_t[rows] * (factor * scale)
+            for_e = jnp.concatenate(
+                [
+                    placed((scaled_q * shift).astype(jnp.bfloat16), side),
+                    placed((do_t[rows] * factor).astype(jnp.bfloat16), side),
+                ],
+                axis=0,
+            )
+            from_e = matmul(e_ref[side], for_e, 1, 1)
+            from_u = matmul(u_ref[side], placed(scaled_q.astype(jnp.bfloat16), side), 1, 1)
+            k_part = from_e[:, : 2 * HD] + from_u
+            v_part = from_e[:, 2 * HD :]
+            k_total = k_part if k_total is None else k_total + k_part
+            v_total = v_part if v_total is None else v_total + v_part
+    out_k[...] = k_total.astype(out_k.dtype)
+    out_v[...] = v_total.astype(out_v.dtype)
+
+
+def key_terms(entries, dtype):
+    heads, keys, rows = entries[0][0].shape
+    steps = heads // 2
+    operands = []
+    in_specs = []
+    for e, u, query_grad, pair, mine, other in entries:
+        operands += [e, u, query_grad, query_grad, pair, mine, other]
+        in_specs += [
+            per_head_spec(keys, rows),
+            per_head_spec(keys, rows),
+            column_spec(rows, 0),
+            column_spec(rows, steps),
+            per_head_spec(8, rows),
+            per_head_spec(8, rows),
+            per_head_spec(8, rows),
+        ]
+    return pl.pallas_call(
+        key_kernel,
+        grid=(steps,),
+        in_specs=in_specs,
+        out_specs=[column_spec(keys, 0), column_spec(keys, 0)],
+        out_shape=[jax.ShapeDtypeStruct((keys, heads * HD), dtype)] * 2,
+        name="key_terms",
+        compiler_params=pltpu.CompilerParams(vmem_limit_bytes=VMEM_LIMIT),
+        cost_estimate=pl.CostEstimate(
+            flops=len(entries) * 6 * heads * HD * rows * keys,
+            transcendentals=0,
+            bytes_accessed=len(entries) * 4 * heads * rows * keys,
+        ),
+    )(*operands)
+
+
+def query_kernel(final, acc, mine, other, *refs):
+    if final:
+        far_o, far_q, out_o, out_q = refs
+    else:
+        out_o, out_q = refs
+    scale = 1.0 / math.sqrt(HD)
+    outs = []
+    grads = []
+    for side in range(2):
+        top, inverse, mean = joined(mine, other, side)
+        factor = jnp.exp2(mine[side, 0:1] - top) * inverse
+        outs.append(acc[side, :HD] * factor)
+        grads.append((acc[side, 2 * HD :] - acc[side, HD : 2 * HD] * mean) * (factor * scale))
+    out_rows = jnp.concatenate(outs, axis=0).T
+    grad_rows = jnp.concatenate(grads, axis=0).T
+    if final:
+        out_rows = out_rows + far_o[...].astype(jnp.float32)
+        grad_rows = grad_rows + far_q[...].astype(jnp.float32)
+    out_o[...] = out_rows.astype(out_o.dtype)
+    out_q[...] = grad_rows.astype(out_q.dtype)
+
+
+def query_terms(acc, mine, other, far):
+    heads, _, rows = acc.shape
+    steps = heads // 2
+    final = far is not None
+    extra = list(far) if final else []
+    return pl.pallas_call(
+        lambda *refs: query_kernel(final, *refs),
+        grid=(steps,),
+        in_specs=[per_head_spec(3 * HD, rows), per_head_spec(8, rows), per_head_spec(8, rows)]
+        + [column_spec(rows, 0)] * len(extra),
+        out_specs=[column_spec(rows, 0), column_spec(rows, 0)],
+        out_shape=[jax.ShapeDtypeStruct((rows, heads * HD), jnp.bfloat16)] * 2,
+        name="query_final" if final else "query_send",
+        compiler_params=pltpu.CompilerParams(vmem_limit_bytes=VMEM_LIMIT),
+        cost_estimate=pl.CostEstimate(
+            flops=8 * heads * HD * rows, transcendentals=0, bytes_accessed=16 * heads * HD * rows
+        ),
+    )(acc, mine, other, *extra)
+
+
+def swapped(x, offset):
+    devices = lax.axis_size("seq")
+    return lax.ppermute(x, "seq", [(i, i ^ offset) for i in range(devices)])
+
+
+def repeats(partners, global_blocks, query_block, key_block, devices):
+    listed = [query_block, (query_block - 1) % devices, (query_block + 1) % devices]
+    listed += [lax.dynamic_index_in_dim(partners[r], query_block, 0, False) for r in range(3)]
+    listed += [global_blocks[0], global_blocks[1]]
+    count = sum((entry == key_block).astype(jnp.float32) for entry in listed)
+    return jnp.where(count > 0.0, jnp.log2(jnp.maximum(count, 1.0)), -1e30).reshape(1)
+
+
+def dense_local(queries, key_states, value_states, grad_output, partners, global_blocks):
+    devices = lax.axis_size("seq")
+    far = devices // 2
+    me = lax.axis_index("seq")
+    key_value = jnp.concatenate([key_states, value_states], axis=1)
+    query_grad = jnp.concatenate([queries, grad_output], axis=1)
+    offsets = list(range(far))
+    key_blocks = [key_value] + [swapped(key_value, o) for o in offsets[1:]]
+    query_blocks = [query_grad, swapped(query_grad, far)]
+    running = [None, None]
+    saved = {}
+    for at in [(0, k) for k in offsets] + [(1, k) for k in offsets]:
+        q, k = at
+        bias = repeats(partners, global_blocks, me ^ (q * far), me ^ offsets[k], devices)
+        e, u, acc, run, pair = pair_terms(bias, query_blocks[q], key_blocks[k], running[q])
+        running[q] = (acc, run)
+        saved[at] = (e, u, query_blocks[q], pair)
+    theirs = swapped(jnp.stack([running[1][1], running[0][1]]), far)
+    others = [theirs[0], theirs[1]]
+    sent = query_terms(running[1][0], running[1][1], others[1], None)
+    came = [swapped(x, far) for x in sent]
+    key_parts = []
+    for k in reversed(offsets):
+        entries = [saved[(q, k)] + (running[q][1], others[q]) for q in range(2)]
+        parts = key_terms(entries, jnp.float32 if k == 0 else jnp.bfloat16)
+        key_parts.append(parts if k == 0 else [swapped(x, offsets[k]) for x in parts])
+    attended, grad_queries = query_terms(running[0][0], running[0][1], others[0], came)
+    grads = [
+        sum(parts[i].astype(jnp.float32) for parts in key_parts).astype(jnp.bfloat16)
+        for i in range(2)
+    ]
+    return (attended, grad_queries, grads[0], grads[1])
+
+
+def local(*operands):
+    devices = lax.axis_size("seq")
+    paired = devices >= 4 and devices & (devices - 1) == 0
+    return (dense_local if paired and devices <= LISTED else routed_local)(*operands)
+
+
 def solution(mesh):
     in_specs = (
         P(("batch", "seq"), None),

time: 712 us -> 199 us (0.28)
  waiting for transfers between devices: 349 us -> 36.3 us
  matrix products: 154 us -> 0 us
  Pallas kernels: 0 us -> 112 us
  local copies, waits for them, and re-layouts: 90.1 us -> 8.51 us
  other arithmetic: 72.1 us -> 2.75 us
  starting transfers between devices: 44.5 us -> 16 us
  between operations: 0.79 us -> 22.3 us
    all_to_all x4 -> x0, waiting for transfers between devices: 223 us -> none  [the longest x1 173 us: route_back(): lax.all_to_all(pieces, 'seq', split_axis=1, concat_axis=1, tiled=True)]
    dot_general x37 -> x0, matrix products: 154 us -> none  [the longest x6 55.6 us: per_head(): lax.dot_general(grad_head, value_head, contract_last, preferred_element_t...]
    pallas_call x0 -> x14, Pallas kernels: none -> 112 us  [the longest x8 70.8 us: pair_terms(): pl.pallas_call(lambda *refs: pair_kernel(first, *refs), grid=(steps,), in...]
    ppermute x4 -> x13, waiting for transfers between devices: 126 us -> 36.3 us  [swapped(): return lax.ppermute(x, 'seq', [(i, i ^ offset) for i in range(devices)])]
    convert_element_type x6 -> x2, other arithmetic: 48.3 us -> 1.84 us  [dense_local(): sum((parts[i].astype(jnp.float32) for parts in key_parts))]
    all_to_all x4 -> x0, starting transfers between devices: 35.1 us -> none  [the longest x1 19.6 us: route_back(): lax.all_to_all(pieces, 'seq', split_axis=1, concat_axis=1, tiled=True)]
    slice x11 -> x2, local copies, waits for them, and re-layouts: 29.1 us -> 0.59 us  [the longest x1 0.58 us: repeats(): listed += [global_blocks[0], global_blocks[1]]]
    unnamed x35 -> x32, local copies, waits for them, and re-layouts: 23.1 us -> 3.92 us
  transfers between devices with their start and end apart: 8 -> 13, of which waited for: 6 -> 5; matrix products, arithmetic and copies ran while one was open for 2% -> 2% of each run, Pallas kernels for 0% -> 41%
where the time goes in v1:
time: 199 us; the launch traced here: 198 us
  Pallas kernels  112 us (56%)
  waiting for transfers between devices  36.3 us (18%)
  between operations  22.3 us (11%)
  starting transfers between devices  16 us (8%)
  local copies, waits for them, and re-layouts  8.51 us (4%)
  other arithmetic  2.75 us (1%)
    pallas_call x8, Pallas kernels, pair_terms(): pl.pallas_call(lambda *refs: pair_kernel(first, *refs), grid=(steps,), in...  70.8 us
    ppermute x13, waiting for transfers between devices, swapped(): return lax.ppermute(x, 'seq', [(i, i ^ offset) for i in range(devices)])  36.3 us
    pallas_call x4, Pallas kernels, key_terms(): pl.pallas_call(key_kernel, grid=(steps,), in_specs=in_specs, out_specs=[c...  33.7 us
    ppermute x13, starting transfers between devices, swapped(): return lax.ppermute(x, 'seq', [(i, i ^ offset) for i in range(devices)])  16 us
    pallas_call x2, Pallas kernels, query_terms(): pl.pallas_call(lambda *refs: query_kernel(final, *refs), grid=(steps,), i...  7.36 us
  transfers between devices with their start and end apart: 13, of which 5 were waited for; matrix products, arithmetic and copies ran while one was open for 2% of the time, Pallas kernels for 41%

profile of v1, /device:TPU:0, one launch (start us, length us, event | category | flops | bytes accessed | tf_op | source)
XLA Modules:
  0.0 197.7 jit_solution(18119479404902140222)
XLA Ops:
  0.7 1.0 constant_dynamic-update-slice_fusion.1
  1.7 1.1 constant_dynamic-update-slice_fusion.refs_1_.refs_2_.refs_3_
  2.8 4.1 %collective-permute-start.3 = (bf16[512,768]{1,0:T(8,128)(2,1)S(1)}, bf16[512,768]{1,0:T(8,128)(2,1)S(1)}, u32[]{:S(2)}, u32[]{:S(2)}) collective-permute-start(bf16[512,768]{1,0:T(8,128)(2,1)S(1)} %constant_dynamic-update-slice_fusion.refs_1_.refs_2_.refs_3_), channel_id=1, source_target_pairs={{0,16},{4,20},{8,24},{12,28},{16,0},{20,4},{24,8},{28,12},{1,17},{... | collective-permute-start | bytes 2359304 | tf_op jit(solution)/shard_map/ppermute | solution.py:385
  6.9 1.0 constant_dynamic-update-slice_fusion.3
  7.9 1.1 constant_dynamic-update-slice_fusion.2.refs_3_.refs_4_
  9.0 1.6 collective-permute-start.2
  10.6 1.6 collective-permute-start.1
  35.8 8.3 %pair_first.2 = (bf16[6,512,512]{2,1,0:T(8,128)(2,1)}, bf16[6,512,512]{2,1,0:T(8,128)(2,1)}, f32[6,192,512]{2,1,0:T(8,128)}, f32[6,8,512]{2,1,0:T(8,128)}, f32[6,8,512]{2,1,0:T(8,128)}) custom-call(f32[1]{0:T(128)} %bitcast.8.refs_0_, bf16[512,768]{1,0:T(8,128)(2,1)} %copy-done, bf16[512,768]{1,0:T(8,128)(2,1)} %copy-done, bf16[512,768]{1,0:T(8,128)(2,1)} %copy-done.2, ...), custom_call_target="tpu_custom_call" | custom-call | flops 805306368 | bytes 6291456 | tf_op jit(solution)/shard_map/pair_first/pallas_call | solution.py:245
  45.0 8.3 %pair_first.3 = (bf16[6,512,512]{2,1,0:T(8,128)(2,1)}, bf16[6,512,512]{2,1,0:T(8,128)(2,1)}, f32[6,192,512]{2,1,0:T(8,128)}, f32[6,8,512]{2,1,0:T(8,128)}, f32[6,8,512]{2,1,0:T(8,128)}) custom-call(f32[1]{0:T(128)} %bitcast.15.refs_0_, bf16[512,768]{1,0:T(8,128)(2,1)} %copy-done.1, bf16[512,768]{1,0:T(8,128)(2,1)} %copy-done.1, bf16[512,768]{1,0:T(8,128)(2,1)} %copy-done.2, ...), custom_call_target="tpu_custom_call" | custom-call | flops 805306368 | bytes 6291456 | tf_op jit(solution)/shard_map/pair_first/pallas_call | solution.py:245
  53.3 9.0 %pair_next.9 = (bf16[6,512,512]{2,1,0:T(8,128)(2,1)}, bf16[6,512,512]{2,1,0:T(8,128)(2,1)}, f32[6,192,512]{2,1,0:T(8,128)}, f32[6,8,512]{2,1,0:T(8,128)}, f32[6,8,512]{2,1,0:T(8,128)}) custom-call(f32[1]{0:T(128)} %bitcast.14.refs_0_, bf16[512,768]{1,0:T(8,128)(2,1)} %copy-done.1, bf16[512,768]{1,0:T(8,128)(2,1)} %copy-done.1, ...), custom_call_target="tpu_custom_call" | custom-call | flops 805306368 | bytes 6291456 | tf_op jit(solution)/shard_map/pair_next/pallas_call | solution.py:245
  62.3 9.0 %pair_next.6 = (bf16[6,512,512]{2,1,0:T(8,128)(2,1)}, bf16[6,512,512]{2,1,0:T(8,128)(2,1)}, f32[6,192,512]{2,1,0:T(8,128)}, f32[6,8,512]{2,1,0:T(8,128)}, f32[6,8,512]{2,1,0:T(8,128)}) custom-call(f32[1]{0:T(128)} %bitcast.7.refs_0_, bf16[512,768]{1,0:T(8,128)(2,1)} %copy-done, bf16[512,768]{1,0:T(8,128)(2,1)} %copy-done, ...), custom_call_target="tpu_custom_call" | custom-call | flops 805306368 | bytes 6291456 | tf_op jit(solution)/shard_map/pair_next/pallas_call | solution.py:245
  71.3 9.0 %pair_next.10 = (bf16[6,512,512]{2,1,0:T(8,128)(2,1)}, bf16[6,512,512]{2,1,0:T(8,128)(2,1)}, f32[6,192,512]{2,1,0:T(8,128)}, f32[6,8,512]{2,1,0:T(8,128)}, f32[6,8,512]{2,1,0:T(8,128)}) custom-call(f32[1]{0:T(128)} %bitcast.13.refs_0_, bf16[512,768]{1,0:T(8,128)(2,1)} %copy-done.1, bf16[512,768]{1,0:T(8,128)(2,1)} %copy-done.1, ...), custom_call_target="tpu_custom_call" | custom-call | flops 805306368 | bytes 6291456 | tf_op jit(solution)/shard_map/pair_next/pallas_call | solution.py:245
  80.3 9.0 %pair_next.7 = (bf16[6,512,512]{2,1,0:T(8,128)(2,1)}, bf16[6,512,512]{2,1,0:T(8,128)(2,1)}, f32[6,192,512]{2,1,0:T(8,128)}, f32[6,8,512]{2,1,0:T(8,128)}, f32[6,8,512]{2,1,0:T(8,128)}) custom-call(f32[1]{0:T(128)} %bitcast.6.refs_0_, bf16[512,768]{1,0:T(8,128)(2,1)} %copy-done, bf16[512,768]{1,0:T(8,128)(2,1)} %copy-done, ...), custom_call_target="tpu_custom_call" | custom-call | flops 805306368 | bytes 6291456 | tf_op jit(solution)/shard_map/pair_next/pallas_call | solution.py:245
  90.3 9.0 %pair_next.11 = (bf16[6,512,512]{2,1,0:T(8,128)(2,1)}, bf16[6,512,512]{2,1,0:T(8,128)(2,1)}, f32[6,192,512]{2,1,0:T(8,128)}, f32[6,8,512]{2,1,0:T(8,128)}, f32[6,8,512]{2,1,0:T(8,128)}) custom-call(f32[1]{0:T(128)} %bitcast.12.refs_0_, bf16[512,768]{1,0:T(8,128)(2,1)} %copy-done.1, bf16[512,768]{1,0:T(8,128)(2,1)} %copy-done.1, bf16[512,768]{1,0:T(8,128)(2,1)} %copy-done.3, ...), custom_call_target="tpu_custom_call" | custom-call | flops 805306368 | bytes 6291456 | tf_op jit(solution)/shard_map/pair_next/pallas_call | solution.py:245
  99.3 9.1 %pair_next.8 = (bf16[6,512,512]{2,1,0:T(8,128)(2,1)}, bf16[6,512,512]{2,1,0:T(8,128)(2,1)}, f32[6,192,512]{2,1,0:T(8,128)}, f32[6,8,512]{2,1,0:T(8,128)}, f32[6,8,512]{2,1,0:T(8,128)}) custom-call(f32[1]{0:T(128)} %bitcast.5.refs_0_, bf16[512,768]{1,0:T(8,128)(2,1)} %copy-done, bf16[512,768]{1,0:T(8,128)(2,1)} %copy-done, bf16[512,768]{1,0:T(8,128)(2,1)} %copy-done.3, ...), custom_call_target="tpu_custom_call" | custom-call | flops 805306368 | bytes 6291456 | tf_op jit(solution)/shard_map/pair_next/pallas_call | solution.py:245
  109.6 10.4 %collective-permute-done.4 = f32[2,6,8,512]{3,2,1,0:T(8,128)S(1)} collective-permute-done((f32[2,6,8,512]{3,2,1,0:T(8,128)S(1)}, f32[2,6,8,512]{3,2,1,0:T(8,128)S(1)}, u32[]{:S(2)}, u32[]{:S(2)}) %collective-permute-start.4) | collective-permute-done | bytes 196640 | tf_op jit(solution)/shard_map/ppermute | solution.py:385
  120.7 3.5 %query_send.1 = (bf16[512,384]{1,0:T(8,128)(2,1)}, bf16[512,384]{1,0:T(8,128)(2,1)}) custom-call(f32[6,192,512]{2,1,0:T(8,128)} %get-tuple-element.71.refs_0_, f32[6,8,512]{2,1,0:T(8,128)} %get-tuple-element.70.refs_1_.refs_12_, f32[6,8,512]{2,1,0:T(8,128)} %get-tuple-element.108.refs_2_.refs_13_), custom_call_target="tpu_custom_call" | custom-call | flops 1572864 | bytes 3145728 | tf_op jit(solution)/shard_map/query_send/pallas_call | solution.py:368
  124.2 8.3 %key_terms.6 = (bf16[512,384]{1,0:T(8,128)(2,1)}, bf16[512,384]{1,0:T(8,128)(2,1)}) custom-call(bf16[6,512,512]{2,1,0:T(8,128)(2,1)} %get-tuple-element.90.refs_0_, bf16[6,512,512]{2,1,0:T(8,128)(2,1)} %get-tuple-element.91.refs_1_, bf16[512,768]{1,0:T(8,128)(2,1)} %copy-done, bf16[512,768]{1,0:T(8,128)(2,1)} %copy-done, ...), custom_call_target="tpu_custom_call" | custom-call | flops 1207959552 | bytes 12582912 | tf_op jit(solution)/shard_map/key_terms/pallas_call | solution.py:325
  132.5 1.6 collective-permute-start.9
  134.1 2.9 %collective-permute-start.6 = (bf16[512,384]{1,0:T(8,128)(2,1)S(1)}, bf16[512,384]{1,0:T(8,128)(2,1)S(1)}, u32[]{:S(2)}, u32[]{:S(2)}) collective-permute-start(bf16[512,384]{1,0:T(8,128)(2,1)S(1)} %copy-done.13), channel_id=1, source_target_pairs={{0,16},{4,20},{8,24},{12,28},{16,0},{20,4},{24,8},{28,12},{1,17},{... | collective-permute-start | bytes 1179656 | tf_op jit(solution)/shard_map/ppermute | solution.py:385
  137.1 8.3 %key_terms.5 = (bf16[512,384]{1,0:T(8,128)(2,1)}, bf16[512,384]{1,0:T(8,128)(2,1)}) custom-call(bf16[6,512,512]{2,1,0:T(8,128)(2,1)} %get-tuple-element.83.refs_0_, bf16[6,512,512]{2,1,0:T(8,128)(2,1)} %get-tuple-element.84.refs_1_, bf16[512,768]{1,0:T(8,128)(2,1)} %copy-done, bf16[512,768]{1,0:T(8,128)(2,1)} %copy-done, ...), custom_call_target="tpu_custom_call" | custom-call | flops 1207959552 | bytes 12582912 | tf_op jit(solution)/shard_map/key_terms/pallas_call | solution.py:325
  145.4 8.4 %key_terms.4 = (bf16[512,384]{1,0:T(8,128)(2,1)}, bf16[512,384]{1,0:T(8,128)(2,1)}) custom-call(bf16[6,512,512]{2,1,0:T(8,128)(2,1)} %get-tuple-element.76.refs_0_, bf16[6,512,512]{2,1,0:T(8,128)(2,1)} %get-tuple-element.77.refs_1_, bf16[512,768]{1,0:T(8,128)(2,1)} %copy-done, bf16[512,768]{1,0:T(8,128)(2,1)} %copy-done, ...), custom_call_target="tpu_custom_call" | custom-call | flops 1207959552 | bytes 12582912 | tf_op jit(solution)/shard_map/key_terms/pallas_call | solution.py:325
  153.9 1.9 collective-permute-start.7
  155.8 1.5 collective-permute-start.12
  157.3 4.3 %collective-permute-done.5.refs_3_ = bf16[512,384]{1,0:T(8,128)(2,1)S(1)} collective-permute-done((bf16[512,384]{1,0:T(8,128)(2,1)S(1)}, bf16[512,384]{1,0:T(8,128)(2,1)S(1)}, u32[]{:S(2)}, u32[]{:S(2)}) %collective-permute-start.5) | collective-permute-done | bytes 393248 | tf_op jit(solution)/shard_map/ppermute | solution.py:385
  161.6 8.3 %collective-permute-done.6.refs_4_ = bf16[512,384]{1,0:T(8,128)(2,1)S(1)} collective-permute-done((bf16[512,384]{1,0:T(8,128)(2,1)S(1)}, bf16[512,384]{1,0:T(8,128)(2,1)S(1)}, u32[]{:S(2)}, u32[]{:S(2)}) %collective-permute-start.6) | collective-permute-done | bytes 393248 | tf_op jit(solution)/shard_map/ppermute | solution.py:385
  169.9 8.7 %key_terms.7 = (f32[512,384]{1,0:T(8,128)}, f32[512,384]{1,0:T(8,128)}) custom-call(bf16[6,512,512]{2,1,0:T(8,128)(2,1)} %get-tuple-element.97.refs_0_, bf16[6,512,512]{2,1,0:T(8,128)(2,1)} %get-tuple-element.98.refs_1_, bf16[512,768]{1,0:T(8,128)(2,1)} %copy-done, bf16[512,768]{1,0:T(8,128)(2,1)} %copy-done, f32[6,8,512]{2,1,0:T(8,128)} %get-tuple-element.99.refs_4_, ...), custom_call_target="tpu_custom_call" | custom-call | flops 1207959552 | bytes 12582912 | tf_op jit(solution)/shard_map/key_terms/pallas_call | solution.py:325
  178.7 3.9 %query_final.1 = (bf16[512,384]{1,0:T(8,128)(2,1)}, bf16[512,384]{1,0:T(8,128)(2,1)}) custom-call(f32[6,192,512]{2,1,0:T(8,128)} %get-tuple-element.62.refs_0_, f32[6,8,512]{2,1,0:T(8,128)} %get-tuple-element.63.refs_1_.refs_5_, f32[6,8,512]{2,1,0:T(8,128)} %get-tuple-element.109.refs_2_.refs_6_, bf16[512,384]{1,0:T(8,128)(2,1)} %copy-done.7, ...), custom_call_target="tpu_custom_call" | custom-call | flops 1572864 | bytes 3145728 | tf_op jit(solution)/shard_map/query_final/pallas_call | solution.py:368
  182.6 0.9 add_convert_fusion.1
  183.5 6.5 %collective-permute-done.11 = bf16[512,384]{1,0:T(8,128)(2,1)S(1)} collective-permute-done((bf16[512,384]{1,0:T(8,128)(2,1)S(1)}, bf16[512,384]{1,0:T(8,128)(2,1)S(1)}, u32[]{:S(2)}, u32[]{:S(2)}) %collective-permute-start.11) | collective-permute-done | bytes 393248 | tf_op jit(solution)/shard_map/ppermute | solution.py:385
  190.0 6.7 %collective-permute-done.10 = bf16[512,384]{1,0:T(8,128)(2,1)S(1)} collective-permute-done((bf16[512,384]{1,0:T(8,128)(2,1)}, bf16[512,384]{1,0:T(8,128)(2,1)S(1)}, u32[]{:S(2)}, u32[]{:S(2)}) %collective-permute-start.10) | collective-permute-done | bytes 393248 | tf_op jit(solution)/shard_map/ppermute | solution.py:385
  196.8 0.9 add_convert_fusion
  (50 shorter events, 6.0 us)
Async XLA Ops:
  0.6 11.9 %copy-start.9 = (s32[2]{0:T(128)S(1)}, s32[2]{0:T(128)}, u32[]{:S(2)}) copy-start(s32[2]{0:T(128)} %param.11) | copy-start | bytes 28
  0.6 17.7 %copy-start.10 = (s32[3,8]{1,0:T(4,128)S(1)}, s32[3,8]{1,0:T(4,128)}, u32[]{:S(2)}) copy-start(s32[3,8]{1,0:T(4,128)} %param.10) | copy-start | bytes 292
  2.8 33.0 %copy-start = (bf16[512,768]{1,0:T(8,128)(2,1)}, bf16[512,768]{1,0:T(8,128)(2,1)S(1)}, u32[]{:S(2)}) copy-start(bf16[512,768]{1,0:T(8,128)(2,1)S(1)} %constant_dynamic-update-slice_fusion.refs_1_.refs_2_.refs_3_) | copy-start | bytes 2359300
  2.8 41.3 %collective-permute-start.3 = (bf16[512,768]{1,0:T(8,128)(2,1)S(1)}, bf16[512,768]{1,0:T(8,128)(2,1)S(1)}, u32[]{:S(2)}, u32[]{:S(2)}) collective-permute-start(bf16[512,768]{1,0:T(8,128)(2,1)S(1)} %constant_dynamic-update-slice_fusion.refs_1_.refs_2_.refs_3_), channel_id=1, source_target_pairs={{0,16},{4,20},{8,24},{12,28},{16,0},{20,4},{24,8},{28,12},{1,17},{... | collective-permute-start | bytes 2359304 | tf_op jit(solution)/shard_map/ppermute | solution.py:385
  9.0 26.8 %copy-start.2 = (bf16[512,768]{1,0:T(8,128)(2,1)}, bf16[512,768]{1,0:T(8,128)(2,1)S(1)}, u32[]{:S(2)}) copy-start(bf16[512,768]{1,0:T(8,128)(2,1)S(1)} %constant_dynamic-update-slice_fusion.2.refs_3_.refs_4_) | copy-start | bytes 2359300
  9.0 44.3 %collective-permute-start.2 = (bf16[512,768]{1,0:T(8,128)(2,1)S(1)}, bf16[512,768]{1,0:T(8,128)(2,1)}, u32[]{:S(2)}, u32[]{:S(2)}) collective-permute-start(bf16[512,768]{1,0:T(8,128)(2,1)S(1)} %constant_dynamic-update-slice_fusion.2.refs_3_.refs_4_), channel_id=1, source_target_pairs={{0,4},{4,0},{8,12},{12,8},{16,20},{20,16},{24,28},{28,24},{1,5},{5... | collective-permute-start | bytes 2359304 | tf_op jit(solution)/shard_map/ppermute | solution.py:385
  10.6 60.7 %collective-permute-start.1 = (bf16[512,768]{1,0:T(8,128)(2,1)S(1)}, bf16[512,768]{1,0:T(8,128)(2,1)}, u32[]{:S(2)}, u32[]{:S(2)}) collective-permute-start(bf16[512,768]{1,0:T(8,128)(2,1)S(1)} %constant_dynamic-update-slice_fusion.2.refs_3_.refs_4_), channel_id=1, source_target_pairs={{0,8},{4,12},{8,0},{12,4},{16,24},{20,28},{24,16},{28,20},{1,9},{5... | collective-permute-start | bytes 2359304 | tf_op jit(solution)/shard_map/ppermute | solution.py:385
  12.2 77.2 %collective-permute-start = (bf16[512,768]{1,0:T(8,128)(2,1)S(1)}, bf16[512,768]{1,0:T(8,128)(2,1)S(1)}, u32[]{:S(2)}, u32[]{:S(2)}) collective-permute-start(bf16[512,768]{1,0:T(8,128)(2,1)S(1)} %constant_dynamic-update-slice_fusion.2.refs_3_.refs_4_), channel_id=1, source_target_pairs={{0,12},{4,8},{8,4},{12,0},{16,28},{20,24},{24,20},{28,16},{1,13},{... | collective-permute-start | bytes 2359304 | tf_op jit(solution)/shard_map/ppermute | solution.py:385
  44.1 0.9 copy-start.1
  89.3 0.9 copy-start.3
  99.3 9.2 %copy-start.4 = (f32[6,8,512]{2,1,0:T(8,128)S(1)}, f32[6,8,512]{2,1,0:T(8,128)}, u32[]{:S(2)}) copy-start(f32[6,8,512]{2,1,0:T(8,128)} %get-tuple-element.70.refs_1_.refs_12_) | copy-start | bytes 294916
  109.3 10.7 %collective-permute-start.4 = (f32[2,6,8,512]{3,2,1,0:T(8,128)S(1)}, f32[2,6,8,512]{3,2,1,0:T(8,128)S(1)}, u32[]{:S(2)}, u32[]{:S(2)}) collective-permute-start(f32[2,6,8,512]{3,2,1,0:T(8,128)S(1)} %pad_maximum_fusion), channel_id=1, source_target_pairs={{0,16},{4,20},{8,24},{12,28},{16,0},{20,4},{24,8},{28,12},{1,17},{... | collective-permute-start | bytes 589832 | tf_op jit(solution)/shard_map/ppermute | solution.py:385
  124.2 9.9 %copy-start.14 = (bf16[512,384]{1,0:T(8,128)(2,1)S(1)}, bf16[512,384]{1,0:T(8,128)(2,1)}, u32[]{:S(2)}) copy-start(bf16[512,384]{1,0:T(8,128)(2,1)} %get-tuple-element.72) | copy-start | bytes 1179652
  124.2 9.9 %copy-start.13 = (bf16[512,384]{1,0:T(8,128)(2,1)S(1)}, bf16[512,384]{1,0:T(8,128)(2,1)}, u32[]{:S(2)}) copy-start(bf16[512,384]{1,0:T(8,128)(2,1)} %get-tuple-element.73) | copy-start | bytes 1179652
  132.5 23.2 %collective-permute-start.9 = (bf16[512,384]{1,0:T(8,128)(2,1)}, bf16[512,384]{1,0:T(8,128)(2,1)S(1)}, u32[]{:S(2)}, u32[]{:S(2)}) collective-permute-start(bf16[512,384]{1,0:T(8,128)(2,1)} %get-tuple-element.96), channel_id=1, source_target_pairs={{0,4},{4,0},{8,12},{12,8},{16,20},{20,16},{24,28},{28,24},{1,5},{5... | collective-permute-start | bytes 1179656 | tf_op jit(solution)/shard_map/ppermute | solution.py:385
  134.1 27.5 %collective-permute-start.5 = (bf16[512,384]{1,0:T(8,128)(2,1)S(1)}, bf16[512,384]{1,0:T(8,128)(2,1)S(1)}, u32[]{:S(2)}, u32[]{:S(2)}) collective-permute-start(bf16[512,384]{1,0:T(8,128)(2,1)S(1)} %copy-done.14), channel_id=1, source_target_pairs={{0,16},{4,20},{8,24},{12,28},{16,0},{20,4},{24,8},{28,12},{1,17},{... | collective-permute-start | bytes 1179656 | tf_op jit(solution)/shard_map/ppermute | solution.py:385
  134.1 35.8 %collective-permute-start.6 = (bf16[512,384]{1,0:T(8,128)(2,1)S(1)}, bf16[512,384]{1,0:T(8,128)(2,1)S(1)}, u32[]{:S(2)}, u32[]{:S(2)}) collective-permute-start(bf16[512,384]{1,0:T(8,128)(2,1)S(1)} %copy-done.13), channel_id=1, source_target_pairs={{0,16},{4,20},{8,24},{12,28},{16,0},{20,4},{24,8},{28,12},{1,17},{... | collective-permute-start | bytes 1179656 | tf_op jit(solution)/shard_map/ppermute | solution.py:385
  145.3 37.2 %collective-permute-start.8 = (bf16[512,384]{1,0:T(8,128)(2,1)}, bf16[512,384]{1,0:T(8,128)(2,1)S(1)}, u32[]{:S(2)}, u32[]{:S(2)}) collective-permute-start(bf16[512,384]{1,0:T(8,128)(2,1)} %get-tuple-element.89), channel_id=1, source_target_pairs={{0,8},{4,12},{8,0},{12,4},{16,24},{20,28},{24,16},{28,20},{1,9},{5... | collective-permute-start | bytes 1179656 | tf_op jit(solution)/shard_map/ppermute | solution.py:385
  145.4 10.4 %copy-start.11 = (bf16[512,384]{1,0:T(8,128)(2,1)S(1)}, bf16[512,384]{1,0:T(8,128)(2,1)}, u32[]{:S(2)}) copy-start(bf16[512,384]{1,0:T(8,128)(2,1)} %get-tuple-element.106) | copy-start | bytes 1179652
  145.4 16.2 %copy-start.12 = (bf16[512,384]{1,0:T(8,128)(2,1)S(1)}, bf16[512,384]{1,0:T(8,128)(2,1)}, u32[]{:S(2)}) copy-start(bf16[512,384]{1,0:T(8,128)(2,1)} %get-tuple-element.105) | copy-start | bytes 1179652
  153.9 28.7 %collective-permute-start.7 = (bf16[512,384]{1,0:T(8,128)(2,1)}, bf16[512,384]{1,0:T(8,128)(2,1)S(1)}, u32[]{:S(2)}, u32[]{:S(2)}) collective-permute-start(bf16[512,384]{1,0:T(8,128)(2,1)} %get-tuple-element.82), channel_id=1, source_target_pairs={{0,12},{4,8},{8,4},{12,0},{16,28},{20,24},{24,20},{28,16},{1,13},{... | collective-permute-start | bytes 1179656 | tf_op jit(solution)/shard_map/ppermute | solution.py:385
  155.8 27.7 %collective-permute-start.12 = (bf16[512,384]{1,0:T(8,128)(2,1)S(1)}, bf16[512,384]{1,0:T(8,128)(2,1)S(1)}, u32[]{:S(2)}, u32[]{:S(2)}) collective-permute-start(bf16[512,384]{1,0:T(8,128)(2,1)S(1)} %copy-done.11), channel_id=1, source_target_pairs={{0,4},{4,0},{8,12},{12,8},{16,20},{20,16},{24,28},{28,24},{1,5},{5... | collective-permute-start | bytes 1179656 | tf_op jit(solution)/shard_map/ppermute | solution.py:385
  161.6 17.1 %copy-start.7 = (bf16[512,384]{1,0:T(8,128)(2,1)}, bf16[512,384]{1,0:T(8,128)(2,1)S(1)}, u32[]{:S(2)}) copy-start(bf16[512,384]{1,0:T(8,128)(2,1)S(1)} %collective-permute-done.5.refs_3_) | copy-start | bytes 1179652
  161.6 28.4 %collective-permute-start.11 = (bf16[512,384]{1,0:T(8,128)(2,1)S(1)}, bf16[512,384]{1,0:T(8,128)(2,1)S(1)}, u32[]{:S(2)}, u32[]{:S(2)}) collective-permute-start(bf16[512,384]{1,0:T(8,128)(2,1)S(1)} %copy-done.12), channel_id=1, source_target_pairs={{0,8},{4,12},{8,0},{12,4},{16,24},{20,28},{24,16},{28,20},{1,9},{5... | collective-permute-start | bytes 1179656 | tf_op jit(solution)/shard_map/ppermute | solution.py:385
  169.9 8.7 %copy-start.8 = (bf16[512,384]{1,0:T(8,128)(2,1)}, bf16[512,384]{1,0:T(8,128)(2,1)S(1)}, u32[]{:S(2)}) copy-start(bf16[512,384]{1,0:T(8,128)(2,1)S(1)} %collective-permute-done.6.refs_4_) | copy-start | bytes 1179652
  169.9 26.8 %collective-permute-start.10 = (bf16[512,384]{1,0:T(8,128)(2,1)}, bf16[512,384]{1,0:T(8,128)(2,1)S(1)}, u32[]{:S(2)}, u32[]{:S(2)}) collective-permute-start(bf16[512,384]{1,0:T(8,128)(2,1)} %get-tuple-element.104), channel_id=1, source_target_pairs={{0,12},{4,8},{8,4},{12,0},{16,28},{20,24},{24,20},{28,16},{1,13},{... | collective-permute-start | bytes 1179656 | tf_op jit(solution)/shard_map/ppermute | solution.py:385
  178.7 3.9 %copy-start.6 = (f32[512,384]{1,0:T(8,128)S(1)}, f32[512,384]{1,0:T(8,128)}, u32[]{:S(2)}) copy-start(f32[512,384]{1,0:T(8,128)} %get-tuple-element.103) | copy-start | bytes 2359300
  178.7 18.1 %copy-start.5 = (f32[512,384]{1,0:T(8,128)S(1)}, f32[512,384]{1,0:T(8,128)}, u32[]{:S(2)}) copy-start(f32[512,384]{1,0:T(8,128)} %get-tuple-element.107) | copy-start | bytes 2359300

commit v2 on v1

--- a/solution.py
+++ b/solution.py
@@ -154,7 +154,8 @@
 
 LISTED = 8
 TO_LOG2 = 1.0 / (math.log(2.0) * math.sqrt(HD))
-VMEM_LIMIT = 56 * 1024 * 1024
+VMEM_LIMIT = 60 * 1024 * 1024
+CHUNK = 256
 
 
 def matmul(a, b, contract_a, contract_b):
@@ -168,52 +169,119 @@
     return jnp.concatenate([rows, blank] if side == 0 else [blank, rows], axis=0)
 
 
-def pair_kernel(first, bias_ref, q_ref, do_ref, k_ref, v_ref, *refs):
+def listed_times(partners_ref, globals_ref, query_block, key_block, devices):
+    count = jnp.int32(0)
+    entries = [query_block, lax.rem(query_block + devices - 1, devices)]
+    entries += [lax.rem(query_block + 1, devices)]
+    entries += [partners_ref[r, query_block] for r in range(partners_ref.shape[0])]
+    entries += [globals_ref[g] for g in range(globals_ref.shape[0])]
+    for entry in entries:
+        count = count + jnp.where(entry == key_block, 1, 0)
+    return count
+
+
+def pair_kernel(first, moves, partners_ref, globals_ref, q_ref, do_ref, k_ref, v_ref, *refs):
     if first:
         e_ref, u_ref, acc_out, run_out, pair_out = refs
     else:
         acc_in, run_in, e_ref, u_ref, acc_out, run_out, pair_out = refs
+    devices = lax.axis_size("seq")
+    me = lax.axis_index("seq")
+    count = listed_times(
+        partners_ref, globals_ref, me ^ moves[0], me ^ moves[1], devices
+    ).astype(jnp.float32)
+    bias = jnp.log2(jnp.full((1, CHUNK), jnp.maximum(count, 1.0), jnp.float32))
+    bias = jnp.where(count > 0.0, bias, -1e30)
     keys = k_ref[...]
     values = v_ref[...]
-    q_t = q_ref[...].T
+    keys_twice = jnp.concatenate([keys, keys], axis=1)
+    q_t = q_ref[...].T.astype(jnp.float32) * TO_LOG2
+    q_high = q_t.astype(jnp.bfloat16)
+    q_low = (q_t - q_high.astype(jnp.float32)).astype(jnp.bfloat16)
     do_t = do_ref[...].T
     k_t = keys.T
     v_t = values.T
-    bias = bias_ref[0]
-    for side in range(2):
-        rows = slice(side * HD, (side + 1) * HD)
-        scores = matmul(keys, placed(q_t[rows], side), 1, 0) * TO_LOG2
+    ones = jnp.ones((16, keys.shape[0]), jnp.bfloat16)
+    units = [(side, at) for side in range(2) for at in range(q_ref.shape[0] // CHUNK)]
+    halves = [slice(0, HD), slice(HD, 2 * HD)]
+    lanes = [slice(at * CHUNK, (at + 1) * CHUNK) for at in range(q_ref.shape[0] // CHUNK)]
+    state = [{} for _ in units]
+
+    def products(n):
+        side, at = units[n]
+        rows, cols = halves[side], lanes[at]
+        both_q = [placed(q_high[rows, cols], side), placed(q_low[rows, cols], side)]
+        state[n]["scores"] = matmul(keys_twice, jnp.concatenate(both_q, axis=0), 1, 0)
+
+    def exponents(n):
+        side, at = units[n]
+        scores = state[n].pop("scores")
         peak = jnp.max(scores, axis=0, keepdims=True)
-        exponent = jnp.exp2(scores - peak)
-        total = jnp.sum(exponent, axis=0, keepdims=True)
-        low = exponent.astype(jnp.bfloat16)
-        e_ref[side] = low
-        both = matmul(jnp.concatenate([v_t[rows], k_t[rows]], axis=0), low, 1, 0)
-        grad_weights = matmul(values, placed(do_t[rows], side), 1, 0)
-        dots = jnp.sum(both[:HD] * do_t[rows].astype(jnp.float32), axis=0, keepdims=True)
+        low = jnp.exp2(scores - peak).astype(jnp.bfloat16)
+        e_ref[side, :, lanes[at]] = low
+        state[n]["peak"] = peak
+        state[n]["low"] = low
+
+    def sums(n):
+        side, at = units[n]
+        rows = halves[side]
+        left = jnp.concatenate([v_t[rows], k_t[rows], ones], axis=0)
+        state[n]["both"] = matmul(left, state[n]["low"], 1, 0)
+
+    def centre(n):
+        side, at = units[n]
+        both = state[n]["both"]
+        total = both[2 * HD : 2 * HD + 1]
+        left = do_t[halves[side], lanes[at]].astype(jnp.float32)
+        dots = jnp.sum(both[:HD] * left, axis=0, keepdims=True)
         mean = dots / total
-        centred = (exponent * (grad_weights - mean)).astype(jnp.bfloat16)
-        u_ref[side] = centred
-        moved = matmul(k_t[rows], centred, 1, 0) + mean * both[HD:]
-        peak = peak + bias
+        grad = matmul(values, placed(do_t[halves[side], lanes[at]], side), 1, 0)
+        centred = state[n].pop("low") * (grad - mean).astype(jnp.bfloat16)
+        u_ref[side, :, lanes[at]] = centred
+        state[n].update(total=total, dots=dots, mean=mean, centred=centred)
+
+    def finish(n):
+        side, at = units[n]
+        cols = lanes[at]
+        one = state[n]
+        both = one["both"]
+        moved = matmul(k_t[halves[side]], one["centred"], 1, 0) + one["mean"] * both[HD : 2 * HD]
+        peak = one["peak"] + bias
         if first:
-            acc_out[side, : 2 * HD] = both
-            acc_out[side, 2 * HD :] = moved
-            top, run_total, run_dots = peak, total, dots
+            acc_out[side, : 2 * HD, cols] = both[: 2 * HD]
+            acc_out[side, 2 * HD :, cols] = moved
+            top, total, dots = peak, one["total"], one["dots"]
         else:
-            old = run_in[side, 0:1]
+            at_row = 3 * side
+            old = run_in[0, at_row : at_row + 1, cols]
             top = jnp.maximum(old, peak)
             keep = jnp.exp2(old - top)
             take = jnp.exp2(peak - top)
-            acc_out[side, : 2 * HD] = acc_in[side, : 2 * HD] * keep + both * take
-            acc_out[side, 2 * HD :] = acc_in[side, 2 * HD :] * keep + moved * take
-            run_total = run_in[side, 1:2] * keep + total * take
-            run_dots = run_in[side, 2:3] * keep + dots * take
-        run_out[side, 0:1] = top
-        run_out[side, 1:2] = run_total
-        run_out[side, 2:3] = run_dots
-        pair_out[side, 0:1] = peak
-        pair_out[side, 1:2] = mean
+            acc_out[side, : 2 * HD, cols] = (
+                acc_in[side, : 2 * HD, cols] * keep + both[: 2 * HD] * take
+            )
+            acc_out[side, 2 * HD :, cols] = acc_in[side, 2 * HD :, cols] * keep + moved * take
+            total = run_in[0, at_row + 1 : at_row + 2, cols] * keep + one["total"] * take
+            dots = run_in[0, at_row + 2 : at_row + 3, cols] * keep + one["dots"] * take
+        for row, value in enumerate((top, total, dots)):
+            run_out[0, 3 * side + row : 3 * side + row + 1, cols] = value
+        for row, value in enumerate((peak, one["mean"])):
+            pair_out[0, 3 * side + row : 3 * side + row + 1, cols] = value
+        state[n].clear()
+
+    last = len(units) - 1
+    products(0)
+    products(1)
+    for n in range(len(units)):
+        exponents(n)
+        sums(n)
+        if n + 2 <= last:
+            products(n + 2)
+        if n >= 1:
+            centre(n - 1)
+            finish(n - 1)
+    centre(last)
+    finish(last)
 
 
 def head_pairs(features):
@@ -228,7 +296,11 @@
     return pl.BlockSpec((2,) + tail, lambda p: (p,) + (0,) * len(tail))
 
 
-def pair_terms(bias, query_grad, key_value, running):
+def stat_rows(rows):
+    return pl.BlockSpec((1, 8, rows), lambda p: (p, 0, 0))
+
+
+def pair_terms(tables, moves, query_grad, key_value, running):
     rows, columns = query_grad.shape
     keys = key_value.shape[0]
     features = columns // 2
@@ -237,15 +309,16 @@
     first = running is None
     state = [] if first else list(running)
     acc = jax.ShapeDtypeStruct((heads, 3 * HD, rows), jnp.float32)
-    stat = jax.ShapeDtypeStruct((heads, 8, rows), jnp.float32)
+    stat = jax.ShapeDtypeStruct((steps, 8, rows), jnp.float32)
     big = jax.ShapeDtypeStruct((heads, keys, rows), jnp.bfloat16)
     acc_spec = per_head_spec(3 * HD, rows)
-    stat_spec = per_head_spec(8, rows)
+    stat_spec = stat_rows(rows)
     big_spec = per_head_spec(keys, rows)
     return pl.pallas_call(
-        lambda *refs: pair_kernel(first, *refs),
+        lambda *refs: pair_kernel(first, moves, *refs),
         grid=(steps,),
         in_specs=[
+            pl.BlockSpec(memory_space=pltpu.SMEM),
             pl.BlockSpec(memory_space=pltpu.SMEM),
             column_spec(rows, 0),
             column_spec(rows, steps),
@@ -262,15 +335,16 @@
             transcendentals=heads * rows * keys,
             bytes_accessed=4 * heads * rows * keys,
         ),
-    )(bias, query_grad, query_grad, key_value, key_value, *state)
+    )(*tables, query_grad, query_grad, key_value, key_value, *state)
 
 
 def joined(mine, other, side):
-    top = jnp.maximum(mine[side, 0:1], other[side, 0:1])
-    here = jnp.exp2(mine[side, 0:1] - top)
-    there = jnp.exp2(other[side, 0:1] - top)
-    inverse = 1.0 / (mine[side, 1:2] * here + other[side, 1:2] * there)
-    mean = (mine[side, 2:3] * here + other[side, 2:3] * there) * inverse
+    at = 3 * side
+    top = jnp.maximum(mine[0, at : at + 1], other[0, at : at + 1])
+    here = jnp.exp2(mine[0, at : at + 1] - top)
+    there = jnp.exp2(other[0, at : at + 1] - top)
+    inverse = 1.0 / (mine[0, at + 1 : at + 2] * here + other[0, at + 1 : at + 2] * there)
+    mean = (mine[0, at + 2 : at + 3] * here + other[0, at + 2 : at + 3] * there) * inverse
     return top, inverse, mean
 
 
@@ -286,8 +360,8 @@
         for side in range(2):
             rows = slice(side * HD, (side + 1) * HD)
             top, inverse, mean = joined(mine, other, side)
-            factor = jnp.exp2(pair_ref[side, 0:1] - top) * inverse
-            shift = pair_ref[side, 1:2] - mean
+            factor = jnp.exp2(pair_ref[0, 3 * side : 3 * side + 1] - top) * inverse
+            shift = pair_ref[0, 3 * side + 1 : 3 * side + 2] - mean
             scaled_q = q_t[rows] * (factor * scale)
             for_e = jnp.concatenate(
                 [
@@ -318,9 +392,9 @@
             per_head_spec(keys, rows),
             column_spec(rows, 0),
             column_spec(rows, steps),
-            per_head_spec(8, rows),
-            per_head_spec(8, rows),
-            per_head_spec(8, rows),
+            stat_rows(rows),
+            stat_rows(rows),
+            stat_rows(rows),
         ]
     return pl.pallas_call(
         key_kernel,
@@ -348,7 +422,7 @@
     grads = []
     for side in range(2):
         top, inverse, mean = joined(mine, other, side)
-        factor = jnp.exp2(mine[side, 0:1] - top) * inverse
+        factor = jnp.exp2(mine[0, 3 * side : 3 * side + 1] - top) * inverse
         outs.append(acc[side, :HD] * factor)
         grads.append((acc[side, 2 * HD :] - acc[side, HD : 2 * HD] * mean) * (factor * scale))
     out_rows = jnp.concatenate(outs, axis=0).T
@@ -368,7 +442,7 @@
     return pl.pallas_call(
         lambda *refs: query_kernel(final, *refs),
         grid=(steps,),
-        in_specs=[per_head_spec(3 * HD, rows), per_head_spec(8, rows), per_head_spec(8, rows)]
+        in_specs=[per_head_spec(3 * HD, rows), stat_rows(rows), stat_rows(rows)]
         + [column_spec(rows, 0)] * len(extra),
         out_specs=[column_spec(rows, 0), column_spec(rows, 0)],
         out_shape=[jax.ShapeDtypeStruct((rows, heads * HD), jnp.bfloat16)] * 2,
@@ -385,40 +459,81 @@
     return lax.ppermute(x, "seq", [(i, i ^ offset) for i in range(devices)])
 
 
-def repeats(partners, global_blocks, query_block, key_block, devices):
-    listed = [query_block, (query_block - 1) % devices, (query_block + 1) % devices]
-    listed += [lax.dynamic_index_in_dim(partners[r], query_block, 0, False) for r in range(3)]
-    listed += [global_blocks[0], global_blocks[1]]
-    count = sum((entry == key_block).astype(jnp.float32) for entry in listed)
-    return jnp.where(count > 0.0, jnp.log2(jnp.maximum(count, 1.0)), -1e30).reshape(1)
+def pack_kernel(k_ref, v_ref, q_ref, do_ref, kv_ref, qd_ref):
+    features = k_ref.shape[1]
+    qd_ref[:, :features] = q_ref[...]
+    qd_ref[:, features:] = do_ref[...]
+    kv_ref[:, :features] = k_ref[...]
+    kv_ref[:, features:] = v_ref[...]
+
+
+def packed(key_states, value_states, queries, grad_output):
+    rows, features = queries.shape
+    both = jax.ShapeDtypeStruct((rows, 2 * features), queries.dtype)
+    whole = pl.BlockSpec(memory_space=pltpu.VMEM)
+    return pl.pallas_call(
+        pack_kernel,
+        in_specs=[whole] * 4,
+        out_specs=[whole] * 2,
+        out_shape=[both, both],
+        name="pack",
+    )(key_states, value_states, queries, grad_output)
+
+
+def after(x, earlier):
+    return lax.optimization_barrier((x, earlier))[0]
 
 
 def dense_local(queries, key_states, value_states, grad_output, partners, global_blocks):
     devices = lax.axis_size("seq")
     far = devices // 2
-    me = lax.axis_index("seq")
-    key_value = jnp.concatenate([key_states, value_states], axis=1)
-    query_grad = jnp.concatenate([queries, grad_output], axis=1)
+    tables = (partners, global_blocks)
+    key_value, query_grad = packed(key_states, value_states, queries, grad_output)
+    query_blocks = [query_grad, swapped(query_grad, far)]
     offsets = list(range(far))
-    key_blocks = [key_value] + [swapped(key_value, o) for o in offsets[1:]]
-    query_blocks = [query_grad, swapped(query_grad, far)]
+    key_blocks = {0: key_value}
     running = [None, None]
     saved = {}
-    for at in [(0, k) for k in offsets] + [(1, k) for k in offsets]:
-        q, k = at
-        bias = repeats(partners, global_blocks, me ^ (q * far), me ^ offsets[k], devices)
-        e, u, acc, run, pair = pair_terms(bias, query_blocks[q], key_blocks[k], running[q])
+    order = [None]
+
+    def pair(q, k):
+        query_block = query_blocks[q]
+        if order[0] is not None:
+            query_block = after(query_block, order[0])
+        e, u, acc, run, stat = pair_terms(
+            tables, (q * far, k), query_block, key_blocks[k], running[q]
+        )
         running[q] = (acc, run)
-        saved[at] = (e, u, query_blocks[q], pair)
-    theirs = swapped(jnp.stack([running[1][1], running[0][1]]), far)
-    others = [theirs[0], theirs[1]]
+        saved[(q, k)] = (e, u, query_blocks[q], stat)
+        order[0] = stat
+
+    neighbours = [o for o in offsets if o and o & (o - 1) == 0]
+    for o in neighbours:
+        key_blocks[o] = swapped(key_value, o)
+    pair(0, 0)
+    relayed = [o for o in offsets if o and o not in neighbours]
+    for o in neighbours[:-1]:
+        pair(0, o)
+    for o in relayed:
+        last = o & -o
+        key_blocks[o] = swapped(after(key_blocks[o - last], order[0]), last)
+    pair(0, neighbours[-1])
+    for o in [0] + neighbours:
+        pair(1, o)
+    for o in relayed:
+        pair(1, o)
+    others = {0: swapped(running[1][1], far)}
+    for o in relayed:
+        pair(0, o)
+    others[1] = swapped(running[0][1], far)
     sent = query_terms(running[1][0], running[1][1], others[1], None)
     came = [swapped(x, far) for x in sent]
     key_parts = []
     for k in reversed(offsets):
         entries = [saved[(q, k)] + (running[q][1], others[q]) for q in range(2)]
         parts = key_terms(entries, jnp.float32 if k == 0 else jnp.bfloat16)
-        key_parts.append(parts if k == 0 else [swapped(x, offsets[k]) for x in parts])
+        key_parts.append(parts if k == 0 else [swapped(x, k) for x in parts])
+    came = [after(x, key_parts[-1][0]) for x in came]
     attended, grad_queries = query_terms(running[0][0], running[0][1], others[0], came)
     grads = [
         sum(parts[i].astype(jnp.float32) for parts in key_parts).astype(jnp.bfloat16)

time: 199 us -> 169 us (0.85)
  between operations: 22.3 us -> 0.78 us
  waiting for transfers between devices: 36.3 us -> 30.3 us
  local copies, waits for them, and re-layouts: 8.51 us -> 3.82 us
  starting transfers between devices: 16 us -> 20.2 us
  Pallas kernels: 112 us -> 110 us
    ppermute x13 -> x14, waiting for transfers between devices: 36.3 us -> 30.3 us  [swapped(): return lax.ppermute(x, 'seq', [(i, i ^ offset) for i in range(devices)])]
    ppermute x13 -> x14, starting transfers between devices: 16 us -> 20.2 us  [swapped(): return lax.ppermute(x, 'seq', [(i, i ^ offset) for i in range(devices)])]
    concatenate x2 -> x0, local copies, waits for them, and re-layouts: 2.12 us -> none  [the longest x1 1.06 us: dense_local(): key_value = jnp.concatenate([key_states, value_states], axis=1)]
    pallas_call x8 -> x9, Pallas kernels: 70.8 us -> 69.4 us  [the longest x8 66.9 us: pair_terms(): pl.pallas_call(lambda *refs: pair_kernel(first, moves, *refs), grid=(step...]
  transfers between devices with their start and end apart: 13 -> 14, of which waited for: 5 -> 8; matrix products, arithmetic and copies ran while one was open for 2% -> 1% of each run, Pallas kernels for 41% -> 49%
where the time goes in v2:
time: 169 us; the launch traced here: 168 us
  Pallas kernels  110 us (65%)
  waiting for transfers between devices  30.3 us (18%)
  starting transfers between devices  20.2 us (12%)
  local copies, waits for them, and re-layouts  3.82 us (2%)
  other arithmetic  2.95 us (2%)
    pallas_call x8, Pallas kernels, pair_terms(): pl.pallas_call(lambda *refs: pair_kernel(first, moves, *refs), grid=(step...  66.9 us
    pallas_call x4, Pallas kernels, key_terms(): pl.pallas_call(key_kernel, grid=(steps,), in_specs=in_specs, out_specs=[c...  33.4 us
    ppermute x14, waiting for transfers between devices, swapped(): return lax.ppermute(x, 'seq', [(i, i ^ offset) for i in range(devices)])  30.3 us
    ppermute x14, starting transfers between devices, swapped(): return lax.ppermute(x, 'seq', [(i, i ^ offset) for i in range(devices)])  20.2 us
    pallas_call x2, Pallas kernels, query_terms(): pl.pallas_call(lambda *refs: query_kernel(final, *refs), grid=(steps,), i...  7.35 us
    unnamed x22, local copies, waits for them, and re-layouts  3.82 us
  transfers between devices with their start and end apart: 14, of which 8 were waited for; matrix products, arithmetic and copies ran while one was open for 1% of the time, Pallas kernels for 49%

profile of v2, /device:TPU:0, one launch (start us, length us, event | category | flops | bytes accessed | tf_op | source)
XLA Modules:
  0.0 168.2 jit_solution(563216398616020444)
XLA Ops:
  0.6 2.6 %pack.1 = (bf16[512,768]{1,0:T(8,128)(2,1)}, bf16[512,768]{1,0:T(8,128)(2,1)}) custom-call(bf16[512,384]{1,0:T(8,128)(2,1)} %k_ref.1, bf16[512,384]{1,0:T(8,128)(2,1)} %v_ref.1, bf16[512,384]{1,0:T(8,128)(2,1)} %q_ref.1, bf16[512,384]{1,0:T(8,128)(2,1)} %do_ref.1), custom_call_target="tpu_custom_call" | custom-call | tf_op jit(solution)/shard_map/pack/pallas_call | solution.py:474
  3.2 3.0 %collective-permute-start.1 = (bf16[512,768]{1,0:T(8,128)(2,1)}, bf16[512,768]{1,0:T(8,128)(2,1)S(1)}, u32[]{:S(2)}, u32[]{:S(2)}) collective-permute-start(bf16[512,768]{1,0:T(8,128)(2,1)} %get-tuple-element.69.refs_4_.refs_5_), channel_id=1, source_target_pairs={{0,4},{4,0},{8,12},{12,8},{16,20},{20,16},{24,28},{28,24},{1,5},{5... | collective-permute-start | bytes 2359304 | tf_op jit(solution)/shard_map/ppermute | solution.py:459
  6.2 1.6 collective-permute-start.2
  7.8 2.6 %collective-permute-start = (bf16[512,768]{1,0:T(8,128)(2,1)}, bf16[512,768]{1,0:T(8,128)(2,1)S(1)}, u32[]{:S(2)}, u32[]{:S(2)}) collective-permute-start(bf16[512,768]{1,0:T(8,128)(2,1)} %get-tuple-element.94.refs_2_.refs_3_), channel_id=1, source_target_pairs={{0,16},{4,20},{8,24},{12,28},{16,0},{20,4},{24,8},{28,12},{1,17},{... | collective-permute-start | bytes 2359304 | tf_op jit(solution)/shard_map/ppermute | solution.py:459
  10.4 8.2 %pair_first.2 = (bf16[6,512,512]{2,1,0:T(8,128)(2,1)}, bf16[6,512,512]{2,1,0:T(8,128)(2,1)}, f32[6,192,512]{2,1,0:T(8,128)}, f32[3,8,512]{2,1,0:T(8,128)}, f32[3,8,512]{2,1,0:T(8,128)}) custom-call(s32[3,8]{1,0:T(4,128)} %refs_0_.15, s32[2]{0:T(128)} %refs_1_.15, bf16[512,768]{1,0:T(8,128)(2,1)} %get-tuple-element.94.refs_2_.refs_3_, ...), custom_call_target="tpu_custom_call" | custom-call | flops 805306368 | bytes 6291456 | tf_op jit(solution)/shard_map/pair_first/pallas_call | solution.py:317
  18.6 5.4 %collective-permute-done.1.refs_4_.refs_5_ = bf16[512,768]{1,0:T(8,128)(2,1)S(1)} collective-permute-done((bf16[512,768]{1,0:T(8,128)(2,1)}, bf16[512,768]{1,0:T(8,128)(2,1)S(1)}, u32[]{:S(2)}, u32[]{:S(2)}) %collective-permute-start.1) | collective-permute-done | bytes 786464 | tf_op jit(solution)/shard_map/ppermute | solution.py:459
  24.8 8.4 %pair_next.6 = (bf16[6,512,512]{2,1,0:T(8,128)(2,1)}, bf16[6,512,512]{2,1,0:T(8,128)(2,1)}, f32[6,192,512]{2,1,0:T(8,128)}, f32[3,8,512]{2,1,0:T(8,128)}, f32[3,8,512]{2,1,0:T(8,128)}) custom-call(s32[3,8]{1,0:T(4,128)} %refs_0_.15, s32[2]{0:T(128)} %refs_1_.15, bf16[512,768]{1,0:T(8,128)(2,1)} %get-tuple-element.94.refs_2_.refs_3_, ...), custom_call_target="tpu_custom_call" | custom-call | flops 805306368 | bytes 6291456 | tf_op jit(solution)/shard_map/pair_next/pallas_call | solution.py:317
  33.2 8.9 %collective-permute-done.2.refs_4_.refs_5_ = bf16[512,768]{1,0:T(8,128)(2,1)S(1)} collective-permute-done((bf16[512,768]{1,0:T(8,128)(2,1)}, bf16[512,768]{1,0:T(8,128)(2,1)S(1)}, u32[]{:S(2)}, u32[]{:S(2)}) %collective-permute-start.2) | collective-permute-done | bytes 786464 | tf_op jit(solution)/shard_map/ppermute | solution.py:459
  43.1 8.4 %pair_next.7 = (bf16[6,512,512]{2,1,0:T(8,128)(2,1)}, bf16[6,512,512]{2,1,0:T(8,128)(2,1)}, f32[6,192,512]{2,1,0:T(8,128)}, f32[3,8,512]{2,1,0:T(8,128)}, f32[3,8,512]{2,1,0:T(8,128)}) custom-call(s32[3,8]{1,0:T(4,128)} %refs_0_.15, s32[2]{0:T(128)} %refs_1_.15, bf16[512,768]{1,0:T(8,128)(2,1)} %get-tuple-element.94.refs_2_.refs_3_, ...), custom_call_target="tpu_custom_call" | custom-call | flops 805306368 | bytes 6291456 | tf_op jit(solution)/shard_map/pair_next/pallas_call | solution.py:317
  51.5 0.9 copy-done
  52.3 8.2 %pair_first.3 = (bf16[6,512,512]{2,1,0:T(8,128)(2,1)}, bf16[6,512,512]{2,1,0:T(8,128)(2,1)}, f32[6,192,512]{2,1,0:T(8,128)}, f32[3,8,512]{2,1,0:T(8,128)}, f32[3,8,512]{2,1,0:T(8,128)}) custom-call(s32[3,8]{1,0:T(4,128)} %refs_0_.15, s32[2]{0:T(128)} %refs_1_.15, bf16[512,768]{1,0:T(8,128)(2,1)} %copy-done, bf16[512,768]{1,0:T(8,128)(2,1)} %copy-done, ...), custom_call_target="tpu_custom_call" | custom-call | flops 805306368 | bytes 6291456 | tf_op jit(solution)/shard_map/pair_first/pallas_call | solution.py:317
  60.5 8.4 %pair_next.8 = (bf16[6,512,512]{2,1,0:T(8,128)(2,1)}, bf16[6,512,512]{2,1,0:T(8,128)(2,1)}, f32[6,192,512]{2,1,0:T(8,128)}, f32[3,8,512]{2,1,0:T(8,128)}, f32[3,8,512]{2,1,0:T(8,128)}) custom-call(s32[3,8]{1,0:T(4,128)} %refs_0_.15, s32[2]{0:T(128)} %refs_1_.15, bf16[512,768]{1,0:T(8,128)(2,1)} %copy-done, bf16[512,768]{1,0:T(8,128)(2,1)} %copy-done, ...), custom_call_target="tpu_custom_call" | custom-call | flops 805306368 | bytes 6291456 | tf_op jit(solution)/shard_map/pair_next/pallas_call | solution.py:317
  68.9 8.4 %pair_next.9 = (bf16[6,512,512]{2,1,0:T(8,128)(2,1)}, bf16[6,512,512]{2,1,0:T(8,128)(2,1)}, f32[6,192,512]{2,1,0:T(8,128)}, f32[3,8,512]{2,1,0:T(8,128)}, f32[3,8,512]{2,1,0:T(8,128)}) custom-call(s32[3,8]{1,0:T(4,128)} %refs_0_.15, s32[2]{0:T(128)} %refs_1_.15, bf16[512,768]{1,0:T(8,128)(2,1)} %copy-done, bf16[512,768]{1,0:T(8,128)(2,1)} %copy-done, ...), custom_call_target="tpu_custom_call" | custom-call | flops 805306368 | bytes 6291456 | tf_op jit(solution)/shard_map/pair_next/pallas_call | solution.py:317
  77.4 0.9 copy-done.3
  78.2 8.4 %pair_next.10 = (bf16[6,512,512]{2,1,0:T(8,128)(2,1)}, bf16[6,512,512]{2,1,0:T(8,128)(2,1)}, f32[6,192,512]{2,1,0:T(8,128)}, f32[3,8,512]{2,1,0:T(8,128)}, f32[3,8,512]{2,1,0:T(8,128)}) custom-call(s32[3,8]{1,0:T(4,128)} %refs_0_.15, s32[2]{0:T(128)} %refs_1_.15, bf16[512,768]{1,0:T(8,128)(2,1)} %copy-done, bf16[512,768]{1,0:T(8,128)(2,1)} %copy-done, ...), custom_call_target="tpu_custom_call" | custom-call | flops 805306368 | bytes 6291456 | tf_op jit(solution)/shard_map/pair_next/pallas_call | solution.py:317
  86.6 8.6 %pair_next.11 = (bf16[6,512,512]{2,1,0:T(8,128)(2,1)}, bf16[6,512,512]{2,1,0:T(8,128)(2,1)}, f32[6,192,512]{2,1,0:T(8,128)}, f32[3,8,512]{2,1,0:T(8,128)}, f32[3,8,512]{2,1,0:T(8,128)}) custom-call(s32[3,8]{1,0:T(4,128)} %refs_0_.15, s32[2]{0:T(128)} %refs_1_.15, bf16[512,768]{1,0:T(8,128)(2,1)} %get-tuple-element.94.refs_2_.refs_3_, ...), custom_call_target="tpu_custom_call" | custom-call | flops 805306368 | bytes 6291456 | tf_op jit(solution)/shard_map/pair_next/pallas_call | solution.py:317
  95.9 2.3 %collective-permute-start.4 = (f32[3,8,512]{2,1,0:T(8,128)S(1)}, f32[3,8,512]{2,1,0:T(8,128)S(1)}, u32[]{:S(2)}, u32[]{:S(2)}) collective-permute-start(f32[3,8,512]{2,1,0:T(8,128)S(1)} %copy-done.4), channel_id=1, source_target_pairs={{0,16},{4,20},{8,24},{12,28},{16,0},{20,4},{24,8},{28,12},{1,17},{... | collective-permute-start | bytes 147464 | tf_op jit(solution)/shard_map/ppermute | solution.py:459
  98.2 2.9 %collective-permute-done.5.refs_2_.refs_13_ = f32[3,8,512]{2,1,0:T(8,128)S(1)} collective-permute-done((f32[3,8,512]{2,1,0:T(8,128)}, f32[3,8,512]{2,1,0:T(8,128)S(1)}, u32[]{:S(2)}, u32[]{:S(2)}) %collective-permute-start.5) | collective-permute-done | bytes 49184 | tf_op jit(solution)/shard_map/ppermute | solution.py:459
  102.2 8.2 %key_terms.5 = (bf16[512,384]{1,0:T(8,128)(2,1)}, bf16[512,384]{1,0:T(8,128)(2,1)}) custom-call(bf16[6,512,512]{2,1,0:T(8,128)(2,1)} %get-tuple-element.112.refs_0_, bf16[6,512,512]{2,1,0:T(8,128)(2,1)} %get-tuple-element.113.refs_1_, bf16[512,768]{1,0:T(8,128)(2,1)} %get-tuple-element.94.refs_2_.refs_3_, ...), custom_call_target="tpu_custom_call" | custom-call | flops 1207959552 | bytes 12582912 | tf_op jit(solution)/shard_map/key_terms/pallas_call | solution.py:399
  110.4 2.3 %collective-permute-start.8 = (bf16[512,384]{1,0:T(8,128)(2,1)}, bf16[512,384]{1,0:T(8,128)(2,1)S(1)}, u32[]{:S(2)}, u32[]{:S(2)}) collective-permute-start(bf16[512,384]{1,0:T(8,128)(2,1)} %get-tuple-element.117), channel_id=1, source_target_pairs={{0,12},{4,8},{8,4},{12,0},{16,28},{20,24},{24,20},{28,16},{1,13},{... | collective-permute-start | bytes 1179656 | tf_op jit(solution)/shard_map/ppermute | solution.py:459
  112.7 3.5 %query_send.1 = (bf16[512,384]{1,0:T(8,128)(2,1)}, bf16[512,384]{1,0:T(8,128)(2,1)}) custom-call(f32[6,192,512]{2,1,0:T(8,128)} %get-tuple-element.100.refs_0_, f32[3,8,512]{2,1,0:T(8,128)} %get-tuple-element.99.refs_1_.refs_12_, f32[3,8,512]{2,1,0:T(8,128)} %copy-done.6), custom_call_target="tpu_custom_call" | custom-call | flops 1572864 | bytes 3145728 | tf_op jit(solution)/shard_map/query_send/pallas_call | solution.py:442
  117.0 2.2 %collective-permute-start.6 = (bf16[512,384]{1,0:T(8,128)(2,1)}, bf16[512,384]{1,0:T(8,128)(2,1)S(1)}, u32[]{:S(2)}, u32[]{:S(2)}) collective-permute-start(bf16[512,384]{1,0:T(8,128)(2,1)} %get-tuple-element.101), channel_id=1, source_target_pairs={{0,16},{4,20},{8,24},{12,28},{16,0},{20,4},{24,8},{28,12},{1,17},{... | collective-permute-start | bytes 1179656 | tf_op jit(solution)/shard_map/ppermute | solution.py:459
  119.2 8.3 %key_terms.6 = (bf16[512,384]{1,0:T(8,128)(2,1)}, bf16[512,384]{1,0:T(8,128)(2,1)}) custom-call(bf16[6,512,512]{2,1,0:T(8,128)(2,1)} %get-tuple-element.118.refs_0_, bf16[6,512,512]{2,1,0:T(8,128)(2,1)} %get-tuple-element.119.refs_1_, bf16[512,768]{1,0:T(8,128)(2,1)} %get-tuple-element.94.refs_2_.refs_3_, ...), custom_call_target="tpu_custom_call" | custom-call | flops 1207959552 | bytes 12582912 | tf_op jit(solution)/shard_map/key_terms/pallas_call | solution.py:399
  127.9 8.2 %key_terms.7 = (bf16[512,384]{1,0:T(8,128)(2,1)}, bf16[512,384]{1,0:T(8,128)(2,1)}) custom-call(bf16[6,512,512]{2,1,0:T(8,128)(2,1)} %get-tuple-element.123.refs_0_, bf16[6,512,512]{2,1,0:T(8,128)(2,1)} %get-tuple-element.124.refs_1_, bf16[512,768]{1,0:T(8,128)(2,1)} %get-tuple-element.94.refs_2_.refs_3_, ...), custom_call_target="tpu_custom_call" | custom-call | flops 1207959552 | bytes 12582912 | tf_op jit(solution)/shard_map/key_terms/pallas_call | solution.py:399
  136.1 1.0 collective-permute-start.10
  137.1 2.2 %collective-permute-start.11 = (bf16[512,384]{1,0:T(8,128)(2,1)}, bf16[512,384]{1,0:T(8,128)(2,1)S(1)}, u32[]{:S(2)}, u32[]{:S(2)}) collective-permute-start(bf16[512,384]{1,0:T(8,128)(2,1)} %get-tuple-element.128), channel_id=1, source_target_pairs={{0,12},{4,8},{8,4},{12,0},{16,28},{20,24},{24,20},{28,16},{1,13},{... | collective-permute-start | bytes 1179656 | tf_op jit(solution)/shard_map/ppermute | solution.py:459
  139.4 5.4 %collective-permute-done.7.refs_4_ = bf16[512,384]{1,0:T(8,128)(2,1)S(1)} collective-permute-done((bf16[512,384]{1,0:T(8,128)(2,1)}, bf16[512,384]{1,0:T(8,128)(2,1)S(1)}, u32[]{:S(2)}, u32[]{:S(2)}) %collective-permute-start.7) | collective-permute-done | bytes 393248 | tf_op jit(solution)/shard_map/ppermute | solution.py:459
  144.8 6.5 %collective-permute-done.6.refs_3_ = bf16[512,384]{1,0:T(8,128)(2,1)S(1)} collective-permute-done((bf16[512,384]{1,0:T(8,128)(2,1)}, bf16[512,384]{1,0:T(8,128)(2,1)S(1)}, u32[]{:S(2)}, u32[]{:S(2)}) %collective-permute-start.6) | collective-permute-done | bytes 393248 | tf_op jit(solution)/shard_map/ppermute | solution.py:459
  152.1 8.6 %key_terms.4 = (f32[512,384]{1,0:T(8,128)}, f32[512,384]{1,0:T(8,128)}) custom-call(bf16[6,512,512]{2,1,0:T(8,128)(2,1)} %get-tuple-element.102.refs_0_, bf16[6,512,512]{2,1,0:T(8,128)(2,1)} %get-tuple-element.103.refs_1_, bf16[512,768]{1,0:T(8,128)(2,1)} %get-tuple-element.94.refs_2_.refs_3_, bf16[512,768]{1,0:T(8,128)(2,1)} %get-tuple-element.94.refs_2_.refs_3_, ...), custom_call_target="tpu_custom_call" | custom-call | flops 1207959552 | bytes 12582912 | tf_op jit(solution)/shard_map/key_terms/pallas_call | solution.py:399
  160.7 3.9 %query_final.1 = (bf16[512,384]{1,0:T(8,128)(2,1)}, bf16[512,384]{1,0:T(8,128)(2,1)}) custom-call(f32[6,192,512]{2,1,0:T(8,128)} %get-tuple-element.97.refs_0_, f32[3,8,512]{2,1,0:T(8,128)} %get-tuple-element.98.refs_5_.refs_1_, f32[3,8,512]{2,1,0:T(8,128)} %copy-done.5, bf16[512,384]{1,0:T(8,128)(2,1)} %copy-done.10, bf16[512,384]{1,0:T(8,128)(2,1)} %copy-done.9), custom_call_target="tpu_custom_call" | custom-call | flops 1572864 | bytes 3145728 | tf_op jit(solution)/shard_map/query_final/pallas_call | solution.py:442
  164.6 0.9 add_convert_fusion.1
  166.2 2.0 %add_convert_fusion = bf16[512,384]{1,0:T(8,128)(2,1)} fusion(f32[512,384]{1,0:T(8,128)S(1)} %copy-done.7, bf16[512,384]{1,0:T(8,128)(2,1)} %collective-permute-done.13, bf16[512,384]{1,0:T(8,128)(2,1)} %collective-permute-done.12, bf16[512,384]{1,0:T(8,128)(2,1)S(1)} %collective-permute-done.11), kind=kLoop, calls=%fused_computation | loop fusion | flops 1376256 | bytes 2359296 | tf_op jit(solution)/shard_map/convert_element_type | solution.py:539
  (35 shorter events, 6.3 us)
Async XLA Ops:
  3.2 20.7 %collective-permute-start.1 = (bf16[512,768]{1,0:T(8,128)(2,1)}, bf16[512,768]{1,0:T(8,128)(2,1)S(1)}, u32[]{:S(2)}, u32[]{:S(2)}) collective-permute-start(bf16[512,768]{1,0:T(8,128)(2,1)} %get-tuple-element.69.refs_4_.refs_5_), channel_id=1, source_target_pairs={{0,4},{4,0},{8,12},{12,8},{16,20},{20,16},{24,28},{28,24},{1,5},{5... | collective-permute-start | bytes 2359304 | tf_op jit(solution)/shard_map/ppermute | solution.py:459
  6.2 35.9 %collective-permute-start.2 = (bf16[512,768]{1,0:T(8,128)(2,1)}, bf16[512,768]{1,0:T(8,128)(2,1)S(1)}, u32[]{:S(2)}, u32[]{:S(2)}) collective-permute-start(bf16[512,768]{1,0:T(8,128)(2,1)} %get-tuple-element.69.refs_4_.refs_5_), channel_id=1, source_target_pairs={{0,8},{4,12},{8,0},{12,4},{16,24},{20,28},{24,16},{28,20},{1,9},{5... | collective-permute-start | bytes 2359304 | tf_op jit(solution)/shard_map/ppermute | solution.py:459
  7.8 43.7 %collective-permute-start = (bf16[512,768]{1,0:T(8,128)(2,1)}, bf16[512,768]{1,0:T(8,128)(2,1)S(1)}, u32[]{:S(2)}, u32[]{:S(2)}) collective-permute-start(bf16[512,768]{1,0:T(8,128)(2,1)} %get-tuple-element.94.refs_2_.refs_3_), channel_id=1, source_target_pairs={{0,16},{4,20},{8,24},{12,28},{16,0},{20,4},{24,8},{28,12},{1,17},{... | collective-permute-start | bytes 2359304 | tf_op jit(solution)/shard_map/ppermute | solution.py:459
  24.0 0.9 copy-start.2
  42.2 0.9 copy-start.1
  42.2 35.2 %collective-permute-start.3 = (bf16[512,768]{1,0:T(8,128)(2,1)S(1)}, bf16[512,768]{1,0:T(8,128)(2,1)S(1)}, u32[]{:S(2)}, u32[]{:S(2)}) collective-permute-start(bf16[512,768]{1,0:T(8,128)(2,1)S(1)} %collective-permute-done.2.refs_4_.refs_5_), channel_id=1, source_target_pairs={{0,4},{4,0},{8,12},{12,8},{16,20},{20,16},{24,28},{28,24},{1,5},{5... | collective-permute-start | bytes 2359304 | tf_op jit(solution)/shard_map/ppermute | solution.py:459
  51.5 0.9 copy-start
  77.4 0.9 copy-start.3
  86.6 9.3 %copy-start.4 = (f32[3,8,512]{2,1,0:T(8,128)S(1)}, f32[3,8,512]{2,1,0:T(8,128)}, u32[]{:S(2)}) copy-start(f32[3,8,512]{2,1,0:T(8,128)} %get-tuple-element.99.refs_1_.refs_12_) | copy-start | bytes 147460
  95.2 5.9 %collective-permute-start.5 = (f32[3,8,512]{2,1,0:T(8,128)}, f32[3,8,512]{2,1,0:T(8,128)S(1)}, u32[]{:S(2)}, u32[]{:S(2)}) collective-permute-start(f32[3,8,512]{2,1,0:T(8,128)} %get-tuple-element.98.refs_5_.refs_1_), channel_id=1, source_target_pairs={{0,16},{4,20},{8,24},{12,28},{16,0},{20,4},{24,8},{28,12},{1,17},{... | collective-permute-start | bytes 147464 | tf_op jit(solution)/shard_map/ppermute | solution.py:459
  95.9 5.7 %collective-permute-start.4 = (f32[3,8,512]{2,1,0:T(8,128)S(1)}, f32[3,8,512]{2,1,0:T(8,128)S(1)}, u32[]{:S(2)}, u32[]{:S(2)}) collective-permute-start(f32[3,8,512]{2,1,0:T(8,128)S(1)} %copy-done.4), channel_id=1, source_target_pairs={{0,16},{4,20},{8,24},{12,28},{16,0},{20,4},{24,8},{28,12},{1,17},{... | collective-permute-start | bytes 147464 | tf_op jit(solution)/shard_map/ppermute | solution.py:459
  101.1 0.6 copy-start.6
  101.6 0.6 copy-start.5
  110.4 26.7 %collective-permute-start.8 = (bf16[512,384]{1,0:T(8,128)(2,1)}, bf16[512,384]{1,0:T(8,128)(2,1)S(1)}, u32[]{:S(2)}, u32[]{:S(2)}) collective-permute-start(bf16[512,384]{1,0:T(8,128)(2,1)} %get-tuple-element.117), channel_id=1, source_target_pairs={{0,12},{4,8},{8,4},{12,0},{16,28},{20,24},{24,20},{28,16},{1,13},{... | collective-permute-start | bytes 1179656 | tf_op jit(solution)/shard_map/ppermute | solution.py:459
  116.2 28.5 %collective-permute-start.7 = (bf16[512,384]{1,0:T(8,128)(2,1)}, bf16[512,384]{1,0:T(8,128)(2,1)S(1)}, u32[]{:S(2)}, u32[]{:S(2)}) collective-permute-start(bf16[512,384]{1,0:T(8,128)(2,1)} %get-tuple-element.108), channel_id=1, source_target_pairs={{0,16},{4,20},{8,24},{12,28},{16,0},{20,4},{24,8},{28,12},{1,17},{... | collective-permute-start | bytes 1179656 | tf_op jit(solution)/shard_map/ppermute | solution.py:459
  117.0 34.3 %collective-permute-start.6 = (bf16[512,384]{1,0:T(8,128)(2,1)}, bf16[512,384]{1,0:T(8,128)(2,1)S(1)}, u32[]{:S(2)}, u32[]{:S(2)}) collective-permute-start(bf16[512,384]{1,0:T(8,128)(2,1)} %get-tuple-element.101), channel_id=1, source_target_pairs={{0,16},{4,20},{8,24},{12,28},{16,0},{20,4},{24,8},{28,12},{1,17},{... | collective-permute-start | bytes 1179656 | tf_op jit(solution)/shard_map/ppermute | solution.py:459
  127.5 37.1 %collective-permute-start.9 = (bf16[512,384]{1,0:T(8,128)(2,1)}, bf16[512,384]{1,0:T(8,128)(2,1)S(1)}, u32[]{:S(2)}, u32[]{:S(2)}) collective-permute-start(bf16[512,384]{1,0:T(8,128)(2,1)} %get-tuple-element.122), channel_id=1, source_target_pairs={{0,8},{4,12},{8,0},{12,4},{16,24},{20,28},{24,16},{28,20},{1,9},{5... | collective-permute-start | bytes 1179656 | tf_op jit(solution)/shard_map/ppermute | solution.py:459
  136.1 28.4 %collective-permute-start.10 = (bf16[512,384]{1,0:T(8,128)(2,1)}, bf16[512,384]{1,0:T(8,128)(2,1)S(1)}, u32[]{:S(2)}, u32[]{:S(2)}) collective-permute-start(bf16[512,384]{1,0:T(8,128)(2,1)} %get-tuple-element.127), channel_id=1, source_target_pairs={{0,4},{4,0},{8,12},{12,8},{16,20},{20,16},{24,28},{28,24},{1,5},{5... | collective-permute-start | bytes 1179656 | tf_op jit(solution)/shard_map/ppermute | solution.py:459
  137.1 28.4 %collective-permute-start.11 = (bf16[512,384]{1,0:T(8,128)(2,1)}, bf16[512,384]{1,0:T(8,128)(2,1)S(1)}, u32[]{:S(2)}, u32[]{:S(2)}) collective-permute-start(bf16[512,384]{1,0:T(8,128)(2,1)} %get-tuple-element.128), channel_id=1, source_target_pairs={{0,12},{4,8},{8,4},{12,0},{16,28},{20,24},{24,20},{28,16},{1,13},{... | collective-permute-start | bytes 1179656 | tf_op jit(solution)/shard_map/ppermute | solution.py:459
  144.8 15.9 %copy-start.9 = (bf16[512,384]{1,0:T(8,128)(2,1)}, bf16[512,384]{1,0:T(8,128)(2,1)S(1)}, u32[]{:S(2)}) copy-start(bf16[512,384]{1,0:T(8,128)(2,1)S(1)} %collective-permute-done.7.refs_4_) | copy-start | bytes 1179652
  144.8 21.2 %collective-permute-start.12 = (bf16[512,384]{1,0:T(8,128)(2,1)}, bf16[512,384]{1,0:T(8,128)(2,1)}, u32[]{:S(2)}, u32[]{:S(2)}) collective-permute-start(bf16[512,384]{1,0:T(8,128)(2,1)} %get-tuple-element.129), channel_id=1, source_target_pairs={{0,8},{4,12},{8,0},{12,4},{16,24},{20,28},{24,16},{28,20},{1,9},{5... | collective-permute-start | bytes 1179656 | tf_op jit(solution)/shard_map/ppermute | solution.py:459
  151.3 9.4 %copy-start.10 = (bf16[512,384]{1,0:T(8,128)(2,1)}, bf16[512,384]{1,0:T(8,128)(2,1)S(1)}, u32[]{:S(2)}) copy-start(bf16[512,384]{1,0:T(8,128)(2,1)S(1)} %collective-permute-done.6.refs_3_) | copy-start | bytes 1179652
  151.3 14.9 %collective-permute-start.13 = (bf16[512,384]{1,0:T(8,128)(2,1)}, bf16[512,384]{1,0:T(8,128)(2,1)}, u32[]{:S(2)}, u32[]{:S(2)}) collective-permute-start(bf16[512,384]{1,0:T(8,128)(2,1)} %get-tuple-element.130), channel_id=1, source_target_pairs={{0,4},{4,0},{8,12},{12,8},{16,20},{20,16},{24,28},{28,24},{1,5},{5... | collective-permute-start | bytes 1179656 | tf_op jit(solution)/shard_map/ppermute | solution.py:459
  160.7 3.9 %copy-start.8 = (f32[512,384]{1,0:T(8,128)S(1)}, f32[512,384]{1,0:T(8,128)}, u32[]{:S(2)}) copy-start(f32[512,384]{1,0:T(8,128)} %get-tuple-element.106) | copy-start | bytes 2359300
  160.7 5.5 %copy-start.7 = (f32[512,384]{1,0:T(8,128)S(1)}, f32[512,384]{1,0:T(8,128)}, u32[]{:S(2)}) copy-start(f32[512,384]{1,0:T(8,128)} %get-tuple-element.131) | copy-start | bytes 2359300

commit v3 on v0

--- a/solution.py
+++ b/solution.py
@@ -3,6 +3,8 @@
 import jax
 import jax.numpy as jnp
 from jax import lax
+from jax.experimental import pallas as pl
+from jax.experimental.pallas import tpu as pltpu
 from jax.sharding import PartitionSpec as P
 
 HEADS = 6
@@ -111,7 +113,7 @@
     return returned.reshape(block_rows, columns)
 
 
-def local(queries, key_states, value_states, grad_output, partners, global_blocks):
+def routed_local(queries, key_states, value_states, grad_output, partners, global_blocks):
     devices = lax.axis_size("seq")
     block_rows = queries.shape[0]
     features = queries.shape[1]
@@ -150,6 +152,574 @@
     )
 
 
+ORDER = [
+    "p0",
+    "c0",
+    "p1",
+    "e0",
+    "c1",
+    "f0",
+    "s0",
+    "p2",
+    "e1",
+    "c2",
+    "s1",
+    "p3",
+    "e2",
+    "c3",
+    "f2",
+    "s2",
+    "f1",
+    "e3",
+    "f3",
+    "s3",
+]
+LISTED = 8
+TO_LOG2 = 1.0 / (math.log(2.0) * math.sqrt(HD))
+VMEM_LIMIT = 60 * 1024 * 1024
+
+
+def matmul(a, b, contract_a, contract_b):
+    return lax.dot_general(
+        a, b, (((contract_a,), (contract_b,)), ((), ())), preferred_element_type=jnp.float32
+    )
+
+
+def placed(rows, side):
+    blank = jnp.zeros_like(rows)
+    return jnp.concatenate([rows, blank] if side == 0 else [blank, rows], axis=0)
+
+
+def listed_times(partners_ref, globals_ref, query_block, key_block, devices):
+    count = jnp.int32(0)
+    entries = [query_block, lax.rem(query_block + devices - 1, devices)]
+    entries += [lax.rem(query_block + 1, devices)]
+    entries += [partners_ref[r, query_block] for r in range(partners_ref.shape[0])]
+    entries += [globals_ref[g] for g in range(globals_ref.shape[0])]
+    for entry in entries:
+        count = count + jnp.where(entry == key_block, 1, 0)
+    return count
+
+
+def chosen(index, values):
+    result = values[0]
+    for at in range(1, len(values)):
+        result = jnp.where(index == at, values[at], result)
+    return result
+
+
+def pairs_kernel(plan, partners_ref, globals_ref, *refs):
+    pairs, query_moves, key_moves, carried = plan
+    queries, keys = len(query_moves), len(key_moves)
+    query_refs = refs[: 2 * queries]
+    key_refs = refs[2 * queries : 2 * (queries + keys)]
+    refs = refs[2 * (queries + keys) :]
+    if carried:
+        acc_in, run_in = refs[:2]
+        refs = refs[2:]
+    e_ref, u_ref, acc_ref, run_ref, pair_ref = refs[:5]
+    q_now, do_now, k_now, v_now, low_kept, both_kept, peak_kept, v_kept, kt_kept, dt_kept = refs[5:]
+    step = pl.program_id(0)
+    total_steps = pl.num_programs(0) - 1
+    per_pair = total_steps // len(pairs)
+    now = jnp.minimum(step, total_steps - 1)
+    then = jnp.maximum(step - 1, 0)
+    slot, old_slot = lax.rem(step, 2), lax.rem(step + 1, 2)
+    pair_now, pair_then = now // per_pair, then // per_pair
+    group = lax.rem(then, per_pair)
+    for at in range(queries):
+
+        @pl.when(chosen(pair_now, [q for q, _ in pairs]) == at)
+        def _():
+            q_now[...] = query_refs[2 * at][...]
+            do_now[...] = query_refs[2 * at + 1][...]
+
+    for at in range(keys):
+
+        @pl.when(chosen(pair_now, [k for _, k in pairs]) == at)
+        def _():
+            k_now[...] = key_refs[2 * at][...]
+            v_now[...] = key_refs[2 * at + 1][...]
+
+    chunk = q_now.shape[0] // 2
+    devices = lax.axis_size("seq")
+    me = lax.axis_index("seq")
+    count = listed_times(
+        partners_ref,
+        globals_ref,
+        me ^ chosen(pair_then, [query_moves[q] for q, _ in pairs]),
+        me ^ chosen(pair_then, [key_moves[k] for _, k in pairs]),
+        devices,
+    ).astype(jnp.float32)
+    bias = jnp.log2(jnp.full((1, chunk), jnp.maximum(count, 1.0), jnp.float32))
+    bias = jnp.where(count > 0.0, bias, -1e30)
+    member = chosen(pair_then, [q for q, _ in pairs])
+    first_head = 2 * group
+
+    key_rows = k_now[...]
+    values = v_now[...]
+    keys_twice = jnp.concatenate([key_rows, key_rows], axis=1)
+    q_t = q_now[...].T.astype(jnp.float32) * TO_LOG2
+    q_high = q_t.astype(jnp.bfloat16)
+    q_low = (q_t - q_high.astype(jnp.float32)).astype(jnp.bfloat16)
+    k_t = key_rows.T
+    v_t = values.T
+    v_kept[slot] = values
+    kt_kept[slot] = k_t
+    dt_kept[slot] = do_now[...].T
+    ones = jnp.ones((16, key_rows.shape[0]), jnp.bfloat16)
+    units = [(side, at) for side in range(2) for at in range(2)]
+    halves = [slice(0, HD), slice(HD, 2 * HD)]
+    lanes = [slice(at * chunk, (at + 1) * chunk) for at in range(2)]
+    scores = {}
+    lows = {}
+    centred = {}
+
+    def products(n):
+        side, at = units[n]
+        both_q = [placed(x[halves[side], lanes[at]], side) for x in (q_high, q_low)]
+        scores[n] = matmul(keys_twice, jnp.concatenate(both_q, axis=0), 1, 0)
+
+    def exponents(n):
+        side, at = units[n]
+        peak = jnp.max(scores[n], axis=0, keepdims=True)
+        low = jnp.exp2(scores.pop(n) - peak).astype(jnp.bfloat16)
+        e_ref[0, side, :, lanes[at]] = low
+        low_kept[slot, side, :, lanes[at]] = low
+        peak_kept[slot, side : side + 1, lanes[at]] = peak
+        lows[n] = low
+
+    def sums(n):
+        side, at = units[n]
+        left = jnp.concatenate([v_t[halves[side]], k_t[halves[side]], ones], axis=0)
+        both_kept[slot, side, :, lanes[at]] = matmul(left, lows.pop(n), 1, 0)
+
+    def centre(n):
+        side, at = units[n]
+        cols = lanes[at]
+        do_t = dt_kept[old_slot, halves[side], cols]
+        upper = both_kept[old_slot, side, :HD, cols]
+        total = both_kept[old_slot, side, 2 * HD : 2 * HD + 1, cols]
+        dots = jnp.sum(upper * do_t.astype(jnp.float32), axis=0, keepdims=True)
+        mean = dots / total
+        grad = matmul(v_kept[old_slot], placed(do_t, side), 1, 0)
+        shifted = low_kept[old_slot, side, :, cols] * (grad - mean).astype(jnp.bfloat16)
+        u_ref[0, side, :, cols] = shifted
+        centred[n] = (shifted, total, dots, mean)
+
+    def finish(n):
+        side, at = units[n]
+        cols = lanes[at]
+        shifted, total, dots, mean = centred.pop(n)
+        both = both_kept[old_slot, side, : 2 * HD, cols]
+        moved = matmul(kt_kept[old_slot, halves[side]], shifted, 1, 0) + mean * both[HD:]
+        peak = peak_kept[old_slot, side : side + 1, cols] + bias
+        head = first_head + side
+        row = 3 * side
+        old = run_ref[member, group, row : row + 1, cols]
+        top = jnp.maximum(old, peak)
+        keep = jnp.exp2(old - top)
+        take = jnp.exp2(peak - top)
+        acc_ref[member, head, : 2 * HD, cols] = (
+            acc_ref[member, head, : 2 * HD, cols] * keep + both * take
+        )
+        acc_ref[member, head, 2 * HD :, cols] = (
+            acc_ref[member, head, 2 * HD :, cols] * keep + moved * take
+        )
+        total = run_ref[member, group, row + 1 : row + 2, cols] * keep + total * take
+        dots = run_ref[member, group, row + 2 : row + 3, cols] * keep + dots * take
+        for at_row, value in enumerate((top, total, dots)):
+            run_ref[member, group, row + at_row : row + at_row + 1, cols] = value
+        for at_row, value in enumerate((peak, mean)):
+            pair_ref[0, row + at_row : row + at_row + 1, cols] = value
+
+    stages = dict(p=products, e=exponents, s=sums, c=centre, f=finish)
+    for name in ORDER:
+        stages[name[0]](int(name[1:]))
+
+    @pl.when(step == 0)
+    def _():
+        acc_ref[...] = jnp.zeros_like(acc_ref)
+        run_ref[...] = jnp.zeros_like(run_ref)
+        for member_at in range(acc_ref.shape[0]):
+            if member_at < carried:
+                acc_ref[member_at] = acc_in[member_at]
+                run_ref[member_at] = run_in[member_at]
+            else:
+                for row in (0, 3):
+                    shape = (run_ref.shape[1], 1, run_ref.shape[3])
+                    run_ref[member_at, :, row : row + 1] = jnp.full(shape, -1e30, jnp.float32)
+
+
+def head_pairs(features):
+    return features // (2 * HD)
+
+
+def column_spec(rows, offset):
+    return pl.BlockSpec((rows, 2 * HD), lambda p: (0, p + offset))
+
+
+def step_spec(offset, steps, used, last, *block):
+    def index(p):
+        now = jnp.minimum(p, last)
+        live = sum(jnp.where(now // steps == at, 1, 0) for at in used)
+        return (0, lax.rem(now, steps) * live + offset)
+
+    return pl.BlockSpec(block, index)
+
+
+def pair_terms(tables, pairs, query_blocks, key_blocks, running):
+    query_moves, query_arrays = zip(*query_blocks)
+    key_moves, key_arrays = zip(*key_blocks)
+    rows, columns = query_arrays[0].shape
+    keys = key_arrays[0].shape[0]
+    features = columns // 2
+    steps = head_pairs(features)
+    heads = 2 * steps
+    total = len(pairs) * steps
+    members = len(query_arrays)
+    state = [] if running is None else list(running)
+    carried = state[0].shape[0] if state else 0
+    plan = (pairs, query_moves, key_moves, carried)
+    acc = jax.ShapeDtypeStruct((members, heads, 3 * HD, rows), jnp.float32)
+    run = jax.ShapeDtypeStruct((members, steps, 8, rows), jnp.float32)
+    stat = jax.ShapeDtypeStruct((total, 8, rows), jnp.float32)
+    big = jax.ShapeDtypeStruct((total, 2, keys, rows), jnp.bfloat16)
+    operands = []
+    in_specs = [pl.BlockSpec(memory_space=pltpu.SMEM)] * 2
+    for kind, arrays in ((0, query_arrays), (1, key_arrays)):
+        for which, array in enumerate(arrays):
+            used = [at for at, pair in enumerate(pairs) if pair[kind] == which]
+            length = array.shape[0]
+            in_specs.append(step_spec(0, steps, used, total - 1, length, 2 * HD))
+            in_specs.append(step_spec(steps, steps, used, total - 1, length, 2 * HD))
+            operands += [array, array]
+    whole = pl.BlockSpec(memory_space=pltpu.VMEM)
+    in_specs += [whole] * len(state)
+    now = lambda p: (jnp.minimum(p, total - 1), 0, 0, 0)
+    then = lambda p: (jnp.maximum(p - 1, 0), 0, 0, 0)
+    block = (1, 2, keys, rows)
+    tile = pltpu.VMEM((rows, 2 * HD), jnp.bfloat16)
+    return pl.pallas_call(
+        lambda *refs: pairs_kernel(plan, *refs),
+        grid=(total + 1,),
+        in_specs=in_specs,
+        out_specs=[
+            pl.BlockSpec(block, now),
+            pl.BlockSpec(block, then),
+            whole,
+            whole,
+            pl.BlockSpec((1, 8, rows), lambda p: then(p)[:3]),
+        ],
+        out_shape=[big, big, acc, run, stat],
+        scratch_shapes=[
+            tile,
+            tile,
+            pltpu.VMEM((keys, 2 * HD), jnp.bfloat16),
+            pltpu.VMEM((keys, 2 * HD), jnp.bfloat16),
+            pltpu.VMEM((2, 2, keys, rows), jnp.bfloat16),
+            pltpu.VMEM((2, 2, 2 * HD + 16, rows), jnp.float32),
+            pltpu.VMEM((2, 8, rows), jnp.float32),
+            pltpu.VMEM((2, keys, 2 * HD), jnp.bfloat16),
+            pltpu.VMEM((2, 2 * HD, keys), jnp.bfloat16),
+            pltpu.VMEM((2, 2 * HD, rows), jnp.bfloat16),
+        ],
+        compiler_params=pltpu.CompilerParams(vmem_limit_bytes=VMEM_LIMIT),
+        cost_estimate=pl.CostEstimate(
+            flops=len(pairs) * 8 * heads * HD * rows * keys,
+            transcendentals=len(pairs) * heads * rows * keys,
+            bytes_accessed=len(pairs) * 4 * heads * rows * keys,
+        ),
+    )(*tables, *operands, *state)
+
+
+def joined(mine, other, side):
+    at = 3 * side
+    top = jnp.maximum(mine[at : at + 1], other[at : at + 1])
+    here = jnp.exp2(mine[at : at + 1] - top)
+    there = jnp.exp2(other[at : at + 1] - top)
+    inverse = 1.0 / (mine[at + 1 : at + 2] * here + other[at + 1 : at + 2] * there)
+    mean = (mine[at + 2 : at + 3] * here + other[at + 2 : at + 3] * there) * inverse
+    share = other[at + 1 : at + 2] * there * inverse
+    return top, inverse, mean, share
+
+
+def key_kernel(*refs):
+    out = refs[-1]
+    features = out.shape[1] // 2
+    scale = 1.0 / math.sqrt(HD)
+    k_total = None
+    v_total = None
+    for at in range(0, len(refs) - 1, 7):
+        e_ref, u_ref, q_ref, do_ref, pair_ref, mine, other = refs[at : at + 7]
+        q_t = q_ref[...].T.astype(jnp.float32)
+        do_t = do_ref[...].T.astype(jnp.float32)
+        for side in range(2):
+            rows = slice(side * HD, (side + 1) * HD)
+            top, inverse, mean, _ = joined(mine.at[0, 0], other.at[0, 0], side)
+            factor = jnp.exp2(pair_ref[0, 3 * side : 3 * side + 1] - top) * inverse
+            shift = pair_ref[0, 3 * side + 1 : 3 * side + 2] - mean
+            scaled_q = q_t[rows] * (factor * scale)
+            for_e = jnp.concatenate(
+                [
+                    placed((scaled_q * shift).astype(jnp.bfloat16), side),
+                    placed((do_t[rows] * factor).astype(jnp.bfloat16), side),
+                ],
+                axis=0,
+            )
+            from_e = matmul(e_ref[0, side], for_e, 1, 1)
+            from_u = matmul(u_ref[0, side], placed(scaled_q.astype(jnp.bfloat16), side), 1, 1)
+            k_part = from_e[:, : 2 * HD] + from_u
+            v_part = from_e[:, 2 * HD :]
+            k_total = k_part if k_total is None else k_total + k_part
+            v_total = v_part if v_total is None else v_total + v_part
+    at = pl.program_id(0) * (2 * HD)
+    out[:, pl.ds(pl.multiple_of(at, 2 * HD), 2 * HD)] = k_total.astype(out.dtype)
+    at = at + features
+    out[:, pl.ds(pl.multiple_of(at, 2 * HD), 2 * HD)] = v_total.astype(out.dtype)
+
+
+def member_rows(member, rows):
+    return pl.BlockSpec((1, 1, 8, rows), lambda p: (member, p, 0, 0))
+
+
+def key_terms(entries, mine, theirs, dtype):
+    operands = []
+    in_specs = []
+    for member, (e, u, query_grad, stat, base) in enumerate(entries):
+        _, _, keys, rows = e.shape
+        steps = head_pairs(query_grad.shape[1] // 2)
+        block = pl.BlockSpec((1, 2, keys, rows), lambda p, base=base: (p + base, 0, 0, 0))
+        operands += [e, u, query_grad, query_grad, stat, mine, theirs]
+        in_specs += [
+            block,
+            block,
+            column_spec(rows, 0),
+            column_spec(rows, steps),
+            pl.BlockSpec((1, 8, rows), lambda p, base=base: (p + base, 0, 0)),
+            member_rows(member, rows),
+            member_rows(1 - member, rows),
+        ]
+    heads = 2 * steps
+    return pl.pallas_call(
+        key_kernel,
+        grid=(steps,),
+        in_specs=in_specs,
+        out_specs=pl.BlockSpec(memory_space=pltpu.VMEM),
+        out_shape=jax.ShapeDtypeStruct((keys, 2 * heads * HD), dtype),
+        name="key_terms",
+        compiler_params=pltpu.CompilerParams(vmem_limit_bytes=VMEM_LIMIT),
+        cost_estimate=pl.CostEstimate(
+            flops=len(entries) * 6 * heads * HD * rows * keys,
+            transcendentals=0,
+            bytes_accessed=len(entries) * 4 * heads * rows * keys,
+        ),
+    )(*operands)
+
+
+def attend_kernel(acc, mine, out):
+    for side in range(2):
+        inverse = 1.0 / mine[0, 0, 3 * side + 1 : 3 * side + 2]
+        out[side * HD : (side + 1) * HD] = (acc[0, side] * inverse).astype(out.dtype)
+
+
+def acc_rows(member, which, rows):
+    return pl.BlockSpec((1, 2, HD, rows), lambda p: (member, p, which, 0))
+
+
+def attend_terms(member, acc, mine):
+    _, heads, _, rows = acc.shape
+    return pl.pallas_call(
+        attend_kernel,
+        grid=(heads // 2,),
+        in_specs=[acc_rows(member, 0, rows), member_rows(member, rows)],
+        out_specs=pl.BlockSpec((2 * HD, rows), lambda p: (p, 0)),
+        out_shape=jax.ShapeDtypeStruct((heads * HD, rows), jnp.bfloat16),
+        name="attend_terms",
+        compiler_params=pltpu.CompilerParams(vmem_limit_bytes=VMEM_LIMIT),
+        cost_estimate=pl.CostEstimate(
+            flops=heads * HD * rows, transcendentals=0, bytes_accessed=6 * heads * HD * rows
+        ),
+    )(acc, mine)
+
+
+def query_kernel(own, *refs):
+    if own:
+        first, second, mine, other, upper, came, out_o, out_q = refs
+    else:
+        first, second, mine, other, out_q = refs
+    scale = 1.0 / math.sqrt(HD)
+    outs = []
+    grads = []
+    for side in range(2):
+        top, inverse, mean, share = joined(mine.at[0, 0], other.at[0, 0], side)
+        factor = jnp.exp2(mine[0, 0, 3 * side : 3 * side + 1] - top) * inverse
+        grads.append((second[0, side] - first[0, side] * mean) * (factor * scale))
+        if own:
+            theirs = came[side * HD : (side + 1) * HD].astype(jnp.float32) * share
+            outs.append(upper[0, side] * factor + theirs)
+    out_q[...] = jnp.concatenate(grads, axis=0).T.astype(out_q.dtype)
+    if own:
+        out_o[...] = jnp.concatenate(outs, axis=0).T.astype(out_o.dtype)
+
+
+def query_terms(member, acc, mine, theirs, came):
+    _, heads, _, rows = acc.shape
+    own = came is not None
+    in_specs = [acc_rows(member, 1, rows), acc_rows(member, 2, rows)]
+    in_specs += [member_rows(member, rows), member_rows(1 - member, rows)]
+    operands = [acc, acc, mine, theirs]
+    shapes = [jax.ShapeDtypeStruct((rows, heads * HD), jnp.float32 if own else jnp.bfloat16)]
+    if own:
+        in_specs += [acc_rows(member, 0, rows), pl.BlockSpec((2 * HD, rows), lambda p: (p, 0))]
+        operands += [acc, came]
+        shapes = [jax.ShapeDtypeStruct((rows, heads * HD), jnp.bfloat16)] + shapes
+    return pl.pallas_call(
+        lambda *refs: query_kernel(own, *refs),
+        grid=(heads // 2,),
+        in_specs=in_specs,
+        out_specs=[column_spec(rows, 0)] * len(shapes),
+        out_shape=shapes,
+        name="query_own" if own else "query_send",
+        compiler_params=pltpu.CompilerParams(vmem_limit_bytes=VMEM_LIMIT),
+        cost_estimate=pl.CostEstimate(
+            flops=8 * heads * HD * rows, transcendentals=0, bytes_accessed=16 * heads * HD * rows
+        ),
+    )(*operands)
+
+
+def final_kernel(query_count, *refs):
+    ins, (out_q, out_k, out_v) = refs[:-3], refs[-3:]
+
+    def summed(parts):
+        total = parts[0][...].astype(jnp.float32)
+        for part in parts[1:]:
+            total = total + part[...].astype(jnp.float32)
+        return total
+
+    out_q[...] = summed(ins[:query_count]).astype(jnp.bfloat16)
+    keys = summed(ins[query_count:])
+    features = out_k.shape[1]
+    out_k[...] = keys[:, :features].astype(jnp.bfloat16)
+    out_v[...] = keys[:, features:].astype(jnp.bfloat16)
+
+
+def final_sums(query_parts, key_parts):
+    rows, features = query_parts[0].shape
+    tile = rows // 4
+    narrow = pl.BlockSpec((tile, features), lambda p: (p, 0))
+    wide = pl.BlockSpec((tile, 2 * features), lambda p: (p, 0))
+    return pl.pallas_call(
+        lambda *refs: final_kernel(len(query_parts), *refs),
+        grid=(rows // tile,),
+        in_specs=[narrow] * len(query_parts) + [wide] * len(key_parts),
+        out_specs=[narrow] * 3,
+        out_shape=[jax.ShapeDtypeStruct((rows, features), jnp.bfloat16)] * 3,
+        name="final_sums",
+    )(*query_parts, *key_parts)
+
+
+def swapped(x, offset):
+    devices = lax.axis_size("seq")
+    return lax.ppermute(x, "seq", [(i, i ^ offset) for i in range(devices)])
+
+
+def pack_kernel(k_ref, v_ref, q_ref, do_ref, kv_ref, qd_ref):
+    features = k_ref.shape[1]
+    qd_ref[:, :features] = q_ref[...]
+    qd_ref[:, features:] = do_ref[...]
+    kv_ref[:, :features] = k_ref[...]
+    kv_ref[:, features:] = v_ref[...]
+
+
+def packed(key_states, value_states, queries, grad_output):
+    rows, features = queries.shape
+    both = jax.ShapeDtypeStruct((rows, 2 * features), queries.dtype)
+    whole = pl.BlockSpec(memory_space=pltpu.VMEM)
+    return pl.pallas_call(
+        pack_kernel,
+        in_specs=[whole] * 4,
+        out_specs=[whole] * 2,
+        out_shape=[both, both],
+        name="pack",
+    )(key_states, value_states, queries, grad_output)
+
+
+def after(x, earlier):
+    return lax.optimization_barrier((x, earlier))[0]
+
+
+def dense_local(queries, key_states, value_states, grad_output, partners, global_blocks):
+    devices = lax.axis_size("seq")
+    far = devices // 2
+    tables = (partners, global_blocks)
+    key_value, query_grad = packed(key_states, value_states, queries, grad_output)
+    offsets = list(range(far))
+    neighbours = [o for o in offsets if o and o & (o - 1) == 0]
+    relayed = [o for o in offsets if o and o not in neighbours]
+    query_blocks = [(0, query_grad), (far, swapped(query_grad, far))]
+    blocks = {0: key_value}
+    for o in neighbours:
+        blocks[o] = swapped(key_value, o)
+    saved = {}
+    last = [None]
+
+    def run(pairs, members, running):
+        used = sorted({k for _, k in pairs})
+        key_blocks = [(k, blocks[k]) for k in used]
+        if last[0] is not None:
+            key_blocks = [(k, after(x, last[0])) for k, x in key_blocks]
+        plan = tuple((q, used.index(k)) for q, k in pairs)
+        e, u, acc, state, stat = pair_terms(
+            tables, plan, query_blocks[:members], key_blocks, running
+        )
+        for at, (q, k) in enumerate(pairs):
+            base = at * (stat.shape[0] // len(pairs))
+            saved[(q, k)] = (e, u, query_blocks[q][1], stat, base)
+        last[0] = stat
+        return (acc, state)
+
+    running = run([(0, 0)], 1, None)
+    for o in neighbours[:-1]:
+        running = run([(0, o)], 1, running)
+    for o in relayed:
+        lowest = o & -o
+        blocks[o] = swapped(after(blocks[o - lowest], last[0]), lowest)
+    rest = [(0, neighbours[-1])] + [(1, o) for o in [0] + neighbours]
+    running = run(rest, 2, running)
+    acc, mine = run([(q, o) for o in relayed for q in (1, 0)], 2, running)
+    theirs = swapped(mine, far)
+    upper = attend_terms(1, acc, mine)
+    came_upper = swapped(upper, far)
+    key_parts = []
+    theirs = after(theirs, upper)
+    for k in offsets[:0:-1]:
+        entries = [saved[(q, k)] for q in range(2)]
+        terms = key_terms(entries, mine, after(theirs, last[0]), jnp.bfloat16)
+        key_parts.append(swapped(terms, k))
+        last[0] = terms
+        if len(key_parts) == 1:
+            sent = query_terms(1, acc, mine, after(theirs, terms), None)[0]
+            came = swapped(sent, far)
+            last[0] = sent
+    own_entries = [saved[(q, 0)] for q in range(2)]
+    own_keys = key_terms(own_entries, mine, after(theirs, last[0]), jnp.float32)
+    came_upper = after(came_upper, own_keys)
+    attended, own_queries = query_terms(0, acc, mine, theirs, came_upper)
+    came = after(came, own_queries)
+    return (attended,) + tuple(final_sums([own_queries, came], [own_keys] + key_parts))
+
+
+def paired(devices):
+    return 4 <= devices <= LISTED and devices & (devices - 1) == 0
+
+
+def local(*operands):
+    if paired(lax.axis_size("seq")):
+        return dense_local(*operands)
+    return routed_local(*operands)
+
+
 def solution(mesh):
     in_specs = (
         P(("batch", "seq"), None),
@@ -165,4 +735,10 @@
         P(("batch", "seq"), None),
         P(("batch", "seq"), None),
     )
-    return jax.shard_map(local, mesh=mesh, in_specs=in_specs, out_specs=out_specs, check_vma=False)
+    step = jax.shard_map(
+        local, mesh=mesh, in_specs=in_specs, out_specs=out_specs, check_vma=False
+    )
+    devices = mesh.shape["seq"]
+    if paired(devices):
+        return step
+    return step

time: 712 us -> 183 us (0.26)
  waiting for transfers between devices: 349 us -> 47.8 us
  matrix products: 154 us -> 0 us
  Pallas kernels: 0 us -> 115 us
  local copies, waits for them, and re-layouts: 90.1 us -> 4.21 us
  other arithmetic: 72.1 us -> 0 us
  starting transfers between devices: 44.5 us -> 14.4 us
    all_to_all x4 -> x0, waiting for transfers between devices: 223 us -> none  [the longest x1 173 us: route_back(): lax.all_to_all(pieces, 'seq', split_axis=1, concat_axis=1, tiled=True)]
    dot_general x37 -> x0, matrix products: 154 us -> none  [the longest x6 55.6 us: per_head(): lax.dot_general(grad_head, value_head, contract_last, preferred_element_t...]
    pallas_call x0 -> x13, Pallas kernels: none -> 115 us  [the longest x4 65.3 us: pair_terms(): pl.pallas_call(lambda *refs: pairs_kernel(plan, *refs), grid=(total + 1,)...]
    ppermute x4 -> x10, waiting for transfers between devices: 126 us -> 47.8 us  [swapped(): return lax.ppermute(x, 'seq', [(i, i ^ offset) for i in range(devices)])]
    convert_element_type x6 -> x0, other arithmetic: 48.3 us -> none  [per_head(): (weights * (grad_weights - row_dots) * scale).astype(jnp.bfloat16)]
    all_to_all x4 -> x0, starting transfers between devices: 35.1 us -> none  [the longest x1 19.6 us: route_back(): lax.all_to_all(pieces, 'seq', split_axis=1, concat_axis=1, tiled=True)]
    slice x11 -> x0, local copies, waits for them, and re-layouts: 29.1 us -> none  [the longest x2 10.9 us: attend(): key_rows[:, features:]]
    unnamed x35 -> x22, local copies, waits for them, and re-layouts: 23.1 us -> 4.21 us
  transfers between devices with their start and end apart: 8 -> 10, of which waited for: 6 -> 7; matrix products, arithmetic and copies ran while one was open for 2% -> 0% of each run, Pallas kernels for 0% -> 34%
where the time goes in v3:
time: 183 us; the launch traced here: 182 us
  Pallas kernels  115 us (63%)
  waiting for transfers between devices  47.8 us (26%)
  starting transfers between devices  14.4 us (8%)
  local copies, waits for them, and re-layouts  4.21 us (2%)
    pallas_call x4, Pallas kernels, pair_terms(): pl.pallas_call(lambda *refs: pairs_kernel(plan, *refs), grid=(total + 1,)...  65.3 us
    ppermute x10, waiting for transfers between devices, swapped(): return lax.ppermute(x, 'seq', [(i, i ^ offset) for i in range(devices)])  47.8 us
    pallas_call x4, Pallas kernels, key_terms(): pl.pallas_call(key_kernel, grid=(steps,), in_specs=in_specs, out_specs=pl...  33.7 us
    ppermute x10, starting transfers between devices, swapped(): return lax.ppermute(x, 'seq', [(i, i ^ offset) for i in range(devices)])  14.4 us
    pallas_call x2, Pallas kernels, query_terms(): pl.pallas_call(lambda *refs: query_kernel(own, *refs), grid=(heads // 2,)...  6.8 us
    pallas_call x1, Pallas kernels, final_sums(): pl.pallas_call(lambda *refs: final_kernel(len(query_parts), *refs), grid=...  4.22 us
    unnamed x22, local copies, waits for them, and re-layouts  4.21 us
  transfers between devices with their start and end apart: 10, of which 7 were waited for; matrix products, arithmetic and copies ran while one was open for 0% of the time, Pallas kernels for 34%

profile of v3, /device:TPU:0, one launch (start us, length us, event | category | flops | bytes accessed | tf_op | source)
XLA Modules:
  0.0 182.4 jit_solution(6091812696233970694)
XLA Ops:
  0.6 2.6 %pack.1 = (bf16[512,768]{1,0:T(8,128)(2,1)}, bf16[512,768]{1,0:T(8,128)(2,1)}) custom-call(bf16[512,384]{1,0:T(8,128)(2,1)} %k_ref.1, bf16[512,384]{1,0:T(8,128)(2,1)} %v_ref.1, bf16[512,384]{1,0:T(8,128)(2,1)} %q_ref.1, bf16[512,384]{1,0:T(8,128)(2,1)} %do_ref.1), custom_call_target="tpu_custom_call" | custom-call | tf_op jit(solution)/shard_map/pack/pallas_call | solution.py:639
  3.2 3.0 %collective-permute-start.2 = (bf16[512,768]{1,0:T(8,128)(2,1)}, bf16[512,768]{1,0:T(8,128)(2,1)S(1)}, u32[]{:S(2)}, u32[]{:S(2)}) collective-permute-start(bf16[512,768]{1,0:T(8,128)(2,1)} %get-tuple-element.52.refs_4_.refs_5_.refs_6_.refs_7_), channel_id=1, source_target_pairs={{0,4},{4,0},{8,12},{12,8},{16,20},{20,16},{24,28},{28,24},{1,5},{5... | collective-permute-start | bytes 2359304 | tf_op jit(solution)/shard_map/ppermute | solution.py:624
  6.2 1.6 collective-permute-start.1
  7.8 2.6 %collective-permute-start = (bf16[512,768]{1,0:T(8,128)(2,1)}, bf16[512,768]{1,0:T(8,128)(2,1)S(1)}, u32[]{:S(2)}, u32[]{:S(2)}) collective-permute-start(bf16[512,768]{1,0:T(8,128)(2,1)} %get-tuple-element.44.refs_2_.refs_3_), channel_id=1, source_target_pairs={{0,16},{4,20},{8,24},{12,28},{16,0},{20,4},{24,8},{28,12},{1,17},{... | collective-permute-start | bytes 2359304 | tf_op jit(solution)/shard_map/ppermute | solution.py:624
  10.4 9.4 %shard_map.93 = (bf16[3,2,512,512]{3,2,1,0:T(8,128)(2,1)}, bf16[3,2,512,512]{3,2,1,0:T(8,128)(2,1)}, f32[1,6,192,512]{3,2,1,0:T(8,128)}, f32[1,3,8,512]{3,2,1,0:T(8,128)}, f32[3,8,512]{2,1,0:T(8,128)}) custom-call(s32[3,8]{1,0:T(4,128)} %refs_0_.7, s32[2]{0:T(128)} %refs_1_.7, bf16[512,768]{1,0:T(8,128)(2,1)} %get-tuple-element.44.refs_2_.refs_3_, ...), custom_call_target="tpu_custom_call" | custom-call | flops 805306368 | bytes 6291456 | tf_op jit(solution)/shard_map/pallas_call | solution.py:403
  19.8 4.1 %collective-permute-done.2.refs_4_.refs_5_.refs_8_.refs_9_ = bf16[512,768]{1,0:T(8,128)(2,1)S(1)} collective-permute-done((bf16[512,768]{1,0:T(8,128)(2,1)}, bf16[512,768]{1,0:T(8,128)(2,1)S(1)}, u32[]{:S(2)}, u32[]{:S(2)}) %collective-permute-start.2) | collective-permute-done | bytes 786464 | tf_op jit(solution)/shard_map/ppermute | solution.py:624
  24.0 0.9 copy-done.2
  24.9 10.4 %shard_map.94 = (bf16[3,2,512,512]{3,2,1,0:T(8,128)(2,1)}, bf16[3,2,512,512]{3,2,1,0:T(8,128)(2,1)}, f32[1,6,192,512]{3,2,1,0:T(8,128)}, f32[1,3,8,512]{3,2,1,0:T(8,128)}, f32[3,8,512]{2,1,0:T(8,128)}) custom-call(s32[3,8]{1,0:T(4,128)} %refs_0_.7, s32[2]{0:T(128)} %refs_1_.7, bf16[512,768]{1,0:T(8,128)(2,1)} %get-tuple-element.44.refs_2_.refs_3_, ...), custom_call_target="tpu_custom_call" | custom-call | flops 805306368 | bytes 6291456 | tf_op jit(solution)/shard_map/pallas_call | solution.py:403
  35.3 6.9 %collective-permute-done.1.refs_10_.refs_11_ = bf16[512,768]{1,0:T(8,128)(2,1)S(1)} collective-permute-done((bf16[512,768]{1,0:T(8,128)(2,1)}, bf16[512,768]{1,0:T(8,128)(2,1)S(1)}, u32[]{:S(2)}, u32[]{:S(2)}) %collective-permute-start.1) | collective-permute-done | bytes 786464 | tf_op jit(solution)/shard_map/ppermute | solution.py:624
  42.6 2.0 %collective-permute-done.refs_4_.refs_5_.refs_9_.refs_10_ = bf16[512,768]{1,0:T(8,128)(2,1)S(1)} collective-permute-done((bf16[512,768]{1,0:T(8,128)(2,1)}, bf16[512,768]{1,0:T(8,128)(2,1)S(1)}, u32[]{:S(2)}, u32[]{:S(2)}) %collective-permute-start) | collective-permute-done | bytes 786464 | tf_op jit(solution)/shard_map/ppermute | solution.py:624
  44.5 0.9 copy-done
  45.4 28.0 %shard_map.95 = (bf16[12,2,512,512]{3,2,1,0:T(8,128)(2,1)}, bf16[12,2,512,512]{3,2,1,0:T(8,128)(2,1)}, f32[2,6,192,512]{3,2,1,0:T(8,128)}, f32[2,3,8,512]{3,2,1,0:T(8,128)}, f32[12,8,512]{2,1,0:T(8,128)}) custom-call(s32[3,8]{1,0:T(4,128)} %refs_0_.7, s32[2]{0:T(128)} %refs_1_.7, bf16[512,768]{1,0:T(8,128)(2,1)} %get-tuple-element.44.refs_2_.refs_3_, ...), custom_call_target="tpu_custom_call" | custom-call | flops 3221225472 | bytes 25165824 | tf_op jit(solution)/shard_map/pallas_call | solution.py:403
  73.4 0.9 copy-done.3
  74.3 17.5 %shard_map.96 = (bf16[6,2,512,512]{3,2,1,0:T(8,128)(2,1)}, bf16[6,2,512,512]{3,2,1,0:T(8,128)(2,1)}, f32[2,6,192,512]{3,2,1,0:T(8,128)}, f32[2,3,8,512]{3,2,1,0:T(8,128)}, f32[6,8,512]{2,1,0:T(8,128)}) custom-call(s32[3,8]{1,0:T(4,128)} %refs_0_.7, s32[2]{0:T(128)} %refs_1_.7, bf16[512,768]{1,0:T(8,128)(2,1)} %get-tuple-element.44.refs_2_.refs_3_, ...), custom_call_target="tpu_custom_call" | custom-call | flops 1610612736 | bytes 12582912 | tf_op jit(solution)/shard_map/pallas_call | solution.py:403
  91.8 0.4 collective-permute-start.4
  92.2 2.7 %attend_terms.1 = bf16[384,512]{1,0:T(8,128)(2,1)} custom-call(f32[2,6,192,512]{3,2,1,0:T(8,128)} %get-tuple-element.60.acc.refs_0_.refs_1_.refs_4_, f32[2,3,8,512]{3,2,1,0:T(8,128)} %get-tuple-element.61.mine.refs_5_.refs_12_.refs_2_), custom_call_target="tpu_custom_call" | custom-call | flops 196608 | bytes 1179648 | tf_op jit(solution)/shard_map/attend_terms/pallas_call | solution.py:532
  94.9 3.6 %collective-permute-done.4.refs_6_.refs_13_.refs_3_ = f32[2,3,8,512]{3,2,1,0:T(8,128)S(1)} collective-permute-done((f32[2,3,8,512]{3,2,1,0:T(8,128)}, f32[2,3,8,512]{3,2,1,0:T(8,128)S(1)}, u32[]{:S(2)}, u32[]{:S(2)}) %collective-permute-start.4) | collective-permute-done | bytes 98336 | tf_op jit(solution)/shard_map/ppermute | solution.py:624
  98.5 0.6 copy-done.1
  99.1 8.3 %key_terms.4 = bf16[512,768]{1,0:T(8,128)(2,1)} custom-call(bf16[6,2,512,512]{3,2,1,0:T(8,128)(2,1)} %get-tuple-element.69.refs_0_.refs_7_, bf16[6,2,512,512]{3,2,1,0:T(8,128)(2,1)} %get-tuple-element.70.refs_1_.refs_8_, bf16[512,768]{1,0:T(8,128)(2,1)} %get-tuple-element.44.refs_2_.refs_3_, bf16[512,768]{1,0:T(8,128)(2,1)} %get-tuple-element.44.refs_2_.refs_3_, ...), custom_call_target="tpu_custom_call" | custom-call | flops 1207959552 | bytes 12582912 | tf_op jit(solution)/shard_map/key_terms/pallas_call | solution.py:504
  107.5 3.1 %query_send.1 = bf16[512,384]{1,0:T(8,128)(2,1)} custom-call(f32[2,6,192,512]{3,2,1,0:T(8,128)} %get-tuple-element.60.acc.refs_0_.refs_1_.refs_4_, f32[2,6,192,512]{3,2,1,0:T(8,128)} %get-tuple-element.60.acc.refs_0_.refs_1_.refs_4_, f32[2,3,8,512]{3,2,1,0:T(8,128)} %get-tuple-element.61.mine.refs_5_.refs_12_.refs_2_, f32[2,3,8,512]{3,2,1,0:T(8,128)} %copy-done.1), custom_call_target="tpu_custom_call" | custom-call | flops 1572864 | bytes 3145728 | tf_op jit(solution)/shard_map/query_send/pallas_call | solution.py:577
  110.5 8.3 %key_terms.5 = bf16[512,768]{1,0:T(8,128)(2,1)} custom-call(bf16[12,2,512,512]{3,2,1,0:T(8,128)(2,1)} %get-tuple-element.67.refs_0_.refs_7_, bf16[12,2,512,512]{3,2,1,0:T(8,128)(2,1)} %get-tuple-element.68.refs_1_.refs_8_, bf16[512,768]{1,0:T(8,128)(2,1)} %get-tuple-element.44.refs_2_.refs_3_, bf16[512,768]{1,0:T(8,128)(2,1)} %get-tuple-element.44.refs_2_.refs_3_, ...), custom_call_target="tpu_custom_call" | custom-call | flops 1207959552 | bytes 12582912 | tf_op jit(solution)/shard_map/key_terms/pallas_call | solution.py:504
  118.9 8.4 %key_terms.6 = bf16[512,768]{1,0:T(8,128)(2,1)} custom-call(bf16[3,2,512,512]{3,2,1,0:T(8,128)(2,1)} %get-tuple-element.65.refs_0_, bf16[3,2,512,512]{3,2,1,0:T(8,128)(2,1)} %get-tuple-element.66.refs_1_, bf16[512,768]{1,0:T(8,128)(2,1)} %get-tuple-element.44.refs_2_.refs_3_, bf16[512,768]{1,0:T(8,128)(2,1)} %get-tuple-element.44.refs_2_.refs_3_, ...), custom_call_target="tpu_custom_call" | custom-call | flops 1207959552 | bytes 12582912 | tf_op jit(solution)/shard_map/key_terms/pallas_call | solution.py:504
  127.3 0.6 collective-permute-start.9
  127.9 3.0 %collective-permute-start.7 = (bf16[512,768]{1,0:T(8,128)(2,1)S(1)}, bf16[512,768]{1,0:T(8,128)(2,1)S(1)}, u32[]{:S(2)}, u32[]{:S(2)}) collective-permute-start(bf16[512,768]{1,0:T(8,128)(2,1)S(1)} %copy-done.7), channel_id=1, source_target_pairs={{0,12},{4,8},{8,4},{12,0},{16,28},{20,24},{24,20},{28,16},{1,13},{... | collective-permute-start | bytes 2359304 | tf_op jit(solution)/shard_map/ppermute | solution.py:624
  131.0 2.8 %collective-permute-start.6 = (bf16[512,384]{1,0:T(8,128)(2,1)S(1)}, bf16[512,384]{1,0:T(8,128)(2,1)}, u32[]{:S(2)}, u32[]{:S(2)}) collective-permute-start(bf16[512,384]{1,0:T(8,128)(2,1)S(1)} %copy-done.8), channel_id=1, source_target_pairs={{0,16},{4,20},{8,24},{12,28},{16,0},{20,4},{24,8},{28,12},{1,17},{... | collective-permute-start | bytes 1179656 | tf_op jit(solution)/shard_map/ppermute | solution.py:624
  133.8 8.6 %key_terms.7.refs_2_ = f32[512,768]{1,0:T(8,128)} custom-call(bf16[3,2,512,512]{3,2,1,0:T(8,128)(2,1)} %get-tuple-element.63.refs_0_, bf16[3,2,512,512]{3,2,1,0:T(8,128)(2,1)} %get-tuple-element.64.refs_1_, bf16[512,768]{1,0:T(8,128)(2,1)} %get-tuple-element.44.refs_2_.refs_3_, bf16[512,768]{1,0:T(8,128)(2,1)} %get-tuple-element.44.refs_2_.refs_3_, ...), custom_call_target="tpu_custom_call" | custom-call | flops 1207959552 | bytes 12582912 | tf_op jit(solution)/shard_map/key_terms/pallas_call | solution.py:504
  142.4 28.9 %collective-permute-done.5.refs_5_ = bf16[384,512]{1,0:T(8,128)(2,1)} collective-permute-done((bf16[384,512]{1,0:T(8,128)(2,1)S(1)}, bf16[384,512]{1,0:T(8,128)(2,1)}, u32[]{:S(2)}, u32[]{:S(2)}) %collective-permute-start.5) | collective-permute-done | bytes 393248 | tf_op jit(solution)/shard_map/ppermute | solution.py:624
  171.3 3.7 %query_own.1 = (bf16[512,384]{1,0:T(8,128)(2,1)}, f32[512,384]{1,0:T(8,128)}) custom-call(f32[2,6,192,512]{3,2,1,0:T(8,128)} %get-tuple-element.60.acc.refs_0_.refs_1_.refs_4_, f32[2,6,192,512]{3,2,1,0:T(8,128)} %get-tuple-element.60.acc.refs_0_.refs_1_.refs_4_, f32[2,3,8,512]{3,2,1,0:T(8,128)} %get-tuple-element.61.mine.refs_5_.refs_12_.refs_2_, ...), custom_call_target="tpu_custom_call" | custom-call | flops 1572864 | bytes 3145728 | tf_op jit(solution)/shard_map/query_own/pallas_call | solution.py:577
  175.0 0.6 collective-permute-done.6.refs_1_
  175.6 1.7 collective-permute-done.7.refs_3_
  177.3 0.9 copy-done.6
  178.2 4.2 %final_sums.1 = (bf16[512,384]{1,0:T(8,128)(2,1)}, bf16[512,384]{1,0:T(8,128)(2,1)}, bf16[512,384]{1,0:T(8,128)(2,1)}) custom-call(f32[512,384]{1,0:T(8,128)} %get-tuple-element.79.refs_0_, bf16[512,384]{1,0:T(8,128)(2,1)} %collective-permute-done.6.refs_1_, f32[512,768]{1,0:T(8,128)} %key_terms.7.refs_2_, bf16[512,768]{1,0:T(8,128)(2,1)} %copy-done.6, ...), custom_call_target="tpu_custom_call" | custom-call | tf_op jit(solution)/shard_map/final_sums/pallas_call | solution.py:612
  (23 shorter events, 0.5 us)
Async XLA Ops:
  3.2 20.7 %collective-permute-start.2 = (bf16[512,768]{1,0:T(8,128)(2,1)}, bf16[512,768]{1,0:T(8,128)(2,1)S(1)}, u32[]{:S(2)}, u32[]{:S(2)}) collective-permute-start(bf16[512,768]{1,0:T(8,128)(2,1)} %get-tuple-element.52.refs_4_.refs_5_.refs_6_.refs_7_), channel_id=1, source_target_pairs={{0,4},{4,0},{8,12},{12,8},{16,20},{20,16},{24,28},{28,24},{1,5},{5... | collective-permute-start | bytes 2359304 | tf_op jit(solution)/shard_map/ppermute | solution.py:624
  6.2 35.9 %collective-permute-start.1 = (bf16[512,768]{1,0:T(8,128)(2,1)}, bf16[512,768]{1,0:T(8,128)(2,1)S(1)}, u32[]{:S(2)}, u32[]{:S(2)}) collective-permute-start(bf16[512,768]{1,0:T(8,128)(2,1)} %get-tuple-element.52.refs_4_.refs_5_.refs_6_.refs_7_), channel_id=1, source_target_pairs={{0,8},{4,12},{8,0},{12,4},{16,24},{20,28},{24,16},{28,20},{1,9},{5... | collective-permute-start | bytes 2359304 | tf_op jit(solution)/shard_map/ppermute | solution.py:624
  7.8 36.7 %collective-permute-start = (bf16[512,768]{1,0:T(8,128)(2,1)}, bf16[512,768]{1,0:T(8,128)(2,1)S(1)}, u32[]{:S(2)}, u32[]{:S(2)}) collective-permute-start(bf16[512,768]{1,0:T(8,128)(2,1)} %get-tuple-element.44.refs_2_.refs_3_), channel_id=1, source_target_pairs={{0,16},{4,20},{8,24},{12,28},{16,0},{20,4},{24,8},{28,12},{1,17},{... | collective-permute-start | bytes 2359304 | tf_op jit(solution)/shard_map/ppermute | solution.py:624
  24.0 0.9 copy-start.2
  42.2 2.4 %copy-start.10 = (bf16[512,768]{1,0:T(8,128)(2,1)}, bf16[512,768]{1,0:T(8,128)(2,1)S(1)}, u32[]{:S(2)}) copy-start(bf16[512,768]{1,0:T(8,128)(2,1)S(1)} %collective-permute-done.1.refs_10_.refs_11_) | copy-start | bytes 2359300
  42.2 31.2 %collective-permute-start.3 = (bf16[512,768]{1,0:T(8,128)(2,1)S(1)}, bf16[512,768]{1,0:T(8,128)(2,1)S(1)}, u32[]{:S(2)}, u32[]{:S(2)}) collective-permute-start(bf16[512,768]{1,0:T(8,128)(2,1)S(1)} %collective-permute-done.1.refs_10_.refs_11_), channel_id=1, source_target_pairs={{0,4},{4,0},{8,12},{12,8},{16,20},{20,16},{24,28},{28,24},{1,5},{5... | collective-permute-start | bytes 2359304 | tf_op jit(solution)/shard_map/ppermute | solution.py:624
  44.5 0.9 copy-start
  73.4 0.9 copy-start.3
  91.8 6.7 %collective-permute-start.4 = (f32[2,3,8,512]{3,2,1,0:T(8,128)}, f32[2,3,8,512]{3,2,1,0:T(8,128)S(1)}, u32[]{:S(2)}, u32[]{:S(2)}) collective-permute-start(f32[2,3,8,512]{3,2,1,0:T(8,128)} %get-tuple-element.61.mine.refs_5_.refs_12_.refs_2_), channel_id=1, source_target_pairs={{0,16},{4,20},{8,24},{12,28},{16,0},{20,4},{24,8},{28,12},{1,17},{... | collective-permute-start | bytes 294920 | tf_op jit(solution)/shard_map/ppermute | solution.py:624
  98.5 0.6 copy-start.1
  118.8 9.0 %copy-start.7 = (bf16[512,768]{1,0:T(8,128)(2,1)S(1)}, bf16[512,768]{1,0:T(8,128)(2,1)}, u32[]{:S(2)}) copy-start(bf16[512,768]{1,0:T(8,128)(2,1)} %key_terms.4) | copy-start | bytes 2359300
  118.9 12.0 %copy-start.9 = (bf16[384,512]{1,0:T(8,128)(2,1)S(1)}, bf16[384,512]{1,0:T(8,128)(2,1)}, u32[]{:S(2)}) copy-start(bf16[384,512]{1,0:T(8,128)(2,1)} %attend_terms.1) | copy-start | bytes 1179652
  118.9 12.1 %copy-start.8 = (bf16[512,384]{1,0:T(8,128)(2,1)S(1)}, bf16[512,384]{1,0:T(8,128)(2,1)}, u32[]{:S(2)}) copy-start(bf16[512,384]{1,0:T(8,128)(2,1)} %query_send.1) | copy-start | bytes 1179652
  127.3 48.3 %collective-permute-start.9 = (bf16[512,768]{1,0:T(8,128)(2,1)}, bf16[512,768]{1,0:T(8,128)(2,1)S(1)}, u32[]{:S(2)}, u32[]{:S(2)}) collective-permute-start(bf16[512,768]{1,0:T(8,128)(2,1)} %key_terms.6), channel_id=1, source_target_pairs={{0,4},{4,0},{8,12},{12,8},{16,20},{20,16},{24,28},{28,24},{1,5},{5... | collective-permute-start | bytes 2359304 | tf_op jit(solution)/shard_map/ppermute | solution.py:624
  127.9 47.7 %collective-permute-start.8 = (bf16[512,768]{1,0:T(8,128)(2,1)}, bf16[512,768]{1,0:T(8,128)(2,1)S(1)}, u32[]{:S(2)}, u32[]{:S(2)}) collective-permute-start(bf16[512,768]{1,0:T(8,128)(2,1)} %key_terms.5), channel_id=1, source_target_pairs={{0,8},{4,12},{8,0},{12,4},{16,24},{20,28},{24,16},{28,20},{1,9},{5... | collective-permute-start | bytes 2359304 | tf_op jit(solution)/shard_map/ppermute | solution.py:624
  127.9 49.4 %collective-permute-start.7 = (bf16[512,768]{1,0:T(8,128)(2,1)S(1)}, bf16[512,768]{1,0:T(8,128)(2,1)S(1)}, u32[]{:S(2)}, u32[]{:S(2)}) collective-permute-start(bf16[512,768]{1,0:T(8,128)(2,1)S(1)} %copy-done.7), channel_id=1, source_target_pairs={{0,12},{4,8},{8,4},{12,0},{16,28},{20,24},{24,20},{28,16},{1,13},{... | collective-permute-start | bytes 2359304 | tf_op jit(solution)/shard_map/ppermute | solution.py:624
  130.9 40.4 %collective-permute-start.5 = (bf16[384,512]{1,0:T(8,128)(2,1)S(1)}, bf16[384,512]{1,0:T(8,128)(2,1)}, u32[]{:S(2)}, u32[]{:S(2)}) collective-permute-start(bf16[384,512]{1,0:T(8,128)(2,1)S(1)} %copy-done.9), channel_id=1, source_target_pairs={{0,16},{4,20},{8,24},{12,28},{16,0},{20,4},{24,8},{28,12},{1,17},{... | collective-permute-start | bytes 1179656 | tf_op jit(solution)/shard_map/ppermute | solution.py:624
  131.0 44.7 %collective-permute-start.6 = (bf16[512,384]{1,0:T(8,128)(2,1)S(1)}, bf16[512,384]{1,0:T(8,128)(2,1)}, u32[]{:S(2)}, u32[]{:S(2)}) collective-permute-start(bf16[512,384]{1,0:T(8,128)(2,1)S(1)} %copy-done.8), channel_id=1, source_target_pairs={{0,16},{4,20},{8,24},{12,28},{16,0},{20,4},{24,8},{28,12},{1,17},{... | collective-permute-start | bytes 1179656 | tf_op jit(solution)/shard_map/ppermute | solution.py:624
  175.6 1.7 copy-start.4
  175.6 1.7 copy-start.5
  177.3 0.9 copy-start.6

commit v4 on v3

--- a/solution.py
+++ b/solution.py
@@ -176,7 +176,8 @@
 ]
 LISTED = 8
 TO_LOG2 = 1.0 / (math.log(2.0) * math.sqrt(HD))
-VMEM_LIMIT = 60 * 1024 * 1024
+VMEM_LIMIT = 40 * 1024 * 1024
+PAIR_LIMIT = 40 * 1024 * 1024
 
 
 def matmul(a, b, contract_a, contract_b):
@@ -424,7 +425,7 @@
             pltpu.VMEM((2, 2 * HD, keys), jnp.bfloat16),
             pltpu.VMEM((2, 2 * HD, rows), jnp.bfloat16),
         ],
-        compiler_params=pltpu.CompilerParams(vmem_limit_bytes=VMEM_LIMIT),
+        compiler_params=pltpu.CompilerParams(vmem_limit_bytes=PAIR_LIMIT),
         cost_estimate=pl.CostEstimate(
             flops=len(pairs) * 8 * heads * HD * rows * keys,
             transcendentals=len(pairs) * heads * rows * keys,
@@ -690,9 +691,8 @@
     acc, mine = run([(q, o) for o in relayed for q in (1, 0)], 2, running)
     theirs = swapped(mine, far)
     upper = attend_terms(1, acc, mine)
-    came_upper = swapped(upper, far)
+    came_upper = swapped(after(upper, theirs), far)
     key_parts = []
-    theirs = after(theirs, upper)
     for k in offsets[:0:-1]:
         entries = [saved[(q, k)] for q in range(2)]
         terms = key_terms(entries, mine, after(theirs, last[0]), jnp.bfloat16)

time: 183 us -> 169 us (0.923)
  Pallas kernels: 115 us -> 88.5 us
  local copies, waits for them, and re-layouts: 4.21 us -> 14.9 us
  waiting for transfers between devices: 47.8 us -> 50.1 us
    pallas_call x4, Pallas kernels: 65.3 us -> 53.4 us  [pair_terms(): pl.pallas_call(lambda *refs: pairs_kernel(plan, *refs), grid=(total + 1,)...]
    unnamed x22 -> x40, local copies, waits for them, and re-layouts: 4.21 us -> 14.9 us
    pallas_call x4, Pallas kernels: 33.7 us -> 25.6 us  [key_terms(): pl.pallas_call(key_kernel, grid=(steps,), in_specs=in_specs, out_specs=pl...]
    pallas_call x2, Pallas kernels: 6.8 us -> 2.48 us  [query_terms(): pl.pallas_call(lambda *refs: query_kernel(own, *refs), grid=(heads // 2,)...]
    pallas_call x1, Pallas kernels: 2.73 us -> 0.19 us  [attend_terms(): pl.pallas_call(attend_kernel, grid=(heads // 2,), in_specs=[acc_rows(memb...]
    ppermute x10, waiting for transfers between devices: 47.8 us -> 50.1 us  [swapped(): return lax.ppermute(x, 'seq', [(i, i ^ offset) for i in range(devices)])]
  transfers between devices with their start and end apart: 10 -> 10, of which waited for: 7 -> 6; matrix products, arithmetic and copies ran while one was open for 0% -> 0% of each run, Pallas kernels for 34% -> 28%
where the time goes in v4:
time: 169 us
  Pallas kernels  88.5 us (52%)
  waiting for transfers between devices  50.1 us (30%)
  local copies, waits for them, and re-layouts  14.9 us (9%)
  starting transfers between devices  14.4 us (9%)
    pallas_call x4, Pallas kernels, pair_terms(): pl.pallas_call(lambda *refs: pairs_kernel(plan, *refs), grid=(total + 1,)...  53.4 us
    ppermute x10, waiting for transfers between devices, swapped(): return lax.ppermute(x, 'seq', [(i, i ^ offset) for i in range(devices)])  50.1 us
    pallas_call x4, Pallas kernels, key_terms(): pl.pallas_call(key_kernel, grid=(steps,), in_specs=in_specs, out_specs=pl...  25.6 us
    unnamed x40, local copies, waits for them, and re-layouts  14.9 us
    ppermute x10, starting transfers between devices, swapped(): return lax.ppermute(x, 'seq', [(i, i ^ offset) for i in range(devices)])  14.4 us
    pallas_call x1, Pallas kernels, final_sums(): pl.pallas_call(lambda *refs: final_kernel(len(query_parts), *refs), grid=...  4.22 us
  transfers between devices with their start and end apart: 10, of which 6 were waited for; matrix products, arithmetic and copies ran while one was open for 0% of the time, Pallas kernels for 28%

profile of v4, /device:TPU:0, one launch (start us, length us, event | category | flops | bytes accessed | tf_op | source)
XLA Modules:
  0.0 168.7 jit_solution(14695656725669894737)
XLA Ops:
  0.6 2.6 %pack.1 = (bf16[512,768]{1,0:T(8,128)(2,1)}, bf16[512,768]{1,0:T(8,128)(2,1)}) custom-call(bf16[512,384]{1,0:T(8,128)(2,1)} %k_ref.1, bf16[512,384]{1,0:T(8,128)(2,1)} %v_ref.1, bf16[512,384]{1,0:T(8,128)(2,1)} %q_ref.1, bf16[512,384]{1,0:T(8,128)(2,1)} %do_ref.1), custom_call_target="tpu_custom_call" | custom-call | tf_op jit(solution)/shard_map/pack/pallas_call | solution.py:640
  3.2 3.0 %collective-permute-start.2 = (bf16[512,768]{1,0:T(8,128)(2,1)}, bf16[512,768]{1,0:T(8,128)(2,1)S(1)}, u32[]{:S(2)}, u32[]{:S(2)}) collective-permute-start(bf16[512,768]{1,0:T(8,128)(2,1)} %get-tuple-element.52.refs_4_.refs_5_.refs_6_.refs_7_), channel_id=1, source_target_pairs={{0,4},{4,0},{8,12},{12,8},{16,20},{20,16},{24,28},{28,24},{1,5},{5... | collective-permute-start | bytes 2359304 | tf_op jit(solution)/shard_map/ppermute | solution.py:625
  6.2 1.6 collective-permute-start.1
  7.8 2.6 %collective-permute-start = (bf16[512,768]{1,0:T(8,128)(2,1)}, bf16[512,768]{1,0:T(8,128)(2,1)S(1)}, u32[]{:S(2)}, u32[]{:S(2)}) collective-permute-start(bf16[512,768]{1,0:T(8,128)(2,1)} %get-tuple-element.44.refs_2_.refs_3_), channel_id=1, source_target_pairs={{0,16},{4,20},{8,24},{12,28},{16,0},{20,4},{24,8},{28,12},{1,17},{... | collective-permute-start | bytes 2359304 | tf_op jit(solution)/shard_map/ppermute | solution.py:625
  10.4 1.2 copy-done
  11.5 1.1 copy-done.12
  12.7 0.7 copy-done.14
  14.0 6.9 %shard_map.93 = (bf16[3,2,512,512]{3,2,1,0:T(8,128)(2,1)S(1)}, bf16[3,2,512,512]{3,2,1,0:T(8,128)(2,1)S(1)}, f32[1,6,192,512]{3,2,1,0:T(8,128)S(1)}, f32[1,3,8,512]{3,2,1,0:T(8,128)S(1)}, f32[3,8,512]{2,1,0:T(8,128)S(1)}) custom-call(s32[3,8]{1,0:T(4,128)S(1)} %copy-done.14, s32[2]{0:T(128)S(1)} %copy-done.15, bf16[512,768]{1,0:T(8,128)(2,1)S(1)} %copy-done, ...), custom_call_target="tpu_custom_call" | custom-call | flops 805306368 | bytes 6291456 | tf_op jit(solution)/shard_map/pallas_call | solution.py:404
  20.9 1.6 copy-done.4
  22.5 1.7 copy-done.6
  24.2 6.9 %shard_map.94 = (bf16[3,2,512,512]{3,2,1,0:T(8,128)(2,1)S(1)}, bf16[3,2,512,512]{3,2,1,0:T(8,128)(2,1)S(1)}, f32[1,6,192,512]{3,2,1,0:T(8,128)S(1)}, f32[1,3,8,512]{3,2,1,0:T(8,128)S(1)}, f32[3,8,512]{2,1,0:T(8,128)S(1)}) custom-call(s32[3,8]{1,0:T(4,128)S(1)} %copy-done.14, s32[2]{0:T(128)S(1)} %copy-done.15, bf16[512,768]{1,0:T(8,128)(2,1)S(1)} %copy-done.1, ...), custom_call_target="tpu_custom_call" | custom-call | flops 805306368 | bytes 6291456 | tf_op jit(solution)/shard_map/pallas_call | solution.py:404
  31.2 1.8 %copy-done.8 = bf16[3,2,512,512]{3,2,1,0:T(8,128)(2,1)} copy-done((bf16[3,2,512,512]{3,2,1,0:T(8,128)(2,1)}, bf16[3,2,512,512]{3,2,1,0:T(8,128)(2,1)S(1)}, u32[]{:S(2)}) %copy-start.8) | copy-done | bytes 3145752
  32.9 1.7 copy-done.10
  34.6 7.5 %collective-permute-done.1.refs_10_.refs_11_ = bf16[512,768]{1,0:T(8,128)(2,1)S(1)} collective-permute-done((bf16[512,768]{1,0:T(8,128)(2,1)}, bf16[512,768]{1,0:T(8,128)(2,1)S(1)}, u32[]{:S(2)}, u32[]{:S(2)}) %collective-permute-start.1) | collective-permute-done | bytes 786464 | tf_op jit(solution)/shard_map/ppermute | solution.py:625
  42.5 2.0 %collective-permute-done.refs_4_.refs_5_.refs_9_.refs_10_ = bf16[512,768]{1,0:T(8,128)(2,1)S(1)} collective-permute-done((bf16[512,768]{1,0:T(8,128)(2,1)}, bf16[512,768]{1,0:T(8,128)(2,1)S(1)}, u32[]{:S(2)}, u32[]{:S(2)}) %collective-permute-start) | collective-permute-done | bytes 786464 | tf_op jit(solution)/shard_map/ppermute | solution.py:625
  44.5 25.5 %shard_map.95 = (bf16[12,2,512,512]{3,2,1,0:T(8,128)(2,1)}, bf16[12,2,512,512]{3,2,1,0:T(8,128)(2,1)}, f32[2,6,192,512]{3,2,1,0:T(8,128)S(1)}, f32[2,3,8,512]{3,2,1,0:T(8,128)S(1)}, f32[12,8,512]{2,1,0:T(8,128)S(1)}) custom-call(s32[3,8]{1,0:T(4,128)S(1)} %copy-done.14, s32[2]{0:T(128)S(1)} %copy-done.15, bf16[512,768]{1,0:T(8,128)(2,1)S(1)} %copy-done.1, ...), custom_call_target="tpu_custom_call" | custom-call | flops 3221225472 | bytes 25165824 | tf_op jit(solution)/shard_map/pallas_call | solution.py:404
  70.0 14.1 %shard_map.96 = (bf16[6,2,512,512]{3,2,1,0:T(8,128)(2,1)}, bf16[6,2,512,512]{3,2,1,0:T(8,128)(2,1)}, f32[2,6,192,512]{3,2,1,0:T(8,128)S(1)}, f32[2,3,8,512]{3,2,1,0:T(8,128)S(1)}, f32[6,8,512]{2,1,0:T(8,128)S(1)}) custom-call(s32[3,8]{1,0:T(4,128)S(1)} %copy-done.14, s32[2]{0:T(128)S(1)} %copy-done.15, bf16[512,768]{1,0:T(8,128)(2,1)S(1)} %copy-done.1, ...), custom_call_target="tpu_custom_call" | custom-call | flops 1610612736 | bytes 12582912 | tf_op jit(solution)/shard_map/pallas_call | solution.py:404
  84.4 6.1 %collective-permute-done.4.refs_6_.refs_13_.refs_3_ = f32[2,3,8,512]{3,2,1,0:T(8,128)S(1)} collective-permute-done((f32[2,3,8,512]{3,2,1,0:T(8,128)S(1)}, f32[2,3,8,512]{3,2,1,0:T(8,128)S(1)}, u32[]{:S(2)}, u32[]{:S(2)}) %collective-permute-start.4) | collective-permute-done | bytes 98336 | tf_op jit(solution)/shard_map/ppermute | solution.py:625
  90.5 2.8 %copy-done.2 = bf16[6,2,512,512]{3,2,1,0:T(8,128)(2,1)S(1)} copy-done((bf16[6,2,512,512]{3,2,1,0:T(8,128)(2,1)S(1)}, bf16[6,2,512,512]{3,2,1,0:T(8,128)(2,1)}, u32[]{:S(2)}) %copy-start.2) | copy-done | bytes 6291480
  93.3 5.8 %key_terms.4 = bf16[512,768]{1,0:T(8,128)(2,1)S(1)} custom-call(bf16[6,2,512,512]{3,2,1,0:T(8,128)(2,1)S(1)} %copy-done.2, bf16[6,2,512,512]{3,2,1,0:T(8,128)(2,1)} %get-tuple-element.70.refs_1_.refs_8_, bf16[512,768]{1,0:T(8,128)(2,1)S(1)} %copy-done.1, bf16[512,768]{1,0:T(8,128)(2,1)S(1)} %copy-done.1, ...), custom_call_target="tpu_custom_call" | custom-call | flops 1207959552 | bytes 12582912 | tf_op jit(solution)/shard_map/key_terms/pallas_call | solution.py:505
  99.8 7.8 %key_terms.5 = bf16[512,768]{1,0:T(8,128)(2,1)S(1)} custom-call(bf16[12,2,512,512]{3,2,1,0:T(8,128)(2,1)} %get-tuple-element.67.refs_0_.refs_7_, bf16[12,2,512,512]{3,2,1,0:T(8,128)(2,1)} %get-tuple-element.68.refs_1_.refs_8_, bf16[512,768]{1,0:T(8,128)(2,1)S(1)} %copy-done.1, bf16[512,768]{1,0:T(8,128)(2,1)S(1)} %copy-done.1, ...), custom_call_target="tpu_custom_call" | custom-call | flops 1207959552 | bytes 12582912 | tf_op jit(solution)/shard_map/key_terms/pallas_call | solution.py:505
  107.7 6.1 %key_terms.6 = bf16[512,768]{1,0:T(8,128)(2,1)S(1)} custom-call(bf16[3,2,512,512]{3,2,1,0:T(8,128)(2,1)S(1)} %copy-done.9, bf16[3,2,512,512]{3,2,1,0:T(8,128)(2,1)S(1)} %copy-done.11, bf16[512,768]{1,0:T(8,128)(2,1)S(1)} %copy-done.1, bf16[512,768]{1,0:T(8,128)(2,1)S(1)} %copy-done.1, f32[3,8,512]{2,1,0:T(8,128)S(1)} %get-tuple-element.50.refs_4_, ...), custom_call_target="tpu_custom_call" | custom-call | flops 1207959552 | bytes 12582912 | tf_op jit(solution)/shard_map/key_terms/pallas_call | solution.py:505
  114.3 3.0 %collective-permute-start.7 = (bf16[512,768]{1,0:T(8,128)(2,1)S(1)}, bf16[512,768]{1,0:T(8,128)(2,1)S(1)}, u32[]{:S(2)}, u32[]{:S(2)}) collective-permute-start(bf16[512,768]{1,0:T(8,128)(2,1)S(1)} %key_terms.4), channel_id=1, source_target_pairs={{0,12},{4,8},{8,4},{12,0},{16,28},{20,24},{24,20},{28,16},{1,13},{... | collective-permute-start | bytes 2359304 | tf_op jit(solution)/shard_map/ppermute | solution.py:625
  117.7 2.8 %collective-permute-start.6 = (bf16[512,384]{1,0:T(8,128)(2,1)S(1)}, bf16[512,384]{1,0:T(8,128)(2,1)S(1)}, u32[]{:S(2)}, u32[]{:S(2)}) collective-permute-start(bf16[512,384]{1,0:T(8,128)(2,1)S(1)} %query_send.1), channel_id=1, source_target_pairs={{0,16},{4,20},{8,24},{12,28},{16,0},{20,4},{24,8},{28,12},{1,17},{... | collective-permute-start | bytes 1179656 | tf_op jit(solution)/shard_map/ppermute | solution.py:625
  120.5 5.9 %key_terms.7.refs_2_ = f32[512,768]{1,0:T(8,128)S(1)} custom-call(bf16[3,2,512,512]{3,2,1,0:T(8,128)(2,1)S(1)} %copy-done.5, bf16[3,2,512,512]{3,2,1,0:T(8,128)(2,1)S(1)} %copy-done.7, bf16[512,768]{1,0:T(8,128)(2,1)S(1)} %copy-done.1, bf16[512,768]{1,0:T(8,128)(2,1)S(1)} %copy-done.1, f32[3,8,512]{2,1,0:T(8,128)S(1)} %get-tuple-element.46.refs_4_, ...), custom_call_target="tpu_custom_call" | custom-call | flops 1207959552 | bytes 12582912 | tf_op jit(solution)/shard_map/key_terms/pallas_call | solution.py:505
  126.4 31.2 %collective-permute-done.5.refs_5_ = bf16[384,512]{1,0:T(8,128)(2,1)S(1)} collective-permute-done((bf16[384,512]{1,0:T(8,128)(2,1)S(1)}, bf16[384,512]{1,0:T(8,128)(2,1)S(1)}, u32[]{:S(2)}, u32[]{:S(2)}) %collective-permute-start.5) | collective-permute-done | bytes 393248 | tf_op jit(solution)/shard_map/ppermute | solution.py:625
  157.6 1.8 %query_own.1 = (bf16[512,384]{1,0:T(8,128)(2,1)}, f32[512,384]{1,0:T(8,128)S(1)}) custom-call(f32[2,6,192,512]{3,2,1,0:T(8,128)S(1)} %get-tuple-element.60.acc.refs_0_.refs_1_.refs_4_, f32[2,6,192,512]{3,2,1,0:T(8,128)S(1)} %get-tuple-element.60.acc.refs_0_.refs_1_.refs_4_, f32[2,3,8,512]{3,2,1,0:T(8,128)S(1)} %get-tuple-element.61.mine.refs_5_.refs_12_.refs_2_, ...), custom_call_target="tpu_custom_call" | custom-call | flops 1572864 | bytes 3145728 | tf_op jit(solution)/shard_map/query_own/pallas_call | solution.py:578
  159.4 0.9 copy-done.13
  160.3 1.5 collective-permute-done.6.refs_1_
  161.8 1.7 %collective-permute-done.7.refs_3_ = bf16[512,768]{1,0:T(8,128)(2,1)S(1)} collective-permute-done((bf16[512,768]{1,0:T(8,128)(2,1)S(1)}, bf16[512,768]{1,0:T(8,128)(2,1)S(1)}, u32[]{:S(2)}, u32[]{:S(2)}) %collective-permute-start.7) | collective-permute-done | bytes 786464 | tf_op jit(solution)/shard_map/ppermute | solution.py:625
  163.6 0.9 copy-done.18
  164.4 4.2 %final_sums.1 = (bf16[512,384]{1,0:T(8,128)(2,1)}, bf16[512,384]{1,0:T(8,128)(2,1)}, bf16[512,384]{1,0:T(8,128)(2,1)}) custom-call(f32[512,384]{1,0:T(8,128)} %copy-done.13, bf16[512,384]{1,0:T(8,128)(2,1)} %copy-done.19, f32[512,768]{1,0:T(8,128)} %copy-done.3, bf16[512,768]{1,0:T(8,128)(2,1)} %copy-done.18, bf16[512,768]{1,0:T(8,128)(2,1)} %copy-done.17, ...), custom_call_target="tpu_custom_call" | custom-call | tf_op jit(solution)/shard_map/final_sums/pallas_call | solution.py:613
  (41 shorter events, 3.0 us)
Async XLA Ops:
  3.2 21.0 %collective-permute-start.2 = (bf16[512,768]{1,0:T(8,128)(2,1)}, bf16[512,768]{1,0:T(8,128)(2,1)S(1)}, u32[]{:S(2)}, u32[]{:S(2)}) collective-permute-start(bf16[512,768]{1,0:T(8,128)(2,1)} %get-tuple-element.52.refs_4_.refs_5_.refs_6_.refs_7_), channel_id=1, source_target_pairs={{0,4},{4,0},{8,12},{12,8},{16,20},{20,16},{24,28},{28,24},{1,5},{5... | collective-permute-start | bytes 2359304 | tf_op jit(solution)/shard_map/ppermute | solution.py:625
  6.2 35.9 %collective-permute-start.1 = (bf16[512,768]{1,0:T(8,128)(2,1)}, bf16[512,768]{1,0:T(8,128)(2,1)S(1)}, u32[]{:S(2)}, u32[]{:S(2)}) collective-permute-start(bf16[512,768]{1,0:T(8,128)(2,1)} %get-tuple-element.52.refs_4_.refs_5_.refs_6_.refs_7_), channel_id=1, source_target_pairs={{0,8},{4,12},{8,0},{12,4},{16,24},{20,28},{24,16},{28,20},{1,9},{5... | collective-permute-start | bytes 2359304 | tf_op jit(solution)/shard_map/ppermute | solution.py:625
  7.8 36.7 %collective-permute-start = (bf16[512,768]{1,0:T(8,128)(2,1)}, bf16[512,768]{1,0:T(8,128)(2,1)S(1)}, u32[]{:S(2)}, u32[]{:S(2)}) collective-permute-start(bf16[512,768]{1,0:T(8,128)(2,1)} %get-tuple-element.44.refs_2_.refs_3_), channel_id=1, source_target_pairs={{0,16},{4,20},{8,24},{12,28},{16,0},{20,4},{24,8},{28,12},{1,17},{... | collective-permute-start | bytes 2359304 | tf_op jit(solution)/shard_map/ppermute | solution.py:625
  10.4 1.2 copy-start
  11.5 1.1 copy-start.12
  12.7 0.7 copy-start.14
  13.3 0.7 copy-start.15
  14.0 10.2 %copy-start.1 = (bf16[512,768]{1,0:T(8,128)(2,1)S(1)}, bf16[512,768]{1,0:T(8,128)(2,1)}, u32[]{:S(2)}) copy-start(bf16[512,768]{1,0:T(8,128)(2,1)} %get-tuple-element.44.refs_2_.refs_3_) | copy-start | bytes 2359300
  20.9 1.6 copy-start.4
  22.5 1.7 copy-start.6
  31.2 1.8 %copy-start.8 = (bf16[3,2,512,512]{3,2,1,0:T(8,128)(2,1)}, bf16[3,2,512,512]{3,2,1,0:T(8,128)(2,1)S(1)}, u32[]{:S(2)}) copy-start(bf16[3,2,512,512]{3,2,1,0:T(8,128)(2,1)S(1)} %get-tuple-element.65.refs_0_) | copy-start | bytes 9437188
  32.9 1.7 copy-start.10
  42.1 27.9 %collective-permute-start.3 = (bf16[512,768]{1,0:T(8,128)(2,1)S(1)}, bf16[512,768]{1,0:T(8,128)(2,1)S(1)}, u32[]{:S(2)}, u32[]{:S(2)}) collective-permute-start(bf16[512,768]{1,0:T(8,128)(2,1)S(1)} %collective-permute-done.1.refs_10_.refs_11_), channel_id=1, source_target_pairs={{0,4},{4,0},{8,12},{12,8},{16,20},{20,16},{24,28},{28,24},{1,5},{5... | collective-permute-start | bytes 2359304 | tf_op jit(solution)/shard_map/ppermute | solution.py:625
  84.1 6.5 %collective-permute-start.4 = (f32[2,3,8,512]{3,2,1,0:T(8,128)S(1)}, f32[2,3,8,512]{3,2,1,0:T(8,128)S(1)}, u32[]{:S(2)}, u32[]{:S(2)}) collective-permute-start(f32[2,3,8,512]{3,2,1,0:T(8,128)S(1)} %get-tuple-element.61.mine.refs_5_.refs_12_.refs_2_), channel_id=1, source_target_pairs={{0,16},{4,20},{8,24},{12,28},{16,0},{20,4},{24,8},{28,12},{1,17},{... | collective-permute-start | bytes 294920 | tf_op jit(solution)/shard_map/ppermute | solution.py:625
  90.5 2.8 %copy-start.2 = (bf16[6,2,512,512]{3,2,1,0:T(8,128)(2,1)S(1)}, bf16[6,2,512,512]{3,2,1,0:T(8,128)(2,1)}, u32[]{:S(2)}) copy-start(bf16[6,2,512,512]{3,2,1,0:T(8,128)(2,1)} %get-tuple-element.69.refs_0_.refs_7_) | copy-start | bytes 18874372
  99.8 7.9 %copy-start.9 = (bf16[3,2,512,512]{3,2,1,0:T(8,128)(2,1)S(1)}, bf16[3,2,512,512]{3,2,1,0:T(8,128)(2,1)}, u32[]{:S(2)}) copy-start(bf16[3,2,512,512]{3,2,1,0:T(8,128)(2,1)} %copy-done.8) | copy-start | bytes 9437188
  99.8 7.9 %copy-start.11 = (bf16[3,2,512,512]{3,2,1,0:T(8,128)(2,1)S(1)}, bf16[3,2,512,512]{3,2,1,0:T(8,128)(2,1)}, u32[]{:S(2)}) copy-start(bf16[3,2,512,512]{3,2,1,0:T(8,128)(2,1)} %copy-done.10) | copy-start | bytes 9437188
  107.7 12.8 %copy-start.7 = (bf16[3,2,512,512]{3,2,1,0:T(8,128)(2,1)S(1)}, bf16[3,2,512,512]{3,2,1,0:T(8,128)(2,1)}, u32[]{:S(2)}) copy-start(bf16[3,2,512,512]{3,2,1,0:T(8,128)(2,1)} %copy-done.6) | copy-start | bytes 9437188
  113.8 6.8 %copy-start.5 = (bf16[3,2,512,512]{3,2,1,0:T(8,128)(2,1)S(1)}, bf16[3,2,512,512]{3,2,1,0:T(8,128)(2,1)}, u32[]{:S(2)}) copy-start(bf16[3,2,512,512]{3,2,1,0:T(8,128)(2,1)} %copy-done.4) | copy-start | bytes 9437188
  113.8 48.1 %collective-permute-start.9 = (bf16[512,768]{1,0:T(8,128)(2,1)S(1)}, bf16[512,768]{1,0:T(8,128)(2,1)S(1)}, u32[]{:S(2)}, u32[]{:S(2)}) collective-permute-start(bf16[512,768]{1,0:T(8,128)(2,1)S(1)} %key_terms.6), channel_id=1, source_target_pairs={{0,4},{4,0},{8,12},{12,8},{16,20},{20,16},{24,28},{28,24},{1,5},{5... | collective-permute-start | bytes 2359304 | tf_op jit(solution)/shard_map/ppermute | solution.py:625
  114.3 47.5 %collective-permute-start.8 = (bf16[512,768]{1,0:T(8,128)(2,1)S(1)}, bf16[512,768]{1,0:T(8,128)(2,1)S(1)}, u32[]{:S(2)}, u32[]{:S(2)}) collective-permute-start(bf16[512,768]{1,0:T(8,128)(2,1)S(1)} %key_terms.5), channel_id=1, source_target_pairs={{0,8},{4,12},{8,0},{12,4},{16,24},{20,28},{24,16},{28,20},{1,9},{5... | collective-permute-start | bytes 2359304 | tf_op jit(solution)/shard_map/ppermute | solution.py:625
  114.3 49.2 %collective-permute-start.7 = (bf16[512,768]{1,0:T(8,128)(2,1)S(1)}, bf16[512,768]{1,0:T(8,128)(2,1)S(1)}, u32[]{:S(2)}, u32[]{:S(2)}) collective-permute-start(bf16[512,768]{1,0:T(8,128)(2,1)S(1)} %key_terms.4), channel_id=1, source_target_pairs={{0,12},{4,8},{8,4},{12,0},{16,28},{20,24},{24,20},{28,16},{1,13},{... | collective-permute-start | bytes 2359304 | tf_op jit(solution)/shard_map/ppermute | solution.py:625
  117.5 40.0 %collective-permute-start.5 = (bf16[384,512]{1,0:T(8,128)(2,1)S(1)}, bf16[384,512]{1,0:T(8,128)(2,1)S(1)}, u32[]{:S(2)}, u32[]{:S(2)}) collective-permute-start(bf16[384,512]{1,0:T(8,128)(2,1)S(1)} %attend_terms.1), channel_id=1, source_target_pairs={{0,16},{4,20},{8,24},{12,28},{16,0},{20,4},{24,8},{28,12},{1,17},{... | collective-permute-start | bytes 1179656 | tf_op jit(solution)/shard_map/ppermute | solution.py:625
  117.7 44.2 %collective-permute-start.6 = (bf16[512,384]{1,0:T(8,128)(2,1)S(1)}, bf16[512,384]{1,0:T(8,128)(2,1)S(1)}, u32[]{:S(2)}, u32[]{:S(2)}) collective-permute-start(bf16[512,384]{1,0:T(8,128)(2,1)S(1)} %query_send.1), channel_id=1, source_target_pairs={{0,16},{4,20},{8,24},{12,28},{16,0},{20,4},{24,8},{28,12},{1,17},{... | collective-permute-start | bytes 1179656 | tf_op jit(solution)/shard_map/ppermute | solution.py:625
  126.4 33.0 %copy-start.3 = (f32[512,768]{1,0:T(8,128)}, f32[512,768]{1,0:T(8,128)S(1)}, u32[]{:S(2)}) copy-start(f32[512,768]{1,0:T(8,128)S(1)} %key_terms.7.refs_2_) | copy-start | bytes 4718596
  159.4 0.9 copy-start.13
  161.8 1.7 %copy-start.19 = (bf16[512,384]{1,0:T(8,128)(2,1)}, bf16[512,384]{1,0:T(8,128)(2,1)S(1)}, u32[]{:S(2)}) copy-start(bf16[512,384]{1,0:T(8,128)(2,1)S(1)} %collective-permute-done.6.refs_1_) | copy-start | bytes 1179652
  161.8 1.7 %copy-start.16 = (bf16[512,768]{1,0:T(8,128)(2,1)}, bf16[512,768]{1,0:T(8,128)(2,1)S(1)}, u32[]{:S(2)}) copy-start(bf16[512,768]{1,0:T(8,128)(2,1)S(1)} %collective-permute-done.9.refs_5_) | copy-start | bytes 2359300
  161.8 1.7 %copy-start.17 = (bf16[512,768]{1,0:T(8,128)(2,1)}, bf16[512,768]{1,0:T(8,128)(2,1)S(1)}, u32[]{:S(2)}) copy-start(bf16[512,768]{1,0:T(8,128)(2,1)S(1)} %collective-permute-done.8.refs_4_) | copy-start | bytes 2359300
  163.6 0.9 copy-start.18

commit v5 on v4

--- a/solution.py
+++ b/solution.py
@@ -589,35 +589,29 @@
     )(*operands)
 
 
-def final_kernel(query_count, *refs):
-    ins, (out_q, out_k, out_v) = refs[:-3], refs[-3:]
-
-    def summed(parts):
-        total = parts[0][...].astype(jnp.float32)
-        for part in parts[1:]:
-            total = total + part[...].astype(jnp.float32)
-        return total
-
-    out_q[...] = summed(ins[:query_count]).astype(jnp.bfloat16)
-    keys = summed(ins[query_count:])
-    features = out_k.shape[1]
-    out_k[...] = keys[:, :features].astype(jnp.bfloat16)
-    out_v[...] = keys[:, features:].astype(jnp.bfloat16)
-
-
-def final_sums(query_parts, key_parts):
-    rows, features = query_parts[0].shape
-    tile = rows // 4
-    narrow = pl.BlockSpec((tile, features), lambda p: (p, 0))
-    wide = pl.BlockSpec((tile, 2 * features), lambda p: (p, 0))
+def summed(parts):
+    total = parts[0][...].astype(jnp.float32)
+    for part in parts[1:]:
+        total = total + part[...].astype(jnp.float32)
+    return total
+
+
+def final_kernel(splits, *refs):
+    total = summed(refs[:-splits])
+    for at, out in enumerate(refs[-splits:]):
+        columns = out.shape[1]
+        out[...] = total[:, at * columns : (at + 1) * columns].astype(jnp.bfloat16)
+
+
+def final_sums(parts, splits):
+    rows, columns = parts[0].shape
     return pl.pallas_call(
-        lambda *refs: final_kernel(len(query_parts), *refs),
-        grid=(rows // tile,),
-        in_specs=[narrow] * len(query_parts) + [wide] * len(key_parts),
-        out_specs=[narrow] * 3,
-        out_shape=[jax.ShapeDtypeStruct((rows, features), jnp.bfloat16)] * 3,
+        lambda *refs: final_kernel(splits, *refs),
+        in_specs=[pl.BlockSpec(memory_space=pltpu.VMEM)] * len(parts),
+        out_specs=[pl.BlockSpec(memory_space=pltpu.VMEM)] * splits,
+        out_shape=[jax.ShapeDtypeStruct((rows, columns // splits), jnp.bfloat16)] * splits,
         name="final_sums",
-    )(*query_parts, *key_parts)
+    )(*parts)
 
 
 def swapped(x, offset):
@@ -707,7 +701,10 @@
     came_upper = after(came_upper, own_keys)
     attended, own_queries = query_terms(0, acc, mine, theirs, came_upper)
     came = after(came, own_queries)
-    return (attended,) + tuple(final_sums([own_queries, came], [own_keys] + key_parts))
+    grad_queries = final_sums([own_queries, came], 1)[0]
+    key_parts = [after(x, grad_queries) for x in key_parts]
+    grad_keys, grad_values = final_sums([own_keys] + key_parts, 2)
+    return (attended, grad_queries, grad_keys, grad_values)
 
 
 def paired(devices):

time: 169 us -> 173 us (1.024)
  Pallas kernels: 88.5 us -> 92.1 us
  local copies, waits for them, and re-layouts: 14.9 us -> 16.8 us
    pallas_call x4, Pallas kernels: 25.6 us -> 28.2 us  [key_terms(): pl.pallas_call(key_kernel, grid=(steps,), in_specs=in_specs, out_specs=pl...]
    unnamed x40, local copies, waits for them, and re-layouts: 14.9 us -> 16.8 us
    pallas_call x1 -> x2, Pallas kernels: 4.22 us -> 5.22 us  [final_sums(): pl.pallas_call(lambda *refs: final_kernel(splits, *refs), in_specs=[pl.Bl...]
  transfers between devices with their start and end apart: 10 -> 10, of which waited for: 6 -> 5; matrix products, arithmetic and copies ran while one was open for 0% -> 0% of each run, Pallas kernels for 28% -> 29%
where the time goes in v5:
time: 173 us
  Pallas kernels  92.1 us (53%)
  waiting for transfers between devices  48.6 us (28%)
  local copies, waits for them, and re-layouts  16.8 us (10%)
  starting transfers between devices  14.3 us (8%)
    pallas_call x4, Pallas kernels, pair_terms(): pl.pallas_call(lambda *refs: pairs_kernel(plan, *refs), grid=(total + 1,)...  53.4 us
    ppermute x10, waiting for transfers between devices, swapped(): return lax.ppermute(x, 'seq', [(i, i ^ offset) for i in range(devices)])  48.6 us
    pallas_call x4, Pallas kernels, key_terms(): pl.pallas_call(key_kernel, grid=(steps,), in_specs=in_specs, out_specs=pl...  28.2 us
    unnamed x40, local copies, waits for them, and re-layouts  16.8 us
    ppermute x10, starting transfers between devices, swapped(): return lax.ppermute(x, 'seq', [(i, i ^ offset) for i in range(devices)])  14.3 us
    pallas_call x2, Pallas kernels, final_sums(): pl.pallas_call(lambda *refs: final_kernel(splits, *refs), in_specs=[pl.Bl...  5.22 us
  transfers between devices with their start and end apart: 10, of which 5 were waited for; matrix products, arithmetic and copies ran while one was open for 0% of the time, Pallas kernels for 29%

profile of v5, /device:TPU:0, one launch (start us, length us, event | category | flops | bytes accessed | tf_op | source)
XLA Modules:
  0.0 172.5 jit_solution(3420854415303738994)
XLA Ops:
  0.6 2.6 %pack.1 = (bf16[512,768]{1,0:T(8,128)(2,1)}, bf16[512,768]{1,0:T(8,128)(2,1)}) custom-call(bf16[512,384]{1,0:T(8,128)(2,1)} %k_ref.1, bf16[512,384]{1,0:T(8,128)(2,1)} %v_ref.1, bf16[512,384]{1,0:T(8,128)(2,1)} %q_ref.1, bf16[512,384]{1,0:T(8,128)(2,1)} %do_ref.1), custom_call_target="tpu_custom_call" | custom-call | tf_op jit(solution)/shard_map/pack/pallas_call | solution.py:634
  3.2 3.0 %collective-permute-start.2 = (bf16[512,768]{1,0:T(8,128)(2,1)}, bf16[512,768]{1,0:T(8,128)(2,1)S(1)}, u32[]{:S(2)}, u32[]{:S(2)}) collective-permute-start(bf16[512,768]{1,0:T(8,128)(2,1)} %get-tuple-element.54.refs_4_.refs_5_.refs_6_.refs_7_), channel_id=1, source_target_pairs={{0,4},{4,0},{8,12},{12,8},{16,20},{20,16},{24,28},{28,24},{1,5},{5... | collective-permute-start | bytes 2359304 | tf_op jit(solution)/shard_map/ppermute | solution.py:619
  6.2 1.6 collective-permute-start.1
  7.8 2.6 %collective-permute-start = (bf16[512,768]{1,0:T(8,128)(2,1)}, bf16[512,768]{1,0:T(8,128)(2,1)S(1)}, u32[]{:S(2)}, u32[]{:S(2)}) collective-permute-start(bf16[512,768]{1,0:T(8,128)(2,1)} %get-tuple-element.46.refs_2_.refs_3_), channel_id=1, source_target_pairs={{0,16},{4,20},{8,24},{12,28},{16,0},{20,4},{24,8},{28,12},{1,17},{... | collective-permute-start | bytes 2359304 | tf_op jit(solution)/shard_map/ppermute | solution.py:619
  10.4 1.2 copy-done
  11.5 1.1 copy-done.12
  14.0 6.9 %shard_map.93 = (bf16[3,2,512,512]{3,2,1,0:T(8,128)(2,1)S(1)}, bf16[3,2,512,512]{3,2,1,0:T(8,128)(2,1)S(1)}, f32[1,6,192,512]{3,2,1,0:T(8,128)S(1)}, f32[1,3,8,512]{3,2,1,0:T(8,128)S(1)}, f32[3,8,512]{2,1,0:T(8,128)S(1)}) custom-call(s32[3,8]{1,0:T(4,128)S(1)} %copy-done.14, s32[2]{0:T(128)S(1)} %copy-done.15, bf16[512,768]{1,0:T(8,128)(2,1)S(1)} %copy-done, ...), custom_call_target="tpu_custom_call" | custom-call | flops 805306368 | bytes 6291456 | tf_op jit(solution)/shard_map/pallas_call | solution.py:404
  20.9 1.6 copy-done.4
  22.5 1.7 copy-done.6
  24.2 6.9 %shard_map.94 = (bf16[3,2,512,512]{3,2,1,0:T(8,128)(2,1)S(1)}, bf16[3,2,512,512]{3,2,1,0:T(8,128)(2,1)S(1)}, f32[1,6,192,512]{3,2,1,0:T(8,128)S(1)}, f32[1,3,8,512]{3,2,1,0:T(8,128)S(1)}, f32[3,8,512]{2,1,0:T(8,128)S(1)}) custom-call(s32[3,8]{1,0:T(4,128)S(1)} %copy-done.14, s32[2]{0:T(128)S(1)} %copy-done.15, bf16[512,768]{1,0:T(8,128)(2,1)S(1)} %copy-done.1, ...), custom_call_target="tpu_custom_call" | custom-call | flops 805306368 | bytes 6291456 | tf_op jit(solution)/shard_map/pallas_call | solution.py:404
  31.2 1.8 %copy-done.8 = bf16[3,2,512,512]{3,2,1,0:T(8,128)(2,1)} copy-done((bf16[3,2,512,512]{3,2,1,0:T(8,128)(2,1)}, bf16[3,2,512,512]{3,2,1,0:T(8,128)(2,1)S(1)}, u32[]{:S(2)}) %copy-start.8) | copy-done | bytes 3145752
  32.9 1.7 copy-done.10
  34.6 7.5 %collective-permute-done.1.refs_10_.refs_11_ = bf16[512,768]{1,0:T(8,128)(2,1)S(1)} collective-permute-done((bf16[512,768]{1,0:T(8,128)(2,1)}, bf16[512,768]{1,0:T(8,128)(2,1)S(1)}, u32[]{:S(2)}, u32[]{:S(2)}) %collective-permute-start.1) | collective-permute-done | bytes 786464 | tf_op jit(solution)/shard_map/ppermute | solution.py:619
  42.5 2.0 %collective-permute-done.refs_4_.refs_5_.refs_9_.refs_10_ = bf16[512,768]{1,0:T(8,128)(2,1)S(1)} collective-permute-done((bf16[512,768]{1,0:T(8,128)(2,1)}, bf16[512,768]{1,0:T(8,128)(2,1)S(1)}, u32[]{:S(2)}, u32[]{:S(2)}) %collective-permute-start) | collective-permute-done | bytes 786464 | tf_op jit(solution)/shard_map/ppermute | solution.py:619
  44.5 25.5 %shard_map.95 = (bf16[12,2,512,512]{3,2,1,0:T(8,128)(2,1)}, bf16[12,2,512,512]{3,2,1,0:T(8,128)(2,1)}, f32[2,6,192,512]{3,2,1,0:T(8,128)S(1)}, f32[2,3,8,512]{3,2,1,0:T(8,128)S(1)}, f32[12,8,512]{2,1,0:T(8,128)S(1)}) custom-call(s32[3,8]{1,0:T(4,128)S(1)} %copy-done.14, s32[2]{0:T(128)S(1)} %copy-done.15, bf16[512,768]{1,0:T(8,128)(2,1)S(1)} %copy-done.1, ...), custom_call_target="tpu_custom_call" | custom-call | flops 3221225472 | bytes 25165824 | tf_op jit(solution)/shard_map/pallas_call | solution.py:404
  70.0 14.0 %shard_map.96 = (bf16[6,2,512,512]{3,2,1,0:T(8,128)(2,1)}, bf16[6,2,512,512]{3,2,1,0:T(8,128)(2,1)}, f32[2,6,192,512]{3,2,1,0:T(8,128)S(1)}, f32[2,3,8,512]{3,2,1,0:T(8,128)S(1)}, f32[6,8,512]{2,1,0:T(8,128)S(1)}) custom-call(s32[3,8]{1,0:T(4,128)S(1)} %copy-done.14, s32[2]{0:T(128)S(1)} %copy-done.15, bf16[512,768]{1,0:T(8,128)(2,1)S(1)} %copy-done.1, ...), custom_call_target="tpu_custom_call" | custom-call | flops 1610612736 | bytes 12582912 | tf_op jit(solution)/shard_map/pallas_call | solution.py:404
  84.4 6.1 %collective-permute-done.4.refs_6_.refs_13_.refs_3_ = f32[2,3,8,512]{3,2,1,0:T(8,128)S(1)} collective-permute-done((f32[2,3,8,512]{3,2,1,0:T(8,128)S(1)}, f32[2,3,8,512]{3,2,1,0:T(8,128)S(1)}, u32[]{:S(2)}, u32[]{:S(2)}) %collective-permute-start.4) | collective-permute-done | bytes 98336 | tf_op jit(solution)/shard_map/ppermute | solution.py:619
  90.5 2.8 %copy-done.2 = bf16[6,2,512,512]{3,2,1,0:T(8,128)(2,1)S(1)} copy-done((bf16[6,2,512,512]{3,2,1,0:T(8,128)(2,1)S(1)}, bf16[6,2,512,512]{3,2,1,0:T(8,128)(2,1)}, u32[]{:S(2)}) %copy-start.2) | copy-done | bytes 6291480
  93.3 6.7 %key_terms.4 = bf16[512,768]{1,0:T(8,128)(2,1)} custom-call(bf16[6,2,512,512]{3,2,1,0:T(8,128)(2,1)S(1)} %copy-done.2, bf16[6,2,512,512]{3,2,1,0:T(8,128)(2,1)} %get-tuple-element.72.refs_1_.refs_8_, bf16[512,768]{1,0:T(8,128)(2,1)S(1)} %copy-done.1, bf16[512,768]{1,0:T(8,128)(2,1)S(1)} %copy-done.1, f32[6,8,512]{2,1,0:T(8,128)S(1)} %get-tuple-element.73.refs_4_.refs_11_, ...), custom_call_target="tpu_custom_call" | custom-call | flops 1207959552 | bytes 12582912 | tf_op jit(solution)/shard_map/key_terms/pallas_call | solution.py:505
  100.7 8.7 %key_terms.5 = bf16[512,768]{1,0:T(8,128)(2,1)} custom-call(bf16[12,2,512,512]{3,2,1,0:T(8,128)(2,1)} %get-tuple-element.69.refs_0_.refs_7_, bf16[12,2,512,512]{3,2,1,0:T(8,128)(2,1)} %get-tuple-element.70.refs_1_.refs_8_, bf16[512,768]{1,0:T(8,128)(2,1)S(1)} %copy-done.1, bf16[512,768]{1,0:T(8,128)(2,1)S(1)} %copy-done.1, ...), custom_call_target="tpu_custom_call" | custom-call | flops 1207959552 | bytes 12582912 | tf_op jit(solution)/shard_map/key_terms/pallas_call | solution.py:505
  109.4 6.9 %key_terms.6 = bf16[512,768]{1,0:T(8,128)(2,1)} custom-call(bf16[3,2,512,512]{3,2,1,0:T(8,128)(2,1)S(1)} %copy-done.9, bf16[3,2,512,512]{3,2,1,0:T(8,128)(2,1)S(1)} %copy-done.11, bf16[512,768]{1,0:T(8,128)(2,1)S(1)} %copy-done.1, bf16[512,768]{1,0:T(8,128)(2,1)S(1)} %copy-done.1, f32[3,8,512]{2,1,0:T(8,128)S(1)} %get-tuple-element.52.refs_4_, ...), custom_call_target="tpu_custom_call" | custom-call | flops 1207959552 | bytes 12582912 | tf_op jit(solution)/shard_map/key_terms/pallas_call | solution.py:505
  116.8 3.0 %collective-permute-start.7 = (bf16[512,768]{1,0:T(8,128)(2,1)}, bf16[512,768]{1,0:T(8,128)(2,1)S(1)}, u32[]{:S(2)}, u32[]{:S(2)}) collective-permute-start(bf16[512,768]{1,0:T(8,128)(2,1)} %key_terms.4), channel_id=1, source_target_pairs={{0,12},{4,8},{8,4},{12,0},{16,28},{20,24},{24,20},{28,16},{1,13},{... | collective-permute-start | bytes 2359304 | tf_op jit(solution)/shard_map/ppermute | solution.py:619
  120.1 2.8 %collective-permute-start.6 = (bf16[512,384]{1,0:T(8,128)(2,1)S(1)}, bf16[512,384]{1,0:T(8,128)(2,1)S(1)}, u32[]{:S(2)}, u32[]{:S(2)}) collective-permute-start(bf16[512,384]{1,0:T(8,128)(2,1)S(1)} %query_send.1), channel_id=1, source_target_pairs={{0,16},{4,20},{8,24},{12,28},{16,0},{20,4},{24,8},{28,12},{1,17},{... | collective-permute-start | bytes 1179656 | tf_op jit(solution)/shard_map/ppermute | solution.py:619
  123.0 5.9 %key_terms.7.refs_0_ = f32[512,768]{1,0:T(8,128)S(1)} custom-call(bf16[3,2,512,512]{3,2,1,0:T(8,128)(2,1)S(1)} %copy-done.5, bf16[3,2,512,512]{3,2,1,0:T(8,128)(2,1)S(1)} %copy-done.7, bf16[512,768]{1,0:T(8,128)(2,1)S(1)} %copy-done.1, bf16[512,768]{1,0:T(8,128)(2,1)S(1)} %copy-done.1, f32[3,8,512]{2,1,0:T(8,128)S(1)} %get-tuple-element.48.refs_4_, ...), custom_call_target="tpu_custom_call" | custom-call | flops 1207959552 | bytes 12582912 | tf_op jit(solution)/shard_map/key_terms/pallas_call | solution.py:505
  128.9 31.4 %collective-permute-done.5.refs_5_ = bf16[384,512]{1,0:T(8,128)(2,1)S(1)} collective-permute-done((bf16[384,512]{1,0:T(8,128)(2,1)S(1)}, bf16[384,512]{1,0:T(8,128)(2,1)S(1)}, u32[]{:S(2)}, u32[]{:S(2)}) %collective-permute-start.5) | collective-permute-done | bytes 393248 | tf_op jit(solution)/shard_map/ppermute | solution.py:619
  160.2 1.8 %query_own.1 = (bf16[512,384]{1,0:T(8,128)(2,1)}, f32[512,384]{1,0:T(8,128)S(1)}) custom-call(f32[2,6,192,512]{3,2,1,0:T(8,128)S(1)} %get-tuple-element.62.acc.refs_0_.refs_1_.refs_4_, f32[2,6,192,512]{3,2,1,0:T(8,128)S(1)} %get-tuple-element.62.acc.refs_0_.refs_1_.refs_4_, f32[2,3,8,512]{3,2,1,0:T(8,128)S(1)} %get-tuple-element.63.mine.refs_5_.refs_12_.refs_2_, ...), custom_call_target="tpu_custom_call" | custom-call | flops 1572864 | bytes 3145728 | tf_op jit(solution)/shard_map/query_own/pallas_call | solution.py:578
  162.1 0.9 copy-done.13
  163.0 1.5 collective-permute-done.6.refs_1_
  165.3 2.0 %final_sums.2 = bf16[512,384]{1,0:T(8,128)(2,1)} custom-call(f32[512,384]{1,0:T(8,128)} %copy-done.13, bf16[512,384]{1,0:T(8,128)(2,1)} %copy-done.19), custom_call_target="tpu_custom_call" | custom-call | tf_op jit(solution)/shard_map/final_sums/pallas_call | solution.py:608
  167.3 0.9 copy-done.16
  168.5 0.9 copy-done.18
  169.3 3.2 %final_sums.3 = (bf16[512,384]{1,0:T(8,128)(2,1)}, bf16[512,384]{1,0:T(8,128)(2,1)}) custom-call(f32[512,768]{1,0:T(8,128)} %copy-done.3, bf16[512,768]{1,0:T(8,128)(2,1)} %copy-done.18, bf16[512,768]{1,0:T(8,128)(2,1)} %copy-done.17, bf16[512,768]{1,0:T(8,128)(2,1)} %copy-done.16), custom_call_target="tpu_custom_call" | custom-call | tf_op jit(solution)/shard_map/final_sums/pallas_call | solution.py:608
  (42 shorter events, 4.6 us)
Async XLA Ops:
  3.2 21.0 %collective-permute-start.2 = (bf16[512,768]{1,0:T(8,128)(2,1)}, bf16[512,768]{1,0:T(8,128)(2,1)S(1)}, u32[]{:S(2)}, u32[]{:S(2)}) collective-permute-start(bf16[512,768]{1,0:T(8,128)(2,1)} %get-tuple-element.54.refs_4_.refs_5_.refs_6_.refs_7_), channel_id=1, source_target_pairs={{0,4},{4,0},{8,12},{12,8},{16,20},{20,16},{24,28},{28,24},{1,5},{5... | collective-permute-start | bytes 2359304 | tf_op jit(solution)/shard_map/ppermute | solution.py:619
  6.2 35.9 %collective-permute-start.1 = (bf16[512,768]{1,0:T(8,128)(2,1)}, bf16[512,768]{1,0:T(8,128)(2,1)S(1)}, u32[]{:S(2)}, u32[]{:S(2)}) collective-permute-start(bf16[512,768]{1,0:T(8,128)(2,1)} %get-tuple-element.54.refs_4_.refs_5_.refs_6_.refs_7_), channel_id=1, source_target_pairs={{0,8},{4,12},{8,0},{12,4},{16,24},{20,28},{24,16},{28,20},{1,9},{5... | collective-permute-start | bytes 2359304 | tf_op jit(solution)/shard_map/ppermute | solution.py:619
  7.8 36.7 %collective-permute-start = (bf16[512,768]{1,0:T(8,128)(2,1)}, bf16[512,768]{1,0:T(8,128)(2,1)S(1)}, u32[]{:S(2)}, u32[]{:S(2)}) collective-permute-start(bf16[512,768]{1,0:T(8,128)(2,1)} %get-tuple-element.46.refs_2_.refs_3_), channel_id=1, source_target_pairs={{0,16},{4,20},{8,24},{12,28},{16,0},{20,4},{24,8},{28,12},{1,17},{... | collective-permute-start | bytes 2359304 | tf_op jit(solution)/shard_map/ppermute | solution.py:619
  10.4 1.2 copy-start
  11.5 1.1 copy-start.12
  12.7 0.7 copy-start.14
  13.3 0.7 copy-start.15
  14.0 10.2 %copy-start.1 = (bf16[512,768]{1,0:T(8,128)(2,1)S(1)}, bf16[512,768]{1,0:T(8,128)(2,1)}, u32[]{:S(2)}) copy-start(bf16[512,768]{1,0:T(8,128)(2,1)} %get-tuple-element.46.refs_2_.refs_3_) | copy-start | bytes 2359300
  20.9 1.6 copy-start.4
  22.5 1.7 copy-start.6
  31.2 1.8 %copy-start.8 = (bf16[3,2,512,512]{3,2,1,0:T(8,128)(2,1)}, bf16[3,2,512,512]{3,2,1,0:T(8,128)(2,1)S(1)}, u32[]{:S(2)}) copy-start(bf16[3,2,512,512]{3,2,1,0:T(8,128)(2,1)S(1)} %get-tuple-element.67.refs_0_) | copy-start | bytes 9437188
  32.9 1.7 copy-start.10
  42.1 27.9 %collective-permute-start.3 = (bf16[512,768]{1,0:T(8,128)(2,1)S(1)}, bf16[512,768]{1,0:T(8,128)(2,1)S(1)}, u32[]{:S(2)}, u32[]{:S(2)}) collective-permute-start(bf16[512,768]{1,0:T(8,128)(2,1)S(1)} %collective-permute-done.1.refs_10_.refs_11_), channel_id=1, source_target_pairs={{0,4},{4,0},{8,12},{12,8},{16,20},{20,16},{24,28},{28,24},{1,5},{5... | collective-permute-start | bytes 2359304 | tf_op jit(solution)/shard_map/ppermute | solution.py:619
  84.1 6.4 %collective-permute-start.4 = (f32[2,3,8,512]{3,2,1,0:T(8,128)S(1)}, f32[2,3,8,512]{3,2,1,0:T(8,128)S(1)}, u32[]{:S(2)}, u32[]{:S(2)}) collective-permute-start(f32[2,3,8,512]{3,2,1,0:T(8,128)S(1)} %get-tuple-element.63.mine.refs_5_.refs_12_.refs_2_), channel_id=1, source_target_pairs={{0,16},{4,20},{8,24},{12,28},{16,0},{20,4},{24,8},{28,12},{1,17},{... | collective-permute-start | bytes 294920 | tf_op jit(solution)/shard_map/ppermute | solution.py:619
  90.5 2.8 %copy-start.2 = (bf16[6,2,512,512]{3,2,1,0:T(8,128)(2,1)S(1)}, bf16[6,2,512,512]{3,2,1,0:T(8,128)(2,1)}, u32[]{:S(2)}) copy-start(bf16[6,2,512,512]{3,2,1,0:T(8,128)(2,1)} %get-tuple-element.71.refs_0_.refs_7_) | copy-start | bytes 18874372
  100.6 8.7 %copy-start.9 = (bf16[3,2,512,512]{3,2,1,0:T(8,128)(2,1)S(1)}, bf16[3,2,512,512]{3,2,1,0:T(8,128)(2,1)}, u32[]{:S(2)}) copy-start(bf16[3,2,512,512]{3,2,1,0:T(8,128)(2,1)} %copy-done.8) | copy-start | bytes 9437188
  100.6 8.7 %copy-start.11 = (bf16[3,2,512,512]{3,2,1,0:T(8,128)(2,1)S(1)}, bf16[3,2,512,512]{3,2,1,0:T(8,128)(2,1)}, u32[]{:S(2)}) copy-start(bf16[3,2,512,512]{3,2,1,0:T(8,128)(2,1)} %copy-done.10) | copy-start | bytes 9437188
  109.4 13.6 %copy-start.7 = (bf16[3,2,512,512]{3,2,1,0:T(8,128)(2,1)S(1)}, bf16[3,2,512,512]{3,2,1,0:T(8,128)(2,1)}, u32[]{:S(2)}) copy-start(bf16[3,2,512,512]{3,2,1,0:T(8,128)(2,1)} %copy-done.6) | copy-start | bytes 9437188
  116.3 6.7 %copy-start.5 = (bf16[3,2,512,512]{3,2,1,0:T(8,128)(2,1)S(1)}, bf16[3,2,512,512]{3,2,1,0:T(8,128)(2,1)}, u32[]{:S(2)}) copy-start(bf16[3,2,512,512]{3,2,1,0:T(8,128)(2,1)} %copy-done.4) | copy-start | bytes 9437188
  116.3 51.0 %collective-permute-start.9 = (bf16[512,768]{1,0:T(8,128)(2,1)}, bf16[512,768]{1,0:T(8,128)(2,1)S(1)}, u32[]{:S(2)}, u32[]{:S(2)}) collective-permute-start(bf16[512,768]{1,0:T(8,128)(2,1)} %key_terms.6), channel_id=1, source_target_pairs={{0,4},{4,0},{8,12},{12,8},{16,20},{20,16},{24,28},{28,24},{1,5},{5... | collective-permute-start | bytes 2359304 | tf_op jit(solution)/shard_map/ppermute | solution.py:619
  116.8 50.5 %collective-permute-start.8 = (bf16[512,768]{1,0:T(8,128)(2,1)}, bf16[512,768]{1,0:T(8,128)(2,1)S(1)}, u32[]{:S(2)}, u32[]{:S(2)}) collective-permute-start(bf16[512,768]{1,0:T(8,128)(2,1)} %key_terms.5), channel_id=1, source_target_pairs={{0,8},{4,12},{8,0},{12,4},{16,24},{20,28},{24,16},{28,20},{1,9},{5... | collective-permute-start | bytes 2359304 | tf_op jit(solution)/shard_map/ppermute | solution.py:619
  116.8 50.5 %collective-permute-start.7 = (bf16[512,768]{1,0:T(8,128)(2,1)}, bf16[512,768]{1,0:T(8,128)(2,1)S(1)}, u32[]{:S(2)}, u32[]{:S(2)}) collective-permute-start(bf16[512,768]{1,0:T(8,128)(2,1)} %key_terms.4), channel_id=1, source_target_pairs={{0,12},{4,8},{8,4},{12,0},{16,28},{20,24},{24,20},{28,16},{1,13},{... | collective-permute-start | bytes 2359304 | tf_op jit(solution)/shard_map/ppermute | solution.py:619
  120.0 40.3 %collective-permute-start.5 = (bf16[384,512]{1,0:T(8,128)(2,1)S(1)}, bf16[384,512]{1,0:T(8,128)(2,1)S(1)}, u32[]{:S(2)}, u32[]{:S(2)}) collective-permute-start(bf16[384,512]{1,0:T(8,128)(2,1)S(1)} %attend_terms.1), channel_id=1, source_target_pairs={{0,16},{4,20},{8,24},{12,28},{16,0},{20,4},{24,8},{28,12},{1,17},{... | collective-permute-start | bytes 1179656 | tf_op jit(solution)/shard_map/ppermute | solution.py:619
  120.1 44.4 %collective-permute-start.6 = (bf16[512,384]{1,0:T(8,128)(2,1)S(1)}, bf16[512,384]{1,0:T(8,128)(2,1)S(1)}, u32[]{:S(2)}, u32[]{:S(2)}) collective-permute-start(bf16[512,384]{1,0:T(8,128)(2,1)S(1)} %query_send.1), channel_id=1, source_target_pairs={{0,16},{4,20},{8,24},{12,28},{16,0},{20,4},{24,8},{28,12},{1,17},{... | collective-permute-start | bytes 1179656 | tf_op jit(solution)/shard_map/ppermute | solution.py:619
  128.9 33.2 %copy-start.3 = (f32[512,768]{1,0:T(8,128)}, f32[512,768]{1,0:T(8,128)S(1)}, u32[]{:S(2)}) copy-start(f32[512,768]{1,0:T(8,128)S(1)} %key_terms.7.refs_0_) | copy-start | bytes 4718596
  162.1 0.9 copy-start.13
  164.5 0.7 copy-start.19
  167.3 0.9 copy-start.16
  167.3 1.1 copy-start.17
  168.5 0.9 copy-start.18
